TPU v7x, 32 devices: a whole 2x2x4 slice. The times are simulated.
32 devices in a mesh: head: 4 (over z), span: 8 (over y, x, core).
Axes of the slice: x: 2, y: 2, z: 4, core: 2. Of those that a mesh axis runs over, the one named last changes fastest.
Arguments:
- queries: bfloat16 [4096, 2048], P(('span', 'head')), may hold values from -6 to 6
- keys: bfloat16 [4096, 2048], P(('span', 'head')), may hold values from -6 to 6
- values: bfloat16 [4096, 2048], P(('span', 'head')), may hold values from -6 to 6
- out_grad: bfloat16 [4096, 2048], P(('span', 'head')), may hold values from -6 to 6
Outputs:
- attn_out: bfloat16 [4096, 2048], P(('span', 'head'))
- query_gradient: bfloat16 [4096, 2048], P(('span', 'head'))
- grad_key: bfloat16 [4096, 2048], P(('span', 'head'))
- grad_value: bfloat16 [4096, 2048], P(('span', 'head'))
All inputs are finite; a program needn't handle non-finite values.
Results may differ from a plain program's by a relative error of at most 0.0058.
Values may be sent and summed in bfloat16 or wider, within the bound.
No kernel may reach another device: no remote copies, remote signals or barrier semaphores. Data moves between devices by JAX's collectives and lax.ppermute only.
A program may use at most 64 MiB of HBM per device.

v0:
```python
import jax
import jax.numpy as jnp
from jax import lax
from jax.sharding import PartitionSpec as P

HEADS = 16
DH = 128


def block_work(queries, keys, values, scaled, position_scale, forward_narrow, back_low):
    length = queries.shape[0]
    head_count = queries.shape[1]
    head_width = queries.shape[2]
    row_count = min(512, length)
    outputs = []
    query_grads = []
    key_acc = jnp.zeros((length, head_count, head_width), jnp.float32)
    value_acc = jnp.zeros((length, head_count, head_width), jnp.float32)
    for block_index in range(length // row_count):
        start_row = block_index * row_count
        end_row = start_row + row_count
        query_lines = queries[start_row:end_row]
        scaled_lines = scaled[start_row:end_row]
        key_cols = keys[:end_row]
        value_cols = values[:end_row]
        row_pos = start_row + lax.iota(jnp.int32, row_count)
        col_pos = lax.iota(jnp.int32, end_row)
        causal = col_pos[None, :] <= row_pos[:, None]
        raw_scores = jnp.einsum(
            "tnd,snd->nts", query_lines, key_cols, preferred_element_type=jnp.float32
        )
        scores = jnp.where(causal[None], raw_scores, 0.0).astype(jnp.bfloat16)
        raw_grads = jnp.einsum(
            "tnd,snd->nts", scaled_lines, value_cols, preferred_element_type=jnp.float32
        )
        score_gradient = jnp.where(causal[None], raw_grads, 0.0).astype(jnp.bfloat16)
        local_out = jnp.einsum(
            "epa,aev->pev", scores, value_cols, preferred_element_type=jnp.float32
        )
        carried_result = jnp.einsum(
            "rwb,wbo->rwo", query_lines, forward_narrow, preferred_element_type=jnp.float32
        )
        row_scale = position_scale[start_row:end_row]
        outputs.append(
            ((local_out + carried_result) * row_scale[:, None, None]).astype(jnp.bfloat16)
        )
        local_query = jnp.einsum(
            "epa,aev->pev", score_gradient, key_cols, preferred_element_type=jnp.float32
        )
        carried_query = jnp.einsum(
            "hsx,smx->hsm", scaled_lines, forward_narrow, preferred_element_type=jnp.float32
        )
        query_grads.append((local_query + carried_query).astype(jnp.bfloat16))
        key_acc = key_acc.at[:end_row].add(
            jnp.einsum(
                "nts,tnd->snd", score_gradient, query_lines, preferred_element_type=jnp.float32
            )
        )
        value_acc = value_acc.at[:end_row].add(
            jnp.einsum("nts,tnd->snd", scores, scaled_lines, preferred_element_type=jnp.float32)
        )
    grad_key = (
        key_acc + jnp.einsum("snv,nvk->snk", values, back_low, preferred_element_type=jnp.float32)
    ).astype(jnp.bfloat16)
    grad_value = (
        value_acc + jnp.einsum("snk,nvk->snv", keys, back_low, preferred_element_type=jnp.float32)
    ).astype(jnp.bfloat16)
    return (
        jnp.concatenate(outputs, axis=0),
        jnp.concatenate(query_grads, axis=0),
        grad_key,
        grad_value,
    )


def attend(pieces):
    queries = pieces[0][:, 0]
    keys = pieces[1][:, 0]
    values = pieces[2][:, 0]
    out_grad = pieces[3][:, 0]
    length = queries.shape[0]
    head_width = queries.shape[2]
    span_index = lax.axis_index("span")
    position = span_index * length + lax.iota(jnp.int32, length)
    position_scale = 1.0 / jnp.sqrt(jnp.float32(head_width) * (position + 1).astype(jnp.float32))
    scaled = (out_grad.astype(jnp.float32) * position_scale[:, None, None]).astype(jnp.bfloat16)
    forward_within = jnp.einsum("xgy,xgi->gyi", keys, values, preferred_element_type=jnp.float32)
    back_local = jnp.einsum("tnv,tnk->nvk", scaled, queries, preferred_element_type=jnp.float32)
    every_fwd, every_back = (
        lax.all_gather(forward_within[None], "span", axis=0, tiled=True),
        lax.all_gather(back_local[None], "span", axis=0, tiled=True),
    )
    block_order = lax.iota(jnp.int32, every_fwd.shape[0])
    lower_mask = (block_order < span_index).astype(jnp.float32)[:, None, None, None]
    upper_mask = (block_order > span_index).astype(jnp.float32)[:, None, None, None]
    fwd_state = jnp.sum(every_fwd * lower_mask, axis=0)
    back_state = jnp.sum(every_back * upper_mask, axis=0)
    forward_narrow = fwd_state.astype(jnp.bfloat16)
    back_low = back_state.astype(jnp.bfloat16)
    results = block_work(queries, keys, values, scaled, position_scale, forward_narrow, back_low)
    return (results[0][:, None], results[1][:, None], results[2][:, None], results[3][:, None])


def split_heads(matrix, group_count):
    return matrix.reshape(matrix.shape[0], group_count, HEADS // group_count, DH)


def merge_heads(grouped):
    return grouped.reshape(grouped.shape[0], HEADS * DH)


def shards(queries, keys, values, out_grad):
    group_count = lax.axis_size("head")
    results = attend(
        (
            lax.all_to_all(
                split_heads(queries, group_count), "head", split_axis=1, concat_axis=0, tiled=True
            ),
            lax.all_to_all(
                split_heads(keys, group_count), "head", split_axis=1, concat_axis=0, tiled=True
            ),
            lax.all_to_all(
                split_heads(values, group_count), "head", split_axis=1, concat_axis=0, tiled=True
            ),
            lax.all_to_all(
                split_heads(out_grad, group_count), "head", split_axis=1, concat_axis=0, tiled=True
            ),
        )
    )
    returned = (
        lax.all_to_all(results[0], "head", split_axis=0, concat_axis=1, tiled=True),
        lax.all_to_all(results[1], "head", split_axis=0, concat_axis=1, tiled=True),
        lax.all_to_all(results[2], "head", split_axis=0, concat_axis=1, tiled=True),
        lax.all_to_all(results[3], "head", split_axis=0, concat_axis=1, tiled=True),
    )
    return (
        merge_heads(returned[0]),
        merge_heads(returned[1]),
        merge_heads(returned[2]),
        merge_heads(returned[3]),
    )


def solution(mesh):
    return jax.shard_map(
        shards,
        mesh=mesh,
        in_specs=(
            P(("span", "head"), None),
            P(("span", "head"), None),
            P(("span", "head"), None),
            P(("span", "head"), None),
        ),
        out_specs=(
            P(("span", "head"), None),
            P(("span", "head"), None),
            P(("span", "head"), None),
            P(("span", "head"), None),
        ),
        check_vma=False,
    )
```

profile of v0, /device:TPU:1, one launch (start us, length us, event | category | flops | bytes accessed | tf_op | source)
XLA Modules:
  0.0 180.1 jit_solution(9970101980685170848)
XLA Ops:
  7.2 1.4 copy.49
  9.6 5.4 %all-to-all-start.1 = ((bf16[128,4,4,128]{3,0,2,1:T(8,128)(2,1)}), bf16[128,4,4,128]{3,0,2,1:T(8,128)(2,1)S(1)}, u32[]{:S(2)}, u32[]{:S(2)}) async-start(bf16[128,4,4,128]{3,0,2,1:T(8,128)(2,1)} %copy.50), calls=%async_computation.1 | async-start | bytes 1048576 | tf_op jit(solution)/shard_map/all_to_all | solution.py:119
  16.3 12.8 %all-to-all-done.1 = bf16[128,4,4,128]{3,0,2,1:T(8,128)(2,1)S(1)} async-done(((bf16[128,4,4,128]{3,0,2,1:T(8,128)(2,1)}), bf16[128,4,4,128]{3,0,2,1:T(8,128)(2,1)S(1)}, u32[]{:S(2)}, u32[]{:S(2)}) %all-to-all-start.1) | async-done | bytes 524320 | tf_op jit(solution)/shard_map/all_to_all | solution.py:119
  29.0 3.5 %all-to-all-start.2 = ((bf16[128,4,4,128]{3,0,2,1:T(8,128)(2,1)}), bf16[128,4,4,128]{3,0,2,1:T(8,128)(2,1)S(1)}, u32[]{:S(2)}, u32[]{:S(2)}) async-start(bf16[128,4,4,128]{3,0,2,1:T(8,128)(2,1)} %copy.53), calls=%async_computation.2 | async-start | bytes 1048576 | tf_op jit(solution)/shard_map/all_to_all | solution.py:122
  32.6 13.9 %all-to-all-done.2 = bf16[128,4,4,128]{3,0,2,1:T(8,128)(2,1)S(1)} async-done(((bf16[128,4,4,128]{3,0,2,1:T(8,128)(2,1)}), bf16[128,4,4,128]{3,0,2,1:T(8,128)(2,1)S(1)}, u32[]{:S(2)}, u32[]{:S(2)}) %all-to-all-start.2) | async-done | bytes 524320 | tf_op jit(solution)/shard_map/all_to_all | solution.py:122
  48.9 3.5 %all-to-all-start = ((bf16[128,4,4,128]{3,0,2,1:T(8,128)(2,1)}), bf16[128,4,4,128]{3,0,2,1:T(8,128)(2,1)S(1)}, u32[]{:S(2)}, u32[]{:S(2)}) async-start(bf16[128,4,4,128]{3,0,2,1:T(8,128)(2,1)} %copy.47), calls=%async_computation | async-start | bytes 1048576 | tf_op jit(solution)/shard_map/all_to_all | solution.py:116
  53.7 12.7 %all-to-all-done = bf16[128,4,4,128]{3,0,2,1:T(8,128)(2,1)S(1)} async-done(((bf16[128,4,4,128]{3,0,2,1:T(8,128)(2,1)}), bf16[128,4,4,128]{3,0,2,1:T(8,128)(2,1)S(1)}, u32[]{:S(2)}, u32[]{:S(2)}) %all-to-all-start) | async-done | bytes 524320 | tf_op jit(solution)/shard_map/all_to_all | solution.py:116
  66.4 3.5 %all-to-all-start.4 = ((bf16[128,4,4,128]{3,0,2,1:T(8,128)(2,1)}), bf16[128,4,4,128]{3,0,2,1:T(8,128)(2,1)S(1)}, u32[]{:S(2)}, u32[]{:S(2)}) async-start(bf16[128,4,4,128]{3,0,2,1:T(8,128)(2,1)} %copy.61), calls=%async_computation.4 | async-start | bytes 1048576 | tf_op jit(solution)/shard_map/all_to_all | solution.py:125
  70.0 13.9 %all-to-all-done.4 = bf16[128,4,4,128]{3,0,2,1:T(8,128)(2,1)S(1)} async-done(((bf16[128,4,4,128]{3,0,2,1:T(8,128)(2,1)}), bf16[128,4,4,128]{3,0,2,1:T(8,128)(2,1)S(1)}, u32[]{:S(2)}, u32[]{:S(2)}) %all-to-all-start.4) | async-done | bytes 524320 | tf_op jit(solution)/shard_map/all_to_all | solution.py:125
  87.0 1.8 %select_convert_fusion = bf16[4,512,512]{2,1,0:T(8,128)(2,1)S(1)} fusion(bf16[512,4,128]{2,0,1:T(8,128)(2,1)} %copy-done, bf16[512,4,128]{2,0,1:T(8,128)(2,1)S(1)} %bitcast.115, pred[512,512]{1,0:T(8,128)(4,1)S(1)} %iota_compare_fusion), kind=kOutput, calls=%fused_computation | convolution fusion | flops 270532608 | bytes 3407872 | tf_op jit(solution)/shard_map/tnd,snd->nts/dot_general | solution.py:33
  88.8 1.7 convolution_bitcast_fusion.1
  90.5 1.9 %multiply_reduce_fusion.1 = bf16[4,128,128]{2,1,0:T(8,128)(2,1)S(1)} fusion(f32[8,4,128,128]{3,2,1,0:T(8,128)} %bitcast.123, f32[8]{0:T(128)S(1)} %compare_convert_fusion.1), kind=kLoop, calls=%fused_computation.3 | loop fusion | flops 983040 | bytes 2228256 | tf_op jit(solution)/shard_map/reduce_sum | solution.py:96
  92.8 1.2 copy.64
  94.0 4.1 %all-to-all-start.5 = ((bf16[512,1,4,128]{3,2,1,0:T(4,128)(2,1)}), bf16[512,1,4,128]{3,2,1,0:T(4,128)(2,1)}, u32[]{:S(2)}, u32[]{:S(2)}) async-start(bf16[512,1,4,128]{3,2,1,0:T(4,128)(2,1)} %copy.64), calls=%async_computation.5 | async-start | bytes 1048576 | tf_op jit(solution)/shard_map/all_to_all | solution.py:132
  98.2 2.9 %convolution_bitcast_fusion = f32[512,4,128]{2,0,1:T(8,128)} fusion(bf16[4,512,512]{2,1,0:T(8,128)(2,1)S(1)} %select_convert_fusion, bf16[512,4,128]{2,0,1:T(8,128)(2,1)} %bitcast.119), kind=kOutput, calls=%fused_computation.4 | convolution fusion | flops 268435456 | bytes 3670016 | tf_op jit(solution)/shard_map/nts,tnd->snd/dot_general | solution.py:55
  101.1 13.2 %all-gather.7.cloned.1.call-done = f32[32,128,128]{2,1,0:T(8,128)} async-done(((f32[4,128,128]{2,1,0:T(8,128)}), f32[32,128,128]{2,1,0:T(8,128)}) %all-gather.7.cloned.1.call-update) | async-done | bytes 2097168 | tf_op jit(solution)/shard_map/all_gather | solution.py:91
  114.3 1.8 %multiply_reduce_fusion = bf16[4,128,128]{2,1,0:T(8,128)(2,1)S(1)} fusion(f32[8,4,128,128]{3,2,1,0:T(8,128)} %bitcast.124, f32[8]{0:T(128)S(1)} %compare_convert_fusion), kind=kLoop, calls=%fused_computation.2 | loop fusion | flops 983040 | bytes 2228256 | tf_op jit(solution)/shard_map/reduce_sum | solution.py:97
  116.4 1.2 copy.70
  117.7 4.3 %all-to-all-start.6 = ((bf16[512,1,4,128]{3,2,1,0:T(4,128)(2,1)}), bf16[512,1,4,128]{3,2,1,0:T(4,128)(2,1)}, u32[]{:S(2)}, u32[]{:S(2)}) async-start(bf16[512,1,4,128]{3,2,1,0:T(4,128)(2,1)} %copy.70), calls=%async_computation.6 | async-start | bytes 1048576 | tf_op jit(solution)/shard_map/all_to_all | solution.py:133
  122.0 1.9 %select_convert_fusion.1 = bf16[4,512,512]{2,1,0:T(8,128)(2,1)S(1)} fusion(bf16[512,4,128]{2,0,1:T(8,128)(2,1)} %bitcast.120, bf16[512,4,128]{2,0,1:T(8,128)(2,1)S(1)} %bitcast.112, pred[512,512]{1,0:T(8,128)(4,1)} %copy-done.10), kind=kOutput, calls=%fused_computation.1 | convolution fusion | flops 270532608 | bytes 3407872 | tf_op jit(solution)/shard_map/tnd,snd->nts/dot_general | solution.py:29
  125.2 1.2 copy.58
  126.4 9.7 %all-to-all-done.6 = bf16[512,1,4,128]{3,2,1,0:T(4,128)(2,1)} async-done(((bf16[512,1,4,128]{3,2,1,0:T(4,128)(2,1)}), bf16[512,1,4,128]{3,2,1,0:T(4,128)(2,1)}, u32[]{:S(2)}, u32[]{:S(2)}) %all-to-all-start.6) | async-done | bytes 524320 | tf_op jit(solution)/shard_map/all_to_all | solution.py:133
  136.1 4.1 %all-to-all-start.3 = ((bf16[512,1,4,128]{3,2,1,0:T(4,128)(2,1)}), bf16[512,1,4,128]{3,2,1,0:T(4,128)(2,1)}, u32[]{:S(2)}, u32[]{:S(2)}) async-start(bf16[512,1,4,128]{3,2,1,0:T(4,128)(2,1)} %copy.58), calls=%async_computation.3 | async-start | bytes 1048576 | tf_op jit(solution)/shard_map/all_to_all | solution.py:131
  142.2 12.2 %all-to-all-done.3 = bf16[512,1,4,128]{3,2,1,0:T(4,128)(2,1)} async-done(((bf16[512,1,4,128]{3,2,1,0:T(4,128)(2,1)}), bf16[512,1,4,128]{3,2,1,0:T(4,128)(2,1)}, u32[]{:S(2)}, u32[]{:S(2)}) %all-to-all-start.3) | async-done | bytes 524320 | tf_op jit(solution)/shard_map/all_to_all | solution.py:131
  154.4 3.6 %all-to-all-start.7 = ((bf16[512,1,4,128]{3,2,1,0:T(4,128)(2,1)}), bf16[512,1,4,128]{3,2,1,0:T(4,128)(2,1)S(1)}, u32[]{:S(2)}, u32[]{:S(2)}) async-start(bf16[512,1,4,128]{3,2,1,0:T(4,128)(2,1)} %copy.73), calls=%async_computation.7 | async-start | bytes 1048576 | tf_op jit(solution)/shard_map/all_to_all | solution.py:134
  158.0 1.2 copy.65
  159.3 1.2 reshape.143
  160.5 1.2 copy.71
  161.7 1.2 reshape.144
  162.9 1.2 copy.59
  164.1 1.2 reshape.141
  165.3 6.6 %all-to-all-done.7 = bf16[512,1,4,128]{3,2,1,0:T(4,128)(2,1)S(1)} async-done(((bf16[512,1,4,128]{3,2,1,0:T(4,128)(2,1)}), bf16[512,1,4,128]{3,2,1,0:T(4,128)(2,1)S(1)}, u32[]{:S(2)}, u32[]{:S(2)}) %all-to-all-start.7) | async-done | bytes 524320 | tf_op jit(solution)/shard_map/all_to_all | solution.py:134
  (56 shorter events, 14.3 us)
Async XLA Ops:
  7.2 7.8 %copy-start.7 = (bf16[128,2048]{1,0:T(8,128)(2,1)S(1)}, bf16[128,2048]{1,0:T(8,128)(2,1)}, u32[]{:S(2)}) copy-start(bf16[128,2048]{1,0:T(8,128)(2,1)} %param.14) | copy-start | bytes 1572868
  9.6 19.5 %all-to-all-start.1 = ((bf16[128,4,4,128]{3,0,2,1:T(8,128)(2,1)}), bf16[128,4,4,128]{3,0,2,1:T(8,128)(2,1)S(1)}, u32[]{:S(2)}, u32[]{:S(2)}) async-start(bf16[128,4,4,128]{3,0,2,1:T(8,128)(2,1)} %copy.50), calls=%async_computation.1 | async-start | bytes 1048576 | tf_op jit(solution)/shard_map/all_to_all | solution.py:119
  29.0 17.5 %all-to-all-start.2 = ((bf16[128,4,4,128]{3,0,2,1:T(8,128)(2,1)}), bf16[128,4,4,128]{3,0,2,1:T(8,128)(2,1)S(1)}, u32[]{:S(2)}, u32[]{:S(2)}) async-start(bf16[128,4,4,128]{3,0,2,1:T(8,128)(2,1)} %copy.53), calls=%async_computation.2 | async-start | bytes 1048576 | tf_op jit(solution)/shard_map/all_to_all | solution.py:122
  32.5 15.1 %copy-start.8 = (bf16[128,2048]{1,0:T(8,128)(2,1)S(1)}, bf16[128,2048]{1,0:T(8,128)(2,1)}, u32[]{:S(2)}) copy-start(bf16[128,2048]{1,0:T(8,128)(2,1)} %param.12) | copy-start | bytes 1572868
  32.5 58.0 %all-gather.5.cloned.1.call-start = ((), (), s32[]{:S(2)}) async-start(), calls=%async_computation.8 | async-start | bytes 2359296 | tf_op jit(solution)/shard_map/all_gather | solution.py:90
  46.6 5.9 %copy-start.9 = (bf16[128,2048]{1,0:T(8,128)(2,1)S(1)}, bf16[128,2048]{1,0:T(8,128)(2,1)}, u32[]{:S(2)}) copy-start(bf16[128,2048]{1,0:T(8,128)(2,1)} %param.15) | copy-start | bytes 1572868
  48.9 17.5 %all-to-all-start = ((bf16[128,4,4,128]{3,0,2,1:T(8,128)(2,1)}), bf16[128,4,4,128]{3,0,2,1:T(8,128)(2,1)S(1)}, u32[]{:S(2)}, u32[]{:S(2)}) async-start(bf16[128,4,4,128]{3,0,2,1:T(8,128)(2,1)} %copy.47), calls=%async_computation | async-start | bytes 1048576 | tf_op jit(solution)/shard_map/all_to_all | solution.py:116
  66.4 17.5 %all-to-all-start.4 = ((bf16[128,4,4,128]{3,0,2,1:T(8,128)(2,1)}), bf16[128,4,4,128]{3,0,2,1:T(8,128)(2,1)S(1)}, u32[]{:S(2)}, u32[]{:S(2)}) async-start(bf16[128,4,4,128]{3,0,2,1:T(8,128)(2,1)} %copy.61), calls=%async_computation.4 | async-start | bytes 1048576 | tf_op jit(solution)/shard_map/all_to_all | solution.py:125
  69.9 44.4 %all-gather.7.cloned.1.call-start = ((), (), s32[]{:S(2)}) async-start(), calls=%async_computation.9 | async-start | bytes 2359296 | tf_op jit(solution)/shard_map/all_gather | solution.py:91
  70.0 14.3 %copy-start.3 = (bf16[4,128,1,4,128]{4,1,0,3,2:T(8,128)(2,1)}, bf16[4,128,1,4,128]{4,1,0,3,2:T(8,128)(2,1)S(1)}, u32[]{:S(2)}) copy-start(bf16[4,128,1,4,128]{4,1,0,3,2:T(8,128)(2,1)S(1)} %copy.48) | copy-start | bytes 1572868
  84.3 0.8 copy-start
  86.3 0.7 copy-start.10
  90.5 2.0 %copy-start.1 = (bf16[512,4,128]{2,0,1:T(8,128)(2,1)S(1)}, bf16[512,4,128]{2,0,1:T(8,128)(2,1)}, u32[]{:S(2)}) copy-start(bf16[512,4,128]{2,0,1:T(8,128)(2,1)} %copy-done) | copy-start | bytes 1572868
  90.5 2.0 %copy-start.6 = (f32[512,4,128]{2,0,1:T(8,128)S(1)}, f32[512,4,128]{2,0,1:T(8,128)}, u32[]{:S(2)}) copy-start(f32[512,4,128]{2,0,1:T(8,128)} %convolution_bitcast_fusion.1) | copy-start | bytes 3145732
  94.0 23.6 %all-to-all-start.5 = ((bf16[512,1,4,128]{3,2,1,0:T(4,128)(2,1)}), bf16[512,1,4,128]{3,2,1,0:T(4,128)(2,1)}, u32[]{:S(2)}, u32[]{:S(2)}) async-start(bf16[512,1,4,128]{3,2,1,0:T(4,128)(2,1)} %copy.64), calls=%async_computation.5 | async-start | bytes 1048576 | tf_op jit(solution)/shard_map/all_to_all | solution.py:132
  101.1 15.0 %copy-start.5 = (f32[512,4,128]{2,0,1:T(8,128)S(1)}, f32[512,4,128]{2,0,1:T(8,128)}, u32[]{:S(2)}) copy-start(f32[512,4,128]{2,0,1:T(8,128)} %convolution_bitcast_fusion) | copy-start | bytes 3145732
  117.7 18.5 %all-to-all-start.6 = ((bf16[512,1,4,128]{3,2,1,0:T(4,128)(2,1)}), bf16[512,1,4,128]{3,2,1,0:T(4,128)(2,1)}, u32[]{:S(2)}, u32[]{:S(2)}) async-start(bf16[512,1,4,128]{3,2,1,0:T(4,128)(2,1)} %copy.70), calls=%async_computation.6 | async-start | bytes 1048576 | tf_op jit(solution)/shard_map/all_to_all | solution.py:133
  123.9 1.0 copy-start.4
  124.9 15.4 %copy-start.2 = (bf16[512,4,128]{2,0,1:T(8,128)(2,1)S(1)}, bf16[512,4,128]{2,0,1:T(8,128)(2,1)}, u32[]{:S(2)}) copy-start(bf16[512,4,128]{2,0,1:T(8,128)(2,1)} %copy-done) | copy-start | bytes 1572868
  136.1 18.3 %all-to-all-start.3 = ((bf16[512,1,4,128]{3,2,1,0:T(4,128)(2,1)}), bf16[512,1,4,128]{3,2,1,0:T(4,128)(2,1)}, u32[]{:S(2)}, u32[]{:S(2)}) async-start(bf16[512,1,4,128]{3,2,1,0:T(4,128)(2,1)} %copy.58), calls=%async_computation.3 | async-start | bytes 1048576 | tf_op jit(solution)/shard_map/all_to_all | solution.py:131
  154.4 17.5 %all-to-all-start.7 = ((bf16[512,1,4,128]{3,2,1,0:T(4,128)(2,1)}), bf16[512,1,4,128]{3,2,1,0:T(4,128)(2,1)S(1)}, u32[]{:S(2)}, u32[]{:S(2)}) async-start(bf16[512,1,4,128]{3,2,1,0:T(4,128)(2,1)} %copy.73), calls=%async_computation.7 | async-start | bytes 1048576 | tf_op jit(solution)/shard_map/all_to_all | solution.py:134
Sparse Core Ops, SparseCore 0:
  47.8 27.9 all-gather.4
  86.3 27.9 all-gather.6
where the time goes:
time: 182 us; the launch traced here: 180 us
  waiting for transfers between devices  95 us (52%)
  starting transfers between devices  32.2 us (18%)
  local copies, waits for them, and re-layouts  21.6 us (12%)
  between operations  14.4 us (8%)
  matrix products  12.8 us (7%)
  other arithmetic  4.1 us (2%)
    all_to_all x1, waiting for transfers between devices, shards(): lax.all_to_all(split_heads(values, group_count), 'head', split_axis=1, co...  13.9 us
    all_to_all x1, waiting for transfers between devices, shards(): lax.all_to_all(split_heads(out_grad, group_count), 'head', split_axis=1,...  13.9 us
    all_gather x1, waiting for transfers between devices, attend(): lax.all_gather(back_local[None], 'span', axis=0, tiled=True)  13.2 us
    all_to_all x1, waiting for transfers between devices, shards(): lax.all_to_all(split_heads(keys, group_count), 'head', split_axis=1, conc...  12.8 us
    all_to_all x1, waiting for transfers between devices, shards(): lax.all_to_all(split_heads(queries, group_count), 'head', split_axis=1, c...  12.7 us
    all_to_all x1, waiting for transfers between devices, shards(): lax.all_to_all(results[0], 'head', split_axis=0, concat_axis=1, tiled=True)  12.2 us
    all_to_all x1, waiting for transfers between devices, shards(): lax.all_to_all(results[2], 'head', split_axis=0, concat_axis=1, tiled=True)  9.72 us
    all_to_all x1, waiting for transfers between devices, shards(): lax.all_to_all(results[3], 'head', split_axis=0, concat_axis=1, tiled=True)  6.61 us
  transfers between devices with their start and end apart: 10, of which 8 were waited for; matrix products, arithmetic and copies ran while one was open for 18% of the time, Pallas kernels for 0%

commit v1 on v0

v1 whole, which is shorter than its diff:
```python
import functools

import jax
import jax.numpy as jnp
from jax import lax
from jax.experimental import pallas as pl
from jax.experimental.pallas import tpu as pltpu
from jax.sharding import PartitionSpec as P

HEADS = 16
DH = 128
STEP = 4
F32 = jnp.float32
BF16 = jnp.bfloat16
NT = (((1,), (1,)), ((), ()))
TN = (((0,), (0,)), ((), ()))


def dot(a, b, dims=None):
    if dims is None:
        return jnp.dot(a, b, preferred_element_type=F32)
    return lax.dot_general(a, b, dims, preferred_element_type=F32)


def coef_of(base, length):
    position = base + lax.broadcasted_iota(jnp.int32, (length, DH), 0)
    return 1.0 / jnp.sqrt(jnp.float32(DH) * (position + 1).astype(F32))


def states_kernel(base, q_ref, k_ref, v_ref, g_ref, st_ref, scaled_ref):
    coef = coef_of(base[0], q_ref.shape[0])
    parts = DH // st_ref.shape[2]
    for h in range(STEP):
        cols = pl.ds(h * DH, DH)
        scaled = (g_ref[:, cols].astype(F32) * coef).astype(BF16)
        scaled_ref[:, cols] = scaled
        fwd = dot(k_ref[:, cols], v_ref[:, cols], TN).astype(BF16)
        back = dot(scaled, q_ref[:, cols], TN).astype(BF16)
        rows = pl.ds(h * parts, parts)
        st_ref[rows, 0] = fwd.reshape(parts, DH // parts, DH)
        st_ref[rows, 1] = back.reshape(parts, DH // parts, DH)


def scores_kernel(q_ref, k_ref, v_ref, c_ref, sc_ref, sct_ref, ds_ref, dst_ref):
    length = q_ref.shape[0]
    row = lax.broadcasted_iota(jnp.int32, (length, length), 0)
    col = lax.broadcasted_iota(jnp.int32, (length, length), 1)
    lower, upper = col <= row, col >= row
    for h in range(STEP):
        cols = pl.ds(h * DH, DH)
        q, k, v, c = q_ref[:, cols], k_ref[:, cols], v_ref[:, cols], c_ref[:, cols]
        sc_ref[h] = jnp.where(lower, dot(q, k, NT), 0.0).astype(BF16)
        sct_ref[h] = jnp.where(upper, dot(k, q, NT), 0.0).astype(BF16)
        ds_ref[h] = jnp.where(lower, dot(c, v, NT), 0.0).astype(BF16)
        dst_ref[h] = jnp.where(upper, dot(v, c, NT), 0.0).astype(BF16)


def scan_kernel(in_ref, out_ref):
    count = in_ref.shape[0]
    shape = in_ref.shape[2:]

    def step(i, carry):
        fwd, back = carry
        out_ref[i, 0] = fwd.astype(BF16)
        last = count - 1 - i
        out_ref[last, 1] = back.astype(BF16)
        return fwd + in_ref[i, 0].astype(F32), back + in_ref[last, 1].astype(F32)

    lax.fori_loop(0, count, step, (jnp.zeros(shape, F32), jnp.zeros(shape, F32)))


def final_kernel(
    base, q_ref, k_ref, v_ref, c_ref, sc_ref, sct_ref, ds_ref, dst_ref, fb_ref,
    out_ref, dq_ref, dk_ref, dv_ref,
):
    coef = coef_of(base[0], q_ref.shape[0])
    parts = DH // fb_ref.shape[2]
    for h in range(STEP):
        cols = pl.ds(h * DH, DH)
        q, k, v, c = q_ref[:, cols], k_ref[:, cols], v_ref[:, cols], c_ref[:, cols]
        rows = pl.ds(h * parts, parts)
        fwd = fb_ref[rows, 0].reshape(DH, DH)
        back = fb_ref[rows, 1].reshape(DH, DH)
        out_ref[:, cols] = ((dot(sc_ref[h], v) + dot(q, fwd)) * coef).astype(BF16)
        dq_ref[:, cols] = (dot(ds_ref[h], k) + dot(c, fwd, NT)).astype(BF16)
        dk_ref[:, cols] = (dot(dst_ref[h], q) + dot(v, back)).astype(BF16)
        dv_ref[:, cols] = (dot(sct_ref[h], c) + dot(k, back, NT)).astype(BF16)


def shards(queries, keys, values, out_grad):
    axes = ("span", "head")
    devices = lax.axis_size(axes)
    length, feat = queries.shape
    base = (lax.axis_index(axes) * length).astype(jnp.int32).reshape(1)
    share = feat // devices
    direct = share % 16 == 0
    block = share if direct else DH
    count = feat // block
    grid = (HEADS // STEP,)
    tokens = pl.BlockSpec((length, STEP * DH), lambda i: (0, i))
    scalar = pl.BlockSpec(memory_space=pltpu.SMEM)
    state = pl.BlockSpec((STEP * DH // block, 2, block, DH), lambda i: (i, 0, 0, 0))
    square = pl.BlockSpec((STEP, length, length), lambda i: (i, 0, 0))
    rows_of = jax.ShapeDtypeStruct((length, feat), BF16)
    square_of = jax.ShapeDtypeStruct((HEADS, length, length), BF16)
    state_of = jax.ShapeDtypeStruct((count, 2, block, DH), BF16)

    states, scaled = pl.pallas_call(
        states_kernel,
        grid=grid,
        in_specs=[scalar] + [tokens] * 4,
        out_specs=[state, tokens],
        out_shape=[state_of, rows_of],
        name="states",
    )(base, queries, keys, values, out_grad)
    squares = pl.pallas_call(
        scores_kernel,
        grid=grid,
        in_specs=[tokens] * 4,
        out_specs=[square] * 4,
        out_shape=[square_of] * 4,
        name="scores",
    )(queries, keys, values, scaled)

    if direct:
        gathered = lax.all_to_all(states, axes, split_axis=0, concat_axis=0, tiled=True)
        summed = pl.pallas_call(
            scan_kernel, out_shape=jax.ShapeDtypeStruct(gathered.shape, BF16), name="scan"
        )(gathered)
        carried = lax.all_to_all(summed, axes, split_axis=0, concat_axis=0, tiled=True)
    else:
        cut = states.swapaxes(1, 2).reshape(devices, share, 2, DH)
        gathered = lax.all_to_all(cut, axes, split_axis=0, concat_axis=0, tiled=True)
        wide = gathered.astype(F32)
        fwd = jnp.cumsum(wide[:, :, 0], axis=0) - wide[:, :, 0]
        back = jnp.flip(jnp.cumsum(jnp.flip(wide[:, :, 1], 0), axis=0), 0) - wide[:, :, 1]
        summed = jnp.stack((fwd, back), axis=2).astype(BF16)
        carried = lax.all_to_all(summed, axes, split_axis=0, concat_axis=0, tiled=True)
        carried = carried.reshape(count, block, 2, DH).swapaxes(1, 2)

    return pl.pallas_call(
        final_kernel,
        grid=grid,
        in_specs=[scalar] + [tokens] * 4 + [square] * 4 + [state],
        out_specs=[tokens] * 4,
        out_shape=[rows_of] * 4,
        name="final",
    )(base, queries, keys, values, scaled, *squares, carried)


def solution(mesh):
    spec = P(("span", "head"), None)
    return jax.shard_map(
        shards, mesh=mesh, in_specs=(spec,) * 4, out_specs=(spec,) * 4, check_vma=False
    )
```

time: 182 us -> 77.3 us (0.42)
  waiting for transfers between devices: 95 us -> 21.6 us
  blocking collectives: 0 us -> 33.5 us
  starting transfers between devices: 32.2 us -> 3.15 us
  local copies, waits for them, and re-layouts: 21.6 us -> 0.96 us
  Pallas kernels: 0 us -> 16.9 us
  between operations: 14.4 us -> 0.65 us
  matrix products: 12.8 us -> 0 us
  other arithmetic: 4.1 us -> 0 us
    all_to_all x8 -> x1, waiting for transfers between devices: 81.8 us -> 21.6 us  [shards(): lax.all_to_all(summed, axes, split_axis=0, concat_axis=0, tiled=True)]
    all_to_all x0 -> x1, blocking collectives: none -> 33.5 us  [shards(): lax.all_to_all(states, axes, split_axis=0, concat_axis=0, tiled=True)]
    all_to_all x8 -> x1, starting transfers between devices: 32.1 us -> 3.15 us  [shards(): lax.all_to_all(summed, axes, split_axis=0, concat_axis=0, tiled=True)]
    pallas_call x0 -> x4, Pallas kernels: none -> 16.9 us  [the longest x1 5.57 us: shards(): pl.pallas_call(final_kernel, grid=grid, in_specs=[scalar] + [tokens] * 4...]
    all_gather x2 -> x0, waiting for transfers between devices: 13.2 us -> none  [the longest x1 13.2 us: attend(): lax.all_gather(back_local[None], 'span', axis=0, tiled=True)]
    dot_general x12 -> x0, matrix products: 12.8 us -> none  [the longest x1 2.93 us: block_work(): jnp.einsum('nts,tnd->snd', score_gradient, query_lines, preferred_element...]
    reshape x8 -> x0, local copies, waits for them, and re-layouts: 8.78 us -> none  [the longest x4 4.73 us: merge_heads(): return grouped.reshape(grouped.shape[0], HEADS * DH)]
    broadcast_in_dim x4 -> x0, local copies, waits for them, and re-layouts: 4.67 us -> none  [the longest x1 1.2 us: attend(): results[1][:, None]]
  transfers between devices with their start and end apart: 10 -> 1, of which waited for: 8 -> 1; matrix products, arithmetic and copies ran while one was open for 18% -> 0% of each run, Pallas kernels for 0% -> 6%
where the time goes in v1:
time: 77.3 us; the launch traced here: 76.8 us
  blocking collectives  33.5 us (43%)
  waiting for transfers between devices  21.6 us (28%)
  Pallas kernels  16.9 us (22%)
  starting transfers between devices  3.15 us (4%)
  local copies, waits for them, and re-layouts  0.96 us (1%)
    all_to_all x1, blocking collectives, shards(): lax.all_to_all(states, axes, split_axis=0, concat_axis=0, tiled=True)  33.5 us
    all_to_all x1, waiting for transfers between devices, shards(): lax.all_to_all(summed, axes, split_axis=0, concat_axis=0, tiled=True)  21.6 us
    pallas_call x1, Pallas kernels, shards(): pl.pallas_call(final_kernel, grid=grid, in_specs=[scalar] + [tokens] * 4...  5.57 us
    pallas_call x1, Pallas kernels, shards(): pl.pallas_call(scores_kernel, grid=grid, in_specs=[tokens] * 4, out_specs...  4.7 us
    pallas_call x1, Pallas kernels, shards(): pl.pallas_call(states_kernel, grid=grid, in_specs=[scalar] + [tokens] * 4...  4.17 us
    all_to_all x1, starting transfers between devices, shards(): lax.all_to_all(summed, axes, split_axis=0, concat_axis=0, tiled=True)  3.15 us
    pallas_call x1, Pallas kernels, shards(): pl.pallas_call(scan_kernel, out_shape=jax.ShapeDtypeStruct(gathered.shape...  2.42 us
  transfers between devices with their start and end apart: 1, of which 1 were waited for; matrix products, arithmetic and copies ran while one was open for 0% of the time, Pallas kernels for 6%

profile of v1, /device:TPU:1, one launch (start us, length us, event | category | flops | bytes accessed | tf_op | source)
XLA Modules:
  0.0 76.8 jit_solution(6976314777812111895)
XLA Ops:
  0.6 4.2 %states.1 = (bf16[32,2,64,128]{3,2,1,0:T(8,128)(2,1)}, bf16[128,2048]{1,0:T(8,128)(2,1)}) custom-call(s32[1]{0:T(128)} %bitcast.base, bf16[128,2048]{1,0:T(8,128)(2,1)} %q_ref.5, bf16[128,2048]{1,0:T(8,128)(2,1)} %k_ref.5, bf16[128,2048]{1,0:T(8,128)(2,1)} %v_ref.5, bf16[128,2048]{1,0:T(8,128)(2,1)} %g_ref.1), custom_call_target="tpu_custom_call" | custom-call | tf_op jit(solution)/shard_map/states/pallas_call | solution.py:108
  4.8 33.5 %all_to_all.10.in_ref = bf16[32,2,64,128]{3,2,1,0:T(8,128)(2,1)} all-to-all(bf16[32,2,64,128]{3,2,1,0:T(8,128)(2,1)} %get-tuple-element.15), channel_id=1, replica_groups=mesh['head'=4,'span'=8] {'span','head'}, dimensions={0} | all-to-all | bytes 2097152 | tf_op jit(solution)/shard_map/all_to_all | solution.py:126
  38.3 2.4 %scan.1 = bf16[32,2,64,128]{3,2,1,0:T(8,128)(2,1)} custom-call(bf16[32,2,64,128]{3,2,1,0:T(8,128)(2,1)} %all_to_all.10.in_ref), custom_call_target="tpu_custom_call" | custom-call | tf_op jit(solution)/shard_map/scan/pallas_call | solution.py:127
  40.7 3.2 %all-to-all-start.1 = ((bf16[32,2,64,128]{3,2,1,0:T(8,128)(2,1)}), bf16[32,2,64,128]{3,2,1,0:T(8,128)(2,1)S(1)}, u32[]{:S(2)}, u32[]{:S(2)}) async-start(bf16[32,2,64,128]{3,2,1,0:T(8,128)(2,1)} %scan.1), calls=%async_computation.1 | async-start | bytes 2097152 | tf_op jit(solution)/shard_map/all_to_all | solution.py:130
  43.9 4.7 %scores.1 = (bf16[16,128,128]{2,1,0:T(8,128)(2,1)}, bf16[16,128,128]{2,1,0:T(8,128)(2,1)}, bf16[16,128,128]{2,1,0:T(8,128)(2,1)}, bf16[16,128,128]{2,1,0:T(8,128)(2,1)}) custom-call(bf16[128,2048]{1,0:T(8,128)(2,1)} %q_ref.5, bf16[128,2048]{1,0:T(8,128)(2,1)} %k_ref.5, bf16[128,2048]{1,0:T(8,128)(2,1)} %v_ref.5, bf16[128,2048]{1,0:T(8,128)(2,1)} %get-tuple-element.10.c_ref), custom_call_target="tpu_custom_call" | custom-call | tf_op jit(solution)/shard_map/scores/pallas_call | solution.py:116
  48.6 21.6 %all-to-all-done.1.fb_ref = bf16[32,2,64,128]{3,2,1,0:T(8,128)(2,1)S(1)} async-done(((bf16[32,2,64,128]{3,2,1,0:T(8,128)(2,1)}), bf16[32,2,64,128]{3,2,1,0:T(8,128)(2,1)S(1)}, u32[]{:S(2)}, u32[]{:S(2)}) %all-to-all-start.1) | async-done | bytes 1048608 | tf_op jit(solution)/shard_map/all_to_all | solution.py:130
  70.2 0.0 copy-start
  70.2 1.0 %copy-done = bf16[32,2,64,128]{3,2,1,0:T(8,128)(2,1)} copy-done((bf16[32,2,64,128]{3,2,1,0:T(8,128)(2,1)}, bf16[32,2,64,128]{3,2,1,0:T(8,128)(2,1)S(1)}, u32[]{:S(2)}) %copy-start) | copy-done | bytes 1048600
  71.2 5.6 %final.1 = (bf16[128,2048]{1,0:T(8,128)(2,1)}, bf16[128,2048]{1,0:T(8,128)(2,1)}, bf16[128,2048]{1,0:T(8,128)(2,1)}, bf16[128,2048]{1,0:T(8,128)(2,1)}) custom-call(s32[1]{0:T(128)} %bitcast.base, bf16[128,2048]{1,0:T(8,128)(2,1)} %q_ref.5, bf16[128,2048]{1,0:T(8,128)(2,1)} %k_ref.5, bf16[128,2048]{1,0:T(8,128)(2,1)} %v_ref.5, ...), custom_call_target="tpu_custom_call" | custom-call | tf_op jit(solution)/shard_map/final/pallas_call | solution.py:141
Async XLA Ops:
  40.7 29.5 %all-to-all-start.1 = ((bf16[32,2,64,128]{3,2,1,0:T(8,128)(2,1)}), bf16[32,2,64,128]{3,2,1,0:T(8,128)(2,1)S(1)}, u32[]{:S(2)}, u32[]{:S(2)}) async-start(bf16[32,2,64,128]{3,2,1,0:T(8,128)(2,1)} %scan.1), calls=%async_computation.1 | async-start | bytes 2097152 | tf_op jit(solution)/shard_map/all_to_all | solution.py:130
  70.2 1.0 %copy-start = (bf16[32,2,64,128]{3,2,1,0:T(8,128)(2,1)}, bf16[32,2,64,128]{3,2,1,0:T(8,128)(2,1)S(1)}, u32[]{:S(2)}) copy-start(bf16[32,2,64,128]{3,2,1,0:T(8,128)(2,1)S(1)} %all-to-all-done.1.fb_ref) | copy-start | bytes 3145732

commit v2 on v1

v2 whole, which is shorter than its diff:
```python
import jax
import jax.numpy as jnp
from jax import lax
from jax.experimental import pallas as pl
from jax.experimental.pallas import tpu as pltpu
from jax.sharding import PartitionSpec as P


HEADS = 16
DH = 128
F32 = jnp.float32
BF16 = jnp.bfloat16
NT = (((1,), (1,)), ((), ()))
TN = (((0,), (0,)), ((), ()))
AXES = ("span", "head")
VMEM = 20 * 2**20


def dot(a, b, dims=None):
    if dims is None:
        return jnp.dot(a, b, preferred_element_type=F32)
    return lax.dot_general(a, b, dims, preferred_element_type=F32)


def coef_of(length):
    base = lax.axis_index(AXES) * length
    position = base + lax.broadcasted_iota(jnp.int32, (length, DH), 0)
    return 1.0 / jnp.sqrt(jnp.float32(DH) * (position + 1).astype(F32))


def group_of(k, groups):
    return lax.axis_index("head") ^ k if groups > 1 else 0


def columns(k, groups, h):
    first = (group_of(k, groups) * (HEADS // groups) + h) * DH
    return pl.ds(pl.multiple_of(first, DH), DH)


def fwd_states_kernel(k_ref, v_ref, s_ref):
    parts = DH // s_ref.shape[1]
    for h in range(HEADS):
        cols = pl.ds(h * DH, DH)
        fwd = dot(k_ref[:, cols], v_ref[:, cols], TN).astype(BF16)
        s_ref[pl.ds(h * parts, parts)] = fwd.reshape(parts, DH // parts, DH)


def back_states_kernel(q_ref, g_ref, c_ref, *t_refs):
    coef = coef_of(q_ref.shape[0])
    groups = len(t_refs)
    for k in reversed(range(groups)):
        for h in range(HEADS // groups):
            cols = columns(k, groups, h)
            scaled = (g_ref[:, cols].astype(F32) * coef).astype(BF16)
            c_ref[:, cols] = scaled
            t_refs[k][pl.ds(h * DH, DH), :] = dot(scaled, q_ref[:, cols], TN).astype(BF16)


def scores_kernel(q_ref, k_ref, v_ref, c_ref, sc_ref, sct_ref, ds_ref, dst_ref):
    length = q_ref.shape[0]
    row = lax.broadcasted_iota(jnp.int32, (length, length), 0)
    col = lax.broadcasted_iota(jnp.int32, (length, length), 1)
    lower, upper = col <= row, col >= row
    for h in range(HEADS):
        cols = pl.ds(h * DH, DH)
        q, k, v, c = q_ref[:, cols], k_ref[:, cols], v_ref[:, cols], c_ref[:, cols]
        sc_ref[h] = jnp.where(lower, dot(q, k, NT), 0.0).astype(BF16)
        sct_ref[h] = jnp.where(upper, dot(k, q, NT), 0.0).astype(BF16)
        ds_ref[h] = jnp.where(lower, dot(c, v, NT), 0.0).astype(BF16)
        dst_ref[h] = jnp.where(upper, dot(v, c, NT), 0.0).astype(BF16)


def fwd_scan_kernel(in_ref, out_ref):
    def step(i, total):
        out_ref[i] = total.astype(BF16)
        return total + in_ref[i].astype(F32)

    lax.fori_loop(0, in_ref.shape[0], step, jnp.zeros(in_ref.shape[1:], F32), unroll=4)


def total_kernel(*refs):
    total = refs[0][...].astype(F32)
    for ref in refs[1:-1]:
        total += ref[...].astype(F32)
    refs[-1][...] = total.astype(BF16)


def pair_kernel(a_ref, b_ref, out_ref):
    out_ref[...] = (a_ref[...].astype(F32) + b_ref[...].astype(F32)).astype(BF16)


def back_combine_kernel(groups, pair_ref, *refs):
    chips = len(refs) - 2 * groups - 1
    t_refs, chip_refs = refs[:groups], refs[groups : groups + chips]
    b_refs, held = refs[groups + chips : -1], refs[-1]
    span, plane = lax.axis_index("span"), lax.axis_index("head")
    for k in range(groups):
        held[plane ^ k] = t_refs[k][...]
    total = jnp.where(span % 2 == 0, pair_ref[...].astype(F32), 0.0)
    chip = span // 2
    for k in range(chips):
        after = (chip ^ (k + 1)) > chip
        total += jnp.where(after, chip_refs[k][...].astype(F32), 0.0)
    for z in reversed(range(groups)):
        own = held[z].astype(F32)
        held[z] = total.astype(BF16)
        total += own
    for k in range(groups):
        b_refs[k][...] = held[plane ^ k]


def fwd_final_kernel(q_ref, k_ref, v_ref, c_ref, sc_ref, ds_ref, f_ref, out_ref, dq_ref):
    coef = coef_of(q_ref.shape[0])
    parts = DH // f_ref.shape[1]
    for h in range(HEADS):
        cols = pl.ds(h * DH, DH)
        fwd = f_ref[pl.ds(h * parts, parts)].reshape(DH, DH)
        own = dot(sc_ref[h], v_ref[:, cols]) + dot(q_ref[:, cols], fwd)
        out_ref[:, cols] = (own * coef).astype(BF16)
        dq = dot(ds_ref[h], k_ref[:, cols]) + dot(c_ref[:, cols], fwd, NT)
        dq_ref[:, cols] = dq.astype(BF16)


def back_final_kernel(q_ref, k_ref, v_ref, c_ref, sct_ref, dst_ref, *refs):
    b_refs, dk_ref, dv_ref = refs[:-2], refs[-2], refs[-1]
    groups = len(b_refs)
    for k in range(groups):
        for h in range(HEADS // groups):
            cols = columns(k, groups, h)
            head = group_of(k, groups) * (HEADS // groups) + h
            back = b_refs[k][pl.ds(h * DH, DH), :]
            dk = dot(dst_ref[head], q_ref[:, cols]) + dot(v_ref[:, cols], back)
            dk_ref[:, cols] = dk.astype(BF16)
            dv = dot(sct_ref[head], c_ref[:, cols]) + dot(k_ref[:, cols], back, NT)
            dv_ref[:, cols] = dv.astype(BF16)


def exchange(x):
    return lax.all_to_all(x, AXES, split_axis=0, concat_axis=0, tiled=True)


def swap(x, axis, k):
    return lax.ppermute(x, axis, [(i, i ^ k) for i in range(lax.axis_size(axis))])


def call(kernel, out, flops, *args, scratch=()):
    moved = sum(a.size * a.dtype.itemsize for a in args)
    return pl.pallas_call(
        kernel,
        out_shape=out,
        scratch_shapes=list(scratch),
        cost_estimate=pl.CostEstimate(flops=flops, bytes_accessed=2 * moved, transcendentals=0),
        compiler_params=pltpu.CompilerParams(vmem_limit_bytes=VMEM),
    )(*args)


def shards(queries, keys, values, out_grad):
    devices, planes, span = lax.axis_size(AXES), lax.axis_size("head"), lax.axis_size("span")
    length, feat = queries.shape
    share = feat // devices
    direct = direct_on(devices, planes, span)
    block = share if direct else DH
    groups = planes if direct else 1
    rows_of = jax.ShapeDtypeStruct((length, feat), BF16)
    square_of = jax.ShapeDtypeStruct((HEADS, length, length), BF16)
    state_of = jax.ShapeDtypeStruct((feat // block, block, DH), BF16)
    piece_of = jax.ShapeDtypeStruct((feat // groups, DH), BF16)
    matmul = 2 * HEADS * length * DH * DH

    scaled, *back_states = call(
        back_states_kernel, [rows_of] + [piece_of] * groups, matmul,
        queries, out_grad,
    )
    if direct:
        own = [back_states[0]] + [swap(back_states[k], "head", k) for k in range(1, groups)]
    states = call(fwd_states_kernel, state_of, matmul, keys, values)
    if direct:
        gathered = exchange(states)
        fwd = exchange(
            call(fwd_scan_kernel, jax.ShapeDtypeStruct(gathered.shape, BF16), 0, gathered),
        )
        total = call(total_kernel, piece_of, 0, *own)
        other = swap(total, "span", 1)
        chip = call(pair_kernel, piece_of, 0, total, other)
        chips = [swap(chip, "span", 2 * k) for k in range(1, span // 2)]
        carried = call(
            lambda *refs: back_combine_kernel(groups, *refs),
            [piece_of] * groups, 0, other, *own, *chips,
            scratch=[pltpu.VMEM((groups, feat // groups, DH), BF16)],
        )
        back = [carried[0]] + [swap(carried[k], "head", k) for k in range(1, groups)]
    else:
        wide = exchange(states.reshape(devices, share, DH)).astype(F32)
        before = jnp.cumsum(wide, axis=0) - wide
        fwd = exchange(before.astype(BF16)).reshape(states.shape)
        wide = jnp.flip(exchange(back_states[0].reshape(devices, share, DH)), 0).astype(F32)
        after = jnp.flip(jnp.cumsum(wide, axis=0) - wide, 0)
        back = [exchange(after.astype(BF16)).reshape(feat, DH)]

    rows = (queries, keys, values, scaled)
    sc, sct, ds, dst = call(scores_kernel, [square_of] * 4, 4 * matmul, *rows)
    dk, dv = call(back_final_kernel, [rows_of] * 2, 4 * matmul, *rows, sct, dst, *back)
    out, dq = call(fwd_final_kernel, [rows_of] * 2, 4 * matmul, *rows, sc, ds, fwd)
    return out, dq, dk, dv


def direct_on(devices, planes, span):
    return HEADS * DH // devices % 16 == 0 and planes in (2, 4) and span in (2, 4, 8)


def solution(mesh):
    spec = P(AXES, None)

    return jax.shard_map(
        shards, mesh=mesh, in_specs=(spec,) * 4, out_specs=(spec,) * 4, check_vma=False
    )
```

time: 77.3 us -> 84.6 us (1.094)
  the two profiles are of different devices: /device:TPU:1 before, /device:TPU:0 now
where the time goes in v2:
time: 84.6 us; the launch traced here: 84.3 us
  waiting for transfers between devices  33.1 us (39%)
  blocking collectives  21.4 us (25%)
  starting transfers between devices  17.6 us (21%)
  Pallas kernels  7.54 us (9%)
  local copies, waits for them, and re-layouts  3.93 us (5%)
    ppermute x10, waiting for transfers between devices, swap(): lax.ppermute(x, axis, [(i, i ^ k) for i in range(lax.axis_size(axis))])  33.1 us
    all_to_all x1, blocking collectives, exchange(): return lax.all_to_all(x, AXES, split_axis=0, concat_axis=0, tiled=True)  21.4 us
    ppermute x10, starting transfers between devices, swap(): lax.ppermute(x, axis, [(i, i ^ k) for i in range(lax.axis_size(axis))])  13.4 us
    pallas_call x9, Pallas kernels, call(): pl.pallas_call(kernel, out_shape=out, scratch_shapes=list(scratch), cost_...  7.54 us
    all_to_all x1, starting transfers between devices, exchange(): return lax.all_to_all(x, AXES, split_axis=0, concat_axis=0, tiled=True)  4.17 us
    unnamed x16, local copies, waits for them, and re-layouts  3.93 us
  transfers between devices with their start and end apart: 11, of which 6 were waited for; matrix products, arithmetic and copies ran while one was open for 0% of the time, Pallas kernels for 5%

profile of v2, /device:TPU:0, one launch (start us, length us, event | category | flops | bytes accessed | tf_op | source)
XLA Modules:
  0.0 84.3 jit_solution(5236730015846903074)
XLA Ops:
  0.6 1.0 %copy-done = bf16[128,2048]{1,0:T(8,128)(2,1)S(1)} copy-done((bf16[128,2048]{1,0:T(8,128)(2,1)S(1)}, bf16[128,2048]{1,0:T(8,128)(2,1)}, u32[]{:S(2)}) %copy-start) | copy-done | bytes 524312
  1.7 1.0 %copy-done.2 = bf16[128,2048]{1,0:T(8,128)(2,1)S(1)} copy-done((bf16[128,2048]{1,0:T(8,128)(2,1)S(1)}, bf16[128,2048]{1,0:T(8,128)(2,1)}, u32[]{:S(2)}) %copy-start.2) | copy-done | bytes 524312
  2.7 0.3 shard_map.77
  3.1 21.4 %all_to_all.10.in_ref = bf16[32,64,128]{2,1,0:T(8,128)(2,1)S(1)} all-to-all(bf16[32,64,128]{2,1,0:T(8,128)(2,1)S(1)} %shard_map.77), channel_id=1, replica_groups=mesh['head'=4,'span'=8] {'span','head'}, dimensions={0} | all-to-all | bytes 1048576 | tf_op jit(solution)/shard_map/all_to_all | solution.py:139
  24.4 0.9 %shard_map.78 = bf16[32,64,128]{2,1,0:T(8,128)(2,1)} custom-call(bf16[32,64,128]{2,1,0:T(8,128)(2,1)S(1)} %all_to_all.10.in_ref), custom_call_target="tpu_custom_call" | custom-call | bytes 1048576 | tf_op jit(solution)/shard_map/pallas_call | solution.py:148
  25.3 4.2 %all-to-all-start.1 = ((bf16[32,64,128]{2,1,0:T(8,128)(2,1)}), bf16[32,64,128]{2,1,0:T(8,128)(2,1)S(1)}, u32[]{:S(2)}, u32[]{:S(2)}) async-start(bf16[32,64,128]{2,1,0:T(8,128)(2,1)} %shard_map.78), calls=%async_computation.1 | async-start | bytes 1048576 | tf_op jit(solution)/shard_map/all_to_all | solution.py:139
  29.6 0.5 shard_map.75
  30.0 1.8 %collective-permute-start = (bf16[512,128]{1,0:T(8,128)(2,1)S(1)}, bf16[512,128]{1,0:T(8,128)(2,1)S(1)}, u32[]{:S(2)}, u32[]{:S(2)}) collective-permute-start(bf16[512,128]{1,0:T(8,128)(2,1)S(1)} %get-tuple-element.29), channel_id=1, source_target_pairs={{0,8},{8,0},{16,24},{24,16},{1,9},{9,1},{17,25},{25,17},{2,10},{10... | collective-permute-start | bytes 393224 | tf_op jit(solution)/shard_map/ppermute | solution.py:143
  31.9 2.4 %collective-permute-start.1 = (bf16[512,128]{1,0:T(8,128)(2,1)S(1)}, bf16[512,128]{1,0:T(8,128)(2,1)S(1)}, u32[]{:S(2)}, u32[]{:S(2)}) collective-permute-start(bf16[512,128]{1,0:T(8,128)(2,1)S(1)} %get-tuple-element.30), channel_id=1, source_target_pairs={{0,16},{8,24},{16,0},{24,8},{1,17},{9,25},{17,1},{25,9},{2,18},{10... | collective-permute-start | bytes 393224 | tf_op jit(solution)/shard_map/ppermute | solution.py:143
  34.3 0.2 collective-permute-start.2
  34.5 8.4 %collective-permute-done.refs_1_.refs_2_ = bf16[512,128]{1,0:T(8,128)(2,1)S(1)} collective-permute-done((bf16[512,128]{1,0:T(8,128)(2,1)S(1)}, bf16[512,128]{1,0:T(8,128)(2,1)S(1)}, u32[]{:S(2)}, u32[]{:S(2)}) %collective-permute-start) | collective-permute-done | bytes 131104 | tf_op jit(solution)/shard_map/ppermute | solution.py:143
  42.9 10.6 %collective-permute-done.1.refs_2_.refs_3_ = bf16[512,128]{1,0:T(8,128)(2,1)S(1)} collective-permute-done((bf16[512,128]{1,0:T(8,128)(2,1)S(1)}, bf16[512,128]{1,0:T(8,128)(2,1)S(1)}, u32[]{:S(2)}, u32[]{:S(2)}) %collective-permute-start.1) | collective-permute-done | bytes 131104 | tf_op jit(solution)/shard_map/ppermute | solution.py:143
  53.5 0.1 shard_map.80.a_ref
  53.6 0.1 collective-permute-start.3
  53.7 1.3 %collective-permute-done.3.b_ref.refs_0_ = bf16[512,128]{1,0:T(8,128)(2,1)S(1)} collective-permute-done((bf16[512,128]{1,0:T(8,128)(2,1)S(1)}, bf16[512,128]{1,0:T(8,128)(2,1)S(1)}, u32[]{:S(2)}, u32[]{:S(2)}) %collective-permute-start.3) | collective-permute-done | bytes 131104 | tf_op jit(solution)/shard_map/ppermute | solution.py:143
  55.0 0.0 copy-start.1
  55.0 1.5 %collective-permute-start.4 = (bf16[512,128]{1,0:T(8,128)(2,1)S(1)}, bf16[512,128]{1,0:T(8,128)(2,1)S(1)}, u32[]{:S(2)}, u32[]{:S(2)}) collective-permute-start(bf16[512,128]{1,0:T(8,128)(2,1)S(1)} %shard_map.81), channel_id=1, source_target_pairs={{0,2},{1,3},{2,0},{3,1},{4,6},{5,7},{6,4},{7,5},{8,10},{9,11},{10,... | collective-permute-start | bytes 393224 | tf_op jit(solution)/shard_map/ppermute | solution.py:143
  56.6 1.5 %collective-permute-start.5 = (bf16[512,128]{1,0:T(8,128)(2,1)S(1)}, bf16[512,128]{1,0:T(8,128)(2,1)S(1)}, u32[]{:S(2)}, u32[]{:S(2)}) collective-permute-start(bf16[512,128]{1,0:T(8,128)(2,1)S(1)} %shard_map.81), channel_id=1, source_target_pairs={{0,4},{1,5},{2,6},{3,7},{4,0},{5,1},{6,2},{7,3},{8,12},{9,13},{10,... | collective-permute-start | bytes 393224 | tf_op jit(solution)/shard_map/ppermute | solution.py:143
  58.1 0.5 collective-permute-start.6
  58.6 2.5 %collective-permute-done.4.refs_5_ = bf16[512,128]{1,0:T(8,128)(2,1)S(1)} collective-permute-done((bf16[512,128]{1,0:T(8,128)(2,1)S(1)}, bf16[512,128]{1,0:T(8,128)(2,1)S(1)}, u32[]{:S(2)}, u32[]{:S(2)}) %collective-permute-start.4) | collective-permute-done | bytes 131104 | tf_op jit(solution)/shard_map/ppermute | solution.py:143
  61.1 3.6 %collective-permute-done.5.refs_6_ = bf16[512,128]{1,0:T(8,128)(2,1)S(1)} collective-permute-done((bf16[512,128]{1,0:T(8,128)(2,1)S(1)}, bf16[512,128]{1,0:T(8,128)(2,1)S(1)}, u32[]{:S(2)}, u32[]{:S(2)}) %collective-permute-start.5) | collective-permute-done | bytes 131104 | tf_op jit(solution)/shard_map/ppermute | solution.py:143
  64.7 0.3 shard_map.82
  65.0 2.9 %collective-permute-start.7 = (bf16[512,128]{1,0:T(8,128)(2,1)S(1)}, bf16[512,128]{1,0:T(8,128)(2,1)S(1)}, u32[]{:S(2)}, u32[]{:S(2)}) collective-permute-start(bf16[512,128]{1,0:T(8,128)(2,1)S(1)} %get-tuple-element.33), channel_id=1, source_target_pairs={{0,8},{8,0},{16,24},{24,16},{1,9},{9,1},{17,25},{25,17},{2,10},{10... | collective-permute-start | bytes 393224 | tf_op jit(solution)/shard_map/ppermute | solution.py:143
  67.9 0.1 collective-permute-start.8
  67.9 2.4 %collective-permute-start.9 = (bf16[512,128]{1,0:T(8,128)(2,1)S(1)}, bf16[512,128]{1,0:T(8,128)(2,1)S(1)}, u32[]{:S(2)}, u32[]{:S(2)}) collective-permute-start(bf16[512,128]{1,0:T(8,128)(2,1)S(1)} %get-tuple-element.35), channel_id=1, source_target_pairs={{0,24},{8,16},{16,8},{24,0},{1,25},{9,17},{17,9},{25,1},{2,26},{10... | collective-permute-start | bytes 393224 | tf_op jit(solution)/shard_map/ppermute | solution.py:143
  70.3 1.6 %shard_map.76 = (bf16[16,128,128]{2,1,0:T(8,128)(2,1)S(1)}, bf16[16,128,128]{2,1,0:T(8,128)(2,1)S(1)}, bf16[16,128,128]{2,1,0:T(8,128)(2,1)S(1)}, bf16[16,128,128]{2,1,0:T(8,128)(2,1)S(1)}) custom-call(bf16[128,2048]{1,0:T(8,128)(2,1)S(1)} %copy-done.4, bf16[128,2048]{1,0:T(8,128)(2,1)S(1)} %copy-done.1, bf16[128,2048]{1,0:T(8,128)(2,1)S(1)} %copy-done.3, ...), custom_call_target="tpu_custom_call" | custom-call | flops 268435456 | bytes 4194304 | tf_op jit(solution)/shard_map/pallas_call | solution.py:148
  71.9 0.0 copy-start.5
  71.9 0.8 copy-done.5
  72.7 6.7 %collective-permute-done.8.refs_2_ = bf16[512,128]{1,0:T(8,128)(2,1)S(1)} collective-permute-done((bf16[512,128]{1,0:T(8,128)(2,1)S(1)}, bf16[512,128]{1,0:T(8,128)(2,1)S(1)}, u32[]{:S(2)}, u32[]{:S(2)}) %collective-permute-start.8) | collective-permute-done | bytes 131104 | tf_op jit(solution)/shard_map/ppermute | solution.py:143
  79.4 1.9 %shard_map.83 = (bf16[128,2048]{1,0:T(8,128)(2,1)}, bf16[128,2048]{1,0:T(8,128)(2,1)}) custom-call(bf16[128,2048]{1,0:T(8,128)(2,1)S(1)} %copy-done.4, bf16[128,2048]{1,0:T(8,128)(2,1)S(1)} %copy-done.1, bf16[128,2048]{1,0:T(8,128)(2,1)S(1)} %copy-done.3, bf16[128,2048]{1,0:T(8,128)(2,1)S(1)} %get-tuple-element.21.c_ref, ...), custom_call_target="tpu_custom_call" | custom-call | flops 268435456 | bytes 7340032 | tf_op jit(solution)/shard_map/pallas_call | solution.py:148
  81.3 1.0 %copy-done.6 = bf16[16,128,128]{2,1,0:T(8,128)(2,1)S(1)} copy-done((bf16[16,128,128]{2,1,0:T(8,128)(2,1)S(1)}, bf16[16,128,128]{2,1,0:T(8,128)(2,1)}, u32[]{:S(2)}) %copy-start.6) | copy-done | bytes 524312
  82.4 1.9 %shard_map.79 = (bf16[128,2048]{1,0:T(8,128)(2,1)}, bf16[128,2048]{1,0:T(8,128)(2,1)}) custom-call(bf16[128,2048]{1,0:T(8,128)(2,1)S(1)} %copy-done.4, bf16[128,2048]{1,0:T(8,128)(2,1)S(1)} %copy-done.1, bf16[128,2048]{1,0:T(8,128)(2,1)S(1)} %copy-done.3, bf16[128,2048]{1,0:T(8,128)(2,1)S(1)} %get-tuple-element.21.c_ref, ...), custom_call_target="tpu_custom_call" | custom-call | flops 268435456 | bytes 7340032 | tf_op jit(solution)/shard_map/pallas_call | solution.py:148
  (16 shorter events, 0.1 us)
Async XLA Ops:
  0.6 1.0 %copy-start = (bf16[128,2048]{1,0:T(8,128)(2,1)S(1)}, bf16[128,2048]{1,0:T(8,128)(2,1)}, u32[]{:S(2)}) copy-start(bf16[128,2048]{1,0:T(8,128)(2,1)} %k_ref.7) | copy-start | bytes 1572868
  1.7 1.0 %copy-start.2 = (bf16[128,2048]{1,0:T(8,128)(2,1)S(1)}, bf16[128,2048]{1,0:T(8,128)(2,1)}, u32[]{:S(2)}) copy-start(bf16[128,2048]{1,0:T(8,128)(2,1)} %v_ref.7) | copy-start | bytes 1572868
  25.3 4.2 %copy-start.4 = (bf16[128,2048]{1,0:T(8,128)(2,1)S(1)}, bf16[128,2048]{1,0:T(8,128)(2,1)}, u32[]{:S(2)}) copy-start(bf16[128,2048]{1,0:T(8,128)(2,1)} %q_ref.7) | copy-start | bytes 1572868
  25.3 4.2 %copy-start.7 = (bf16[128,2048]{1,0:T(8,128)(2,1)S(1)}, bf16[128,2048]{1,0:T(8,128)(2,1)}, u32[]{:S(2)}) copy-start(bf16[128,2048]{1,0:T(8,128)(2,1)} %g_ref.1) | copy-start | bytes 1572868
  25.3 56.0 %all-to-all-start.1 = ((bf16[32,64,128]{2,1,0:T(8,128)(2,1)}), bf16[32,64,128]{2,1,0:T(8,128)(2,1)S(1)}, u32[]{:S(2)}, u32[]{:S(2)}) async-start(bf16[32,64,128]{2,1,0:T(8,128)(2,1)} %shard_map.78), calls=%async_computation.1 | async-start | bytes 1048576 | tf_op jit(solution)/shard_map/all_to_all | solution.py:139
  30.0 12.9 %collective-permute-start = (bf16[512,128]{1,0:T(8,128)(2,1)S(1)}, bf16[512,128]{1,0:T(8,128)(2,1)S(1)}, u32[]{:S(2)}, u32[]{:S(2)}) collective-permute-start(bf16[512,128]{1,0:T(8,128)(2,1)S(1)} %get-tuple-element.29), channel_id=1, source_target_pairs={{0,8},{8,0},{16,24},{24,16},{1,9},{9,1},{17,25},{25,17},{2,10},{10... | collective-permute-start | bytes 393224 | tf_op jit(solution)/shard_map/ppermute | solution.py:143
  31.9 21.6 %collective-permute-start.1 = (bf16[512,128]{1,0:T(8,128)(2,1)S(1)}, bf16[512,128]{1,0:T(8,128)(2,1)S(1)}, u32[]{:S(2)}, u32[]{:S(2)}) collective-permute-start(bf16[512,128]{1,0:T(8,128)(2,1)S(1)} %get-tuple-element.30), channel_id=1, source_target_pairs={{0,16},{8,24},{16,0},{24,8},{1,17},{9,25},{17,1},{25,9},{2,18},{10... | collective-permute-start | bytes 393224 | tf_op jit(solution)/shard_map/ppermute | solution.py:143
  34.3 19.2 %collective-permute-start.2 = (bf16[512,128]{1,0:T(8,128)(2,1)S(1)}, bf16[512,128]{1,0:T(8,128)(2,1)S(1)}, u32[]{:S(2)}, u32[]{:S(2)}) collective-permute-start(bf16[512,128]{1,0:T(8,128)(2,1)S(1)} %get-tuple-element.31), channel_id=1, source_target_pairs={{0,24},{8,16},{16,8},{24,0},{1,25},{9,17},{17,9},{25,1},{2,26},{10... | collective-permute-start | bytes 393224 | tf_op jit(solution)/shard_map/ppermute | solution.py:143
  53.6 1.4 %collective-permute-start.3 = (bf16[512,128]{1,0:T(8,128)(2,1)S(1)}, bf16[512,128]{1,0:T(8,128)(2,1)S(1)}, u32[]{:S(2)}, u32[]{:S(2)}) collective-permute-start(bf16[512,128]{1,0:T(8,128)(2,1)S(1)} %shard_map.80.a_ref), channel_id=1, source_target_pairs={{0,1},{1,0},{2,3},{3,2},{4,5},{5,4},{6,7},{7,6},{8,9},{9,8},{10,11... | collective-permute-start | bytes 393224 | tf_op jit(solution)/shard_map/ppermute | solution.py:143
  55.0 15.3 %copy-start.1 = (bf16[128,2048]{1,0:T(8,128)(2,1)S(1)}, bf16[128,2048]{1,0:T(8,128)(2,1)}, u32[]{:S(2)}) copy-start(bf16[128,2048]{1,0:T(8,128)(2,1)} %k_ref.7) | copy-start | bytes 1572868
  55.0 15.3 %copy-start.3 = (bf16[128,2048]{1,0:T(8,128)(2,1)S(1)}, bf16[128,2048]{1,0:T(8,128)(2,1)}, u32[]{:S(2)}) copy-start(bf16[128,2048]{1,0:T(8,128)(2,1)} %v_ref.7) | copy-start | bytes 1572868
  55.0 6.0 %collective-permute-start.4 = (bf16[512,128]{1,0:T(8,128)(2,1)S(1)}, bf16[512,128]{1,0:T(8,128)(2,1)S(1)}, u32[]{:S(2)}, u32[]{:S(2)}) collective-permute-start(bf16[512,128]{1,0:T(8,128)(2,1)S(1)} %shard_map.81), channel_id=1, source_target_pairs={{0,2},{1,3},{2,0},{3,1},{4,6},{5,7},{6,4},{7,5},{8,10},{9,11},{10,... | collective-permute-start | bytes 393224 | tf_op jit(solution)/shard_map/ppermute | solution.py:143
  56.6 8.1 %collective-permute-start.5 = (bf16[512,128]{1,0:T(8,128)(2,1)S(1)}, bf16[512,128]{1,0:T(8,128)(2,1)S(1)}, u32[]{:S(2)}, u32[]{:S(2)}) collective-permute-start(bf16[512,128]{1,0:T(8,128)(2,1)S(1)} %shard_map.81), channel_id=1, source_target_pairs={{0,4},{1,5},{2,6},{3,7},{4,0},{5,1},{6,2},{7,3},{8,12},{9,13},{10,... | collective-permute-start | bytes 393224 | tf_op jit(solution)/shard_map/ppermute | solution.py:143
  58.1 6.6 %collective-permute-start.6 = (bf16[512,128]{1,0:T(8,128)(2,1)S(1)}, bf16[512,128]{1,0:T(8,128)(2,1)S(1)}, u32[]{:S(2)}, u32[]{:S(2)}) collective-permute-start(bf16[512,128]{1,0:T(8,128)(2,1)S(1)} %shard_map.81), channel_id=1, source_target_pairs={{0,6},{1,7},{2,4},{3,5},{4,2},{5,3},{6,0},{7,1},{8,14},{9,15},{10,... | collective-permute-start | bytes 393224 | tf_op jit(solution)/shard_map/ppermute | solution.py:143
  65.0 7.7 %collective-permute-start.7 = (bf16[512,128]{1,0:T(8,128)(2,1)S(1)}, bf16[512,128]{1,0:T(8,128)(2,1)S(1)}, u32[]{:S(2)}, u32[]{:S(2)}) collective-permute-start(bf16[512,128]{1,0:T(8,128)(2,1)S(1)} %get-tuple-element.33), channel_id=1, source_target_pairs={{0,8},{8,0},{16,24},{24,16},{1,9},{9,1},{17,25},{25,17},{2,10},{10... | collective-permute-start | bytes 393224 | tf_op jit(solution)/shard_map/ppermute | solution.py:143
  67.9 11.5 %collective-permute-start.8 = (bf16[512,128]{1,0:T(8,128)(2,1)S(1)}, bf16[512,128]{1,0:T(8,128)(2,1)S(1)}, u32[]{:S(2)}, u32[]{:S(2)}) collective-permute-start(bf16[512,128]{1,0:T(8,128)(2,1)S(1)} %get-tuple-element.34), channel_id=1, source_target_pairs={{0,16},{8,24},{16,0},{24,8},{1,17},{9,25},{17,1},{25,9},{2,18},{10... | collective-permute-start | bytes 393224 | tf_op jit(solution)/shard_map/ppermute | solution.py:143
  67.9 11.4 %collective-permute-start.9 = (bf16[512,128]{1,0:T(8,128)(2,1)S(1)}, bf16[512,128]{1,0:T(8,128)(2,1)S(1)}, u32[]{:S(2)}, u32[]{:S(2)}) collective-permute-start(bf16[512,128]{1,0:T(8,128)(2,1)S(1)} %get-tuple-element.35), channel_id=1, source_target_pairs={{0,24},{8,16},{16,8},{24,0},{1,25},{9,17},{17,9},{25,1},{2,26},{10... | collective-permute-start | bytes 393224 | tf_op jit(solution)/shard_map/ppermute | solution.py:143
  71.9 0.8 copy-start.5
  81.3 1.0 %copy-start.6 = (bf16[16,128,128]{2,1,0:T(8,128)(2,1)S(1)}, bf16[16,128,128]{2,1,0:T(8,128)(2,1)}, u32[]{:S(2)}) copy-start(bf16[16,128,128]{2,1,0:T(8,128)(2,1)} %copy-done.5) | copy-start | bytes 1572868

commit v3 on v2

--- a/solution.py
+++ b/solution.py
@@ -45,29 +45,40 @@
         s_ref[pl.ds(h * parts, parts)] = fwd.reshape(parts, DH // parts, DH)
 
 
-def back_states_kernel(q_ref, g_ref, c_ref, *t_refs):
-    coef = coef_of(q_ref.shape[0])
-    groups = len(t_refs)
-    for k in reversed(range(groups)):
+def back_states_kernel(q_hbm, g_hbm, c_hbm, *refs):
+    t_hbms, (q_ref, g_ref, c_ref, t_ref, in_sems, out_sems) = refs[:-6], refs[-6:]
+    groups = len(t_hbms)
+    width = HEADS // groups * DH
+    order = list(range(1, groups)) + [0]
+    loads = {}
+    for k in order:
+        cols = pl.ds(pl.multiple_of(group_of(k, groups) * width, DH), width)
+        loads[k] = [
+            pltpu.make_async_copy(g_hbm.at[:, cols], g_ref.at[k], in_sems.at[0, k]),
+            pltpu.make_async_copy(q_hbm.at[:, cols], q_ref.at[k], in_sems.at[1, k]),
+        ]
+        for copy in loads[k]:
+            copy.start()
+    coef = coef_of(q_hbm.shape[0])
+    stores = []
+    for k in order:
+        for copy in loads[k]:
+            copy.wait()
         for h in range(HEADS // groups):
-            cols = columns(k, groups, h)
-            scaled = (g_ref[:, cols].astype(F32) * coef).astype(BF16)
-            c_ref[:, cols] = scaled
-            t_refs[k][pl.ds(h * DH, DH), :] = dot(scaled, q_ref[:, cols], TN).astype(BF16)
-
-
-def scores_kernel(q_ref, k_ref, v_ref, c_ref, sc_ref, sct_ref, ds_ref, dst_ref):
-    length = q_ref.shape[0]
-    row = lax.broadcasted_iota(jnp.int32, (length, length), 0)
-    col = lax.broadcasted_iota(jnp.int32, (length, length), 1)
-    lower, upper = col <= row, col >= row
-    for h in range(HEADS):
-        cols = pl.ds(h * DH, DH)
-        q, k, v, c = q_ref[:, cols], k_ref[:, cols], v_ref[:, cols], c_ref[:, cols]
-        sc_ref[h] = jnp.where(lower, dot(q, k, NT), 0.0).astype(BF16)
-        sct_ref[h] = jnp.where(upper, dot(k, q, NT), 0.0).astype(BF16)
-        ds_ref[h] = jnp.where(lower, dot(c, v, NT), 0.0).astype(BF16)
-        dst_ref[h] = jnp.where(upper, dot(v, c, NT), 0.0).astype(BF16)
+            cols = pl.ds(h * DH, DH)
+            scaled = (g_ref[k, :, cols].astype(F32) * coef).astype(BF16)
+            c_ref[k, :, cols] = scaled
+            t_ref[k, cols, :] = dot(scaled, q_ref[k, :, cols], TN).astype(BF16)
+        cols = pl.ds(pl.multiple_of(group_of(k, groups) * width, DH), width)
+        group = [
+            pltpu.make_async_copy(t_ref.at[k], t_hbms[k], out_sems.at[0, k]),
+            pltpu.make_async_copy(c_ref.at[k], c_hbm.at[:, cols], out_sems.at[1, k]),
+        ]
+        for copy in group:
+            copy.start()
+        stores += group
+    for copy in stores:
+        copy.wait()
 
 
 def fwd_scan_kernel(in_ref, out_ref):
@@ -109,30 +120,71 @@
         b_refs[k][...] = held[plane ^ k]
 
 
-def fwd_final_kernel(q_ref, k_ref, v_ref, c_ref, sc_ref, ds_ref, f_ref, out_ref, dq_ref):
-    coef = coef_of(q_ref.shape[0])
+def masked(a, b, mask):
+    return jnp.where(mask, dot(a, b, NT), 0.0).astype(BF16)
+
+
+def square_of(length):
+    row = lax.broadcasted_iota(jnp.int32, (length, length), 0)
+    return row, lax.broadcasted_iota(jnp.int32, (length, length), 1)
+
+
+def write(outs, held, sems, slot, first, width):
+    cols = pl.ds(pl.multiple_of(first, DH), width)
+    copies = [
+        pltpu.make_async_copy(held.at[i, slot], out.at[:, cols], sems.at[i, slot])
+        for i, out in enumerate(outs)
+    ]
+    for copy in copies:
+        copy.start()
+    return copies
+
+
+def fwd_final_kernel(q_ref, k_ref, v_ref, c_ref, f_ref, out_hbm, dq_hbm, held, sems):
+    length = q_ref.shape[0]
+    coef = coef_of(length)
     parts = DH // f_ref.shape[1]
-    for h in range(HEADS):
-        cols = pl.ds(h * DH, DH)
-        fwd = f_ref[pl.ds(h * parts, parts)].reshape(DH, DH)
-        own = dot(sc_ref[h], v_ref[:, cols]) + dot(q_ref[:, cols], fwd)
-        out_ref[:, cols] = (own * coef).astype(BF16)
-        dq = dot(ds_ref[h], k_ref[:, cols]) + dot(c_ref[:, cols], fwd, NT)
-        dq_ref[:, cols] = dq.astype(BF16)
-
-
-def back_final_kernel(q_ref, k_ref, v_ref, c_ref, sct_ref, dst_ref, *refs):
-    b_refs, dk_ref, dv_ref = refs[:-2], refs[-2], refs[-1]
+    slots = held.shape[1]
+    row, col = square_of(length)
+    copies = []
+    for slot in range(slots):
+        for i in range(HEADS // slots):
+            h = slot * (HEADS // slots) + i
+            cols, to = pl.ds(h * DH, DH), pl.ds(i * DH, DH)
+            q, k, v, c = q_ref[:, cols], k_ref[:, cols], v_ref[:, cols], c_ref[:, cols]
+            fwd = f_ref[pl.ds(h * parts, parts)].reshape(DH, DH)
+            own = dot(masked(q, k, col <= row), v) + dot(q, fwd)
+            held[0, slot, :, to] = (own * coef).astype(BF16)
+            dq = dot(masked(c, v, col <= row), k) + dot(c, fwd, NT)
+            held[1, slot, :, to] = dq.astype(BF16)
+        width = HEADS // slots * DH
+        copies += write((out_hbm, dq_hbm), held, sems, slot, slot * width, width)
+    for copy in copies:
+        copy.wait()
+
+
+def back_final_kernel(q_ref, k_ref, v_ref, c_ref, *refs):
+    b_refs, (dk_hbm, dv_hbm, held, sems) = refs[:-4], refs[-4:]
     groups = len(b_refs)
-    for k in range(groups):
-        for h in range(HEADS // groups):
-            cols = columns(k, groups, h)
-            head = group_of(k, groups) * (HEADS // groups) + h
-            back = b_refs[k][pl.ds(h * DH, DH), :]
-            dk = dot(dst_ref[head], q_ref[:, cols]) + dot(v_ref[:, cols], back)
-            dk_ref[:, cols] = dk.astype(BF16)
-            dv = dot(sct_ref[head], c_ref[:, cols]) + dot(k_ref[:, cols], back, NT)
-            dv_ref[:, cols] = dv.astype(BF16)
+    slots = held.shape[1]
+    row, col = square_of(q_ref.shape[0])
+    copies = []
+    for slot in range(slots):
+        for i in range(HEADS // slots):
+            g = slot * groups // slots
+            h = slot * (HEADS // slots) + i - g * (HEADS // groups)
+            cols, to = columns(g, groups, h), pl.ds(i * DH, DH)
+            q, k, v, c = q_ref[:, cols], k_ref[:, cols], v_ref[:, cols], c_ref[:, cols]
+            back = b_refs[g][pl.ds(h * DH, DH), :]
+            dk = dot(masked(v, c, col >= row), q) + dot(v, back)
+            held[0, slot, :, to] = dk.astype(BF16)
+            dv = dot(masked(k, q, col >= row), c) + dot(k, back, NT)
+            held[1, slot, :, to] = dv.astype(BF16)
+        width = HEADS // slots * DH
+        first = group_of(slot, groups) * width if groups > 1 else slot * width
+        copies += write((dk_hbm, dv_hbm), held, sems, slot, first, width)
+    for copy in copies:
+        copy.wait()
 
 
 def exchange(x):
@@ -143,14 +195,20 @@
     return lax.ppermute(x, axis, [(i, i ^ k) for i in range(lax.axis_size(axis))])
 
 
-def call(kernel, out, flops, *args, scratch=()):
+def call(kernel, out, flops, *args, scratch=(), ins=None, outs=None, limit=VMEM):
     moved = sum(a.size * a.dtype.itemsize for a in args)
+    vmem = pl.BlockSpec(memory_space=pltpu.VMEM)
+    ins = [vmem] * len(args) if ins is None else ins
+    if outs is None:
+        outs = [vmem] * len(out) if isinstance(out, list) else vmem
     return pl.pallas_call(
         kernel,
         out_shape=out,
+        in_specs=ins,
+        out_specs=outs,
         scratch_shapes=list(scratch),
         cost_estimate=pl.CostEstimate(flops=flops, bytes_accessed=2 * moved, transcendentals=0),
-        compiler_params=pltpu.CompilerParams(vmem_limit_bytes=VMEM),
+        compiler_params=pltpu.CompilerParams(vmem_limit_bytes=limit),
     )(*args)
 
 
@@ -162,14 +220,25 @@
     block = share if direct else DH
     groups = planes if direct else 1
     rows_of = jax.ShapeDtypeStruct((length, feat), BF16)
-    square_of = jax.ShapeDtypeStruct((HEADS, length, length), BF16)
     state_of = jax.ShapeDtypeStruct((feat // block, block, DH), BF16)
     piece_of = jax.ShapeDtypeStruct((feat // groups, DH), BF16)
     matmul = 2 * HEADS * length * DH * DH
+    hbm = pl.BlockSpec(memory_space=pltpu.HBM)
+    vmem = pl.BlockSpec(memory_space=pltpu.VMEM)
+    staged = [pltpu.VMEM((groups, length, feat // groups), BF16)] * 3
+    staged += [
+        pltpu.VMEM((groups, feat // groups, DH), BF16),
+        pltpu.SemaphoreType.DMA((2, groups)),
+        pltpu.SemaphoreType.DMA((2, groups)),
+    ]
+    held = [
+        pltpu.VMEM((2, 4, length, feat // 4), BF16),
+        pltpu.SemaphoreType.DMA((2, 4)),
+    ]
 
     scaled, *back_states = call(
         back_states_kernel, [rows_of] + [piece_of] * groups, matmul,
-        queries, out_grad,
+        queries, out_grad, scratch=staged, ins=[hbm] * 2, outs=[hbm] * (groups + 1), limit=None,
     )
     if direct:
         own = [back_states[0]] + [swap(back_states[k], "head", k) for k in range(1, groups)]
@@ -198,9 +267,14 @@
         back = [exchange(after.astype(BF16)).reshape(feat, DH)]
 
     rows = (queries, keys, values, scaled)
-    sc, sct, ds, dst = call(scores_kernel, [square_of] * 4, 4 * matmul, *rows)
-    dk, dv = call(back_final_kernel, [rows_of] * 2, 4 * matmul, *rows, sct, dst, *back)
-    out, dq = call(fwd_final_kernel, [rows_of] * 2, 4 * matmul, *rows, sc, ds, fwd)
+    out, dq = call(
+        fwd_final_kernel, [rows_of] * 2, 6 * matmul, *rows, fwd,
+        scratch=held, outs=[hbm] * 2,
+    )
+    dk, dv = call(
+        back_final_kernel, [rows_of] * 2, 6 * matmul, *rows, *back,
+        scratch=held, outs=[hbm] * 2,
+    )
     return out, dq, dk, dv
 
 

time: 84.6 us -> 88.4 us (1.045)
  Pallas kernels: 7.54 us -> 11.3 us
  waiting for transfers between devices: 33.1 us -> 34.1 us
  local copies, waits for them, and re-layouts: 3.93 us -> 3 us
    pallas_call x9 -> x8, Pallas kernels: 7.54 us -> 11.3 us  [call(): pl.pallas_call(kernel, out_shape=out, in_specs=ins, out_specs=outs, scrat...]
    ppermute x10, waiting for transfers between devices: 33.1 us -> 34.1 us  [swap(): lax.ppermute(x, axis, [(i, i ^ k) for i in range(lax.axis_size(axis))])]
    unnamed x16 -> x14, local copies, waits for them, and re-layouts: 3.93 us -> 3 us
  transfers between devices with their start and end apart: 11 -> 11, of which waited for: 6 -> 7; matrix products, arithmetic and copies ran while one was open for 0% -> 0% of each run, Pallas kernels for 5% -> 8%
where the time goes in v3:
time: 88.4 us; the launch traced here: 88.1 us
  waiting for transfers between devices  34.1 us (39%)
  blocking collectives  21.4 us (24%)
  starting transfers between devices  17.6 us (20%)
  Pallas kernels  11.3 us (13%)
  local copies, waits for them, and re-layouts  3 us (3%)
    ppermute x10, waiting for transfers between devices, swap(): lax.ppermute(x, axis, [(i, i ^ k) for i in range(lax.axis_size(axis))])  34.1 us
    all_to_all x1, blocking collectives, exchange(): return lax.all_to_all(x, AXES, split_axis=0, concat_axis=0, tiled=True)  21.4 us
    ppermute x10, starting transfers between devices, swap(): lax.ppermute(x, axis, [(i, i ^ k) for i in range(lax.axis_size(axis))])  13.4 us
    pallas_call x8, Pallas kernels, call(): pl.pallas_call(kernel, out_shape=out, in_specs=ins, out_specs=outs, scrat...  11.3 us
    all_to_all x1, starting transfers between devices, exchange(): return lax.all_to_all(x, AXES, split_axis=0, concat_axis=0, tiled=True)  4.17 us
    unnamed x14, local copies, waits for them, and re-layouts  3 us
  transfers between devices with their start and end apart: 11, of which 7 were waited for; matrix products, arithmetic and copies ran while one was open for 0% of the time, Pallas kernels for 8%

profile of v3, /device:TPU:0, one launch (start us, length us, event | category | flops | bytes accessed | tf_op | source)
XLA Modules:
  0.0 88.1 jit_solution(11703387816031787538)
XLA Ops:
  0.6 0.0 copy-start
  0.6 1.0 %copy-done = bf16[128,2048]{1,0:T(8,128)(2,1)S(1)} copy-done((bf16[128,2048]{1,0:T(8,128)(2,1)S(1)}, bf16[128,2048]{1,0:T(8,128)(2,1)}, u32[]{:S(2)}) %copy-start) | copy-done | bytes 524312
  1.7 1.0 %copy-done.2 = bf16[128,2048]{1,0:T(8,128)(2,1)S(1)} copy-done((bf16[128,2048]{1,0:T(8,128)(2,1)S(1)}, bf16[128,2048]{1,0:T(8,128)(2,1)}, u32[]{:S(2)}) %copy-start.2) | copy-done | bytes 524312
  2.7 0.3 shard_map.76
  3.1 21.4 %all_to_all.10.in_ref = bf16[32,64,128]{2,1,0:T(8,128)(2,1)S(1)} all-to-all(bf16[32,64,128]{2,1,0:T(8,128)(2,1)S(1)} %shard_map.76), channel_id=1, replica_groups=mesh['head'=4,'span'=8] {'span','head'}, dimensions={0} | all-to-all | bytes 1048576 | tf_op jit(solution)/shard_map/all_to_all | solution.py:191
  24.4 0.9 %shard_map.77 = bf16[32,64,128]{2,1,0:T(8,128)(2,1)} custom-call(bf16[32,64,128]{2,1,0:T(8,128)(2,1)S(1)} %all_to_all.10.in_ref), custom_call_target="tpu_custom_call" | custom-call | bytes 1048576 | tf_op jit(solution)/shard_map/pallas_call | solution.py:204
  25.3 4.2 %all-to-all-start.1 = ((bf16[32,64,128]{2,1,0:T(8,128)(2,1)}), bf16[32,64,128]{2,1,0:T(8,128)(2,1)S(1)}, u32[]{:S(2)}, u32[]{:S(2)}) async-start(bf16[32,64,128]{2,1,0:T(8,128)(2,1)} %shard_map.77), calls=%async_computation.1 | async-start | bytes 1048576 | tf_op jit(solution)/shard_map/all_to_all | solution.py:191
  29.5 2.7 %shard_map.75 = (bf16[128,2048]{1,0:T(8,128)(2,1)}, bf16[512,128]{1,0:T(8,128)(2,1)}, bf16[512,128]{1,0:T(8,128)(2,1)}, bf16[512,128]{1,0:T(8,128)(2,1)}, bf16[512,128]{1,0:T(8,128)(2,1)}) custom-call(bf16[128,2048]{1,0:T(8,128)(2,1)} %q_ref.3, bf16[128,2048]{1,0:T(8,128)(2,1)} %g_hbm.1), custom_call_target="tpu_custom_call" | custom-call | flops 67108864 | bytes 2097152 | tf_op jit(solution)/shard_map/pallas_call | solution.py:204
  32.2 1.8 %collective-permute-start = (bf16[512,128]{1,0:T(8,128)(2,1)}, bf16[512,128]{1,0:T(8,128)(2,1)S(1)}, u32[]{:S(2)}, u32[]{:S(2)}) collective-permute-start(bf16[512,128]{1,0:T(8,128)(2,1)} %get-tuple-element.21), channel_id=1, source_target_pairs={{0,8},{8,0},{16,24},{24,16},{1,9},{9,1},{17,25},{25,17},{2,10},{10... | collective-permute-start | bytes 393224 | tf_op jit(solution)/shard_map/ppermute | solution.py:195
  34.1 2.4 %collective-permute-start.1 = (bf16[512,128]{1,0:T(8,128)(2,1)}, bf16[512,128]{1,0:T(8,128)(2,1)S(1)}, u32[]{:S(2)}, u32[]{:S(2)}) collective-permute-start(bf16[512,128]{1,0:T(8,128)(2,1)} %get-tuple-element.22), channel_id=1, source_target_pairs={{0,16},{8,24},{16,0},{24,8},{1,17},{9,25},{17,1},{25,9},{2,18},{10... | collective-permute-start | bytes 393224 | tf_op jit(solution)/shard_map/ppermute | solution.py:195
  36.5 0.2 collective-permute-start.2
  36.7 6.2 %collective-permute-done.refs_1_.refs_2_ = bf16[512,128]{1,0:T(8,128)(2,1)S(1)} collective-permute-done((bf16[512,128]{1,0:T(8,128)(2,1)}, bf16[512,128]{1,0:T(8,128)(2,1)S(1)}, u32[]{:S(2)}, u32[]{:S(2)}) %collective-permute-start) | collective-permute-done | bytes 131104 | tf_op jit(solution)/shard_map/ppermute | solution.py:195
  42.9 10.6 %collective-permute-done.1.refs_2_.refs_3_ = bf16[512,128]{1,0:T(8,128)(2,1)S(1)} collective-permute-done((bf16[512,128]{1,0:T(8,128)(2,1)}, bf16[512,128]{1,0:T(8,128)(2,1)S(1)}, u32[]{:S(2)}, u32[]{:S(2)}) %collective-permute-start.1) | collective-permute-done | bytes 131104 | tf_op jit(solution)/shard_map/ppermute | solution.py:195
  53.5 0.9 %copy-done.6 = bf16[512,128]{1,0:T(8,128)(2,1)S(1)} copy-done((bf16[512,128]{1,0:T(8,128)(2,1)S(1)}, bf16[512,128]{1,0:T(8,128)(2,1)}, u32[]{:S(2)}) %copy-start.6) | copy-done | bytes 131096
  54.4 0.1 shard_map.79.a_ref
  54.5 0.1 collective-permute-start.3
  54.6 1.3 %collective-permute-done.3.b_ref.refs_0_ = bf16[512,128]{1,0:T(8,128)(2,1)S(1)} collective-permute-done((bf16[512,128]{1,0:T(8,128)(2,1)S(1)}, bf16[512,128]{1,0:T(8,128)(2,1)S(1)}, u32[]{:S(2)}, u32[]{:S(2)}) %collective-permute-start.3) | collective-permute-done | bytes 131104 | tf_op jit(solution)/shard_map/ppermute | solution.py:195
  55.9 0.0 copy-start.1
  56.0 2.5 %collective-permute-start.6 = (bf16[512,128]{1,0:T(8,128)(2,1)S(1)}, bf16[512,128]{1,0:T(8,128)(2,1)S(1)}, u32[]{:S(2)}, u32[]{:S(2)}) collective-permute-start(bf16[512,128]{1,0:T(8,128)(2,1)S(1)} %shard_map.80), channel_id=1, source_target_pairs={{0,6},{1,7},{2,4},{3,5},{4,2},{5,3},{6,0},{7,1},{8,14},{9,15},{10,... | collective-permute-start | bytes 393224 | tf_op jit(solution)/shard_map/ppermute | solution.py:195
  58.4 0.5 collective-permute-start.5
  58.9 0.6 collective-permute-start.4
  59.5 3.4 %collective-permute-done.6.refs_7_ = bf16[512,128]{1,0:T(8,128)(2,1)S(1)} collective-permute-done((bf16[512,128]{1,0:T(8,128)(2,1)S(1)}, bf16[512,128]{1,0:T(8,128)(2,1)S(1)}, u32[]{:S(2)}, u32[]{:S(2)}) %collective-permute-start.6) | collective-permute-done | bytes 131104 | tf_op jit(solution)/shard_map/ppermute | solution.py:195
  62.9 2.4 %collective-permute-done.5.refs_6_ = bf16[512,128]{1,0:T(8,128)(2,1)S(1)} collective-permute-done((bf16[512,128]{1,0:T(8,128)(2,1)S(1)}, bf16[512,128]{1,0:T(8,128)(2,1)S(1)}, u32[]{:S(2)}, u32[]{:S(2)}) %collective-permute-start.5) | collective-permute-done | bytes 131104 | tf_op jit(solution)/shard_map/ppermute | solution.py:195
  65.3 0.0 collective-permute-done.4.refs_5_
  65.3 0.3 shard_map.81
  65.7 2.9 %collective-permute-start.7 = (bf16[512,128]{1,0:T(8,128)(2,1)S(1)}, bf16[512,128]{1,0:T(8,128)(2,1)S(1)}, u32[]{:S(2)}, u32[]{:S(2)}) collective-permute-start(bf16[512,128]{1,0:T(8,128)(2,1)S(1)} %get-tuple-element.25), channel_id=1, source_target_pairs={{0,8},{8,0},{16,24},{24,16},{1,9},{9,1},{17,25},{25,17},{2,10},{10... | collective-permute-start | bytes 393224 | tf_op jit(solution)/shard_map/ppermute | solution.py:195
  68.5 0.1 collective-permute-start.8
  68.6 2.4 %collective-permute-start.9 = (bf16[512,128]{1,0:T(8,128)(2,1)S(1)}, bf16[512,128]{1,0:T(8,128)(2,1)S(1)}, u32[]{:S(2)}, u32[]{:S(2)}) collective-permute-start(bf16[512,128]{1,0:T(8,128)(2,1)S(1)} %get-tuple-element.27), channel_id=1, source_target_pairs={{0,24},{8,16},{16,8},{24,0},{1,25},{9,17},{17,9},{25,1},{2,26},{10... | collective-permute-start | bytes 393224 | tf_op jit(solution)/shard_map/ppermute | solution.py:195
  71.0 2.3 %collective-permute-done.7.refs_1_ = bf16[512,128]{1,0:T(8,128)(2,1)S(1)} collective-permute-done((bf16[512,128]{1,0:T(8,128)(2,1)S(1)}, bf16[512,128]{1,0:T(8,128)(2,1)S(1)}, u32[]{:S(2)}, u32[]{:S(2)}) %collective-permute-start.7) | collective-permute-done | bytes 131104 | tf_op jit(solution)/shard_map/ppermute | solution.py:195
  73.2 7.8 %collective-permute-done.8.refs_2_ = bf16[512,128]{1,0:T(8,128)(2,1)S(1)} collective-permute-done((bf16[512,128]{1,0:T(8,128)(2,1)S(1)}, bf16[512,128]{1,0:T(8,128)(2,1)S(1)}, u32[]{:S(2)}, u32[]{:S(2)}) %collective-permute-start.8) | collective-permute-done | bytes 131104 | tf_op jit(solution)/shard_map/ppermute | solution.py:195
  81.1 3.5 %shard_map.82 = (bf16[128,2048]{1,0:T(8,128)(2,1)}, bf16[128,2048]{1,0:T(8,128)(2,1)}) custom-call(bf16[128,2048]{1,0:T(8,128)(2,1)S(1)} %copy-done.4, bf16[128,2048]{1,0:T(8,128)(2,1)S(1)} %copy-done.1, bf16[128,2048]{1,0:T(8,128)(2,1)S(1)} %copy-done.3, bf16[128,2048]{1,0:T(8,128)(2,1)S(1)} %copy-done.5, bf16[512,128]{1,0:T(8,128)(2,1)S(1)} %get-tuple-element.24.refs_0_, ...), custom_call_target="tpu_custom_call" | custom-call | flops 402653184 | bytes 5242880 | tf_op jit(solution)/shard_map/pallas_call | solution.py:204
  84.6 3.5 %shard_map.78 = (bf16[128,2048]{1,0:T(8,128)(2,1)}, bf16[128,2048]{1,0:T(8,128)(2,1)}) custom-call(bf16[128,2048]{1,0:T(8,128)(2,1)S(1)} %copy-done.4, bf16[128,2048]{1,0:T(8,128)(2,1)S(1)} %copy-done.1, bf16[128,2048]{1,0:T(8,128)(2,1)S(1)} %copy-done.3, bf16[128,2048]{1,0:T(8,128)(2,1)S(1)} %copy-done.5, bf16[32,64,128]{2,1,0:T(8,128)(2,1)S(1)} %all-to-all-done.1.f_ref), custom_call_target="tpu_custom_call" | custom-call | flops 402653184 | bytes 5242880 | tf_op jit(solution)/shard_map/pallas_call | solution.py:204
  (13 shorter events, 0.1 us)
Async XLA Ops:
  0.6 1.0 %copy-start = (bf16[128,2048]{1,0:T(8,128)(2,1)S(1)}, bf16[128,2048]{1,0:T(8,128)(2,1)}, u32[]{:S(2)}) copy-start(bf16[128,2048]{1,0:T(8,128)(2,1)} %k_ref.5) | copy-start | bytes 1572868
  1.7 1.0 %copy-start.2 = (bf16[128,2048]{1,0:T(8,128)(2,1)S(1)}, bf16[128,2048]{1,0:T(8,128)(2,1)}, u32[]{:S(2)}) copy-start(bf16[128,2048]{1,0:T(8,128)(2,1)} %v_ref.5) | copy-start | bytes 1572868
  25.3 59.3 %all-to-all-start.1 = ((bf16[32,64,128]{2,1,0:T(8,128)(2,1)}), bf16[32,64,128]{2,1,0:T(8,128)(2,1)S(1)}, u32[]{:S(2)}, u32[]{:S(2)}) async-start(bf16[32,64,128]{2,1,0:T(8,128)(2,1)} %shard_map.77), calls=%async_computation.1 | async-start | bytes 1048576 | tf_op jit(solution)/shard_map/all_to_all | solution.py:191
  32.2 10.6 %collective-permute-start = (bf16[512,128]{1,0:T(8,128)(2,1)}, bf16[512,128]{1,0:T(8,128)(2,1)S(1)}, u32[]{:S(2)}, u32[]{:S(2)}) collective-permute-start(bf16[512,128]{1,0:T(8,128)(2,1)} %get-tuple-element.21), channel_id=1, source_target_pairs={{0,8},{8,0},{16,24},{24,16},{1,9},{9,1},{17,25},{25,17},{2,10},{10... | collective-permute-start | bytes 393224 | tf_op jit(solution)/shard_map/ppermute | solution.py:195
  34.1 19.4 %collective-permute-start.1 = (bf16[512,128]{1,0:T(8,128)(2,1)}, bf16[512,128]{1,0:T(8,128)(2,1)S(1)}, u32[]{:S(2)}, u32[]{:S(2)}) collective-permute-start(bf16[512,128]{1,0:T(8,128)(2,1)} %get-tuple-element.22), channel_id=1, source_target_pairs={{0,16},{8,24},{16,0},{24,8},{1,17},{9,25},{17,1},{25,9},{2,18},{10... | collective-permute-start | bytes 393224 | tf_op jit(solution)/shard_map/ppermute | solution.py:195
  36.5 17.0 %collective-permute-start.2 = (bf16[512,128]{1,0:T(8,128)(2,1)}, bf16[512,128]{1,0:T(8,128)(2,1)S(1)}, u32[]{:S(2)}, u32[]{:S(2)}) collective-permute-start(bf16[512,128]{1,0:T(8,128)(2,1)} %get-tuple-element.23), channel_id=1, source_target_pairs={{0,24},{8,16},{16,8},{24,0},{1,25},{9,17},{17,9},{25,1},{2,26},{10... | collective-permute-start | bytes 393224 | tf_op jit(solution)/shard_map/ppermute | solution.py:195
  53.5 0.9 %copy-start.6 = (bf16[512,128]{1,0:T(8,128)(2,1)S(1)}, bf16[512,128]{1,0:T(8,128)(2,1)}, u32[]{:S(2)}) copy-start(bf16[512,128]{1,0:T(8,128)(2,1)} %get-tuple-element.20.refs_0_.refs_1_) | copy-start | bytes 393220
  54.4 26.7 %copy-start.4 = (bf16[128,2048]{1,0:T(8,128)(2,1)S(1)}, bf16[128,2048]{1,0:T(8,128)(2,1)}, u32[]{:S(2)}) copy-start(bf16[128,2048]{1,0:T(8,128)(2,1)} %q_ref.3) | copy-start | bytes 1572868
  54.4 26.7 %copy-start.5 = (bf16[128,2048]{1,0:T(8,128)(2,1)S(1)}, bf16[128,2048]{1,0:T(8,128)(2,1)}, u32[]{:S(2)}) copy-start(bf16[128,2048]{1,0:T(8,128)(2,1)} %get-tuple-element.17.c_ref) | copy-start | bytes 1572868
  54.5 1.4 %collective-permute-start.3 = (bf16[512,128]{1,0:T(8,128)(2,1)S(1)}, bf16[512,128]{1,0:T(8,128)(2,1)S(1)}, u32[]{:S(2)}, u32[]{:S(2)}) collective-permute-start(bf16[512,128]{1,0:T(8,128)(2,1)S(1)} %shard_map.79.a_ref), channel_id=1, source_target_pairs={{0,1},{1,0},{2,3},{3,2},{4,5},{5,4},{6,7},{7,6},{8,9},{9,8},{10,11... | collective-permute-start | bytes 393224 | tf_op jit(solution)/shard_map/ppermute | solution.py:195
  55.9 25.2 %copy-start.1 = (bf16[128,2048]{1,0:T(8,128)(2,1)S(1)}, bf16[128,2048]{1,0:T(8,128)(2,1)}, u32[]{:S(2)}) copy-start(bf16[128,2048]{1,0:T(8,128)(2,1)} %k_ref.5) | copy-start | bytes 1572868
  55.9 25.2 %copy-start.3 = (bf16[128,2048]{1,0:T(8,128)(2,1)S(1)}, bf16[128,2048]{1,0:T(8,128)(2,1)}, u32[]{:S(2)}) copy-start(bf16[128,2048]{1,0:T(8,128)(2,1)} %v_ref.5) | copy-start | bytes 1572868
  56.0 6.9 %collective-permute-start.6 = (bf16[512,128]{1,0:T(8,128)(2,1)S(1)}, bf16[512,128]{1,0:T(8,128)(2,1)S(1)}, u32[]{:S(2)}, u32[]{:S(2)}) collective-permute-start(bf16[512,128]{1,0:T(8,128)(2,1)S(1)} %shard_map.80), channel_id=1, source_target_pairs={{0,6},{1,7},{2,4},{3,5},{4,2},{5,3},{6,0},{7,1},{8,14},{9,15},{10,... | collective-permute-start | bytes 393224 | tf_op jit(solution)/shard_map/ppermute | solution.py:195
  58.4 6.9 %collective-permute-start.5 = (bf16[512,128]{1,0:T(8,128)(2,1)S(1)}, bf16[512,128]{1,0:T(8,128)(2,1)S(1)}, u32[]{:S(2)}, u32[]{:S(2)}) collective-permute-start(bf16[512,128]{1,0:T(8,128)(2,1)S(1)} %shard_map.80), channel_id=1, source_target_pairs={{0,4},{1,5},{2,6},{3,7},{4,0},{5,1},{6,2},{7,3},{8,12},{9,13},{10,... | collective-permute-start | bytes 393224 | tf_op jit(solution)/shard_map/ppermute | solution.py:195
  58.9 6.4 %collective-permute-start.4 = (bf16[512,128]{1,0:T(8,128)(2,1)S(1)}, bf16[512,128]{1,0:T(8,128)(2,1)S(1)}, u32[]{:S(2)}, u32[]{:S(2)}) collective-permute-start(bf16[512,128]{1,0:T(8,128)(2,1)S(1)} %shard_map.80), channel_id=1, source_target_pairs={{0,2},{1,3},{2,0},{3,1},{4,6},{5,7},{6,4},{7,5},{8,10},{9,11},{10,... | collective-permute-start | bytes 393224 | tf_op jit(solution)/shard_map/ppermute | solution.py:195
  65.7 7.6 %collective-permute-start.7 = (bf16[512,128]{1,0:T(8,128)(2,1)S(1)}, bf16[512,128]{1,0:T(8,128)(2,1)S(1)}, u32[]{:S(2)}, u32[]{:S(2)}) collective-permute-start(bf16[512,128]{1,0:T(8,128)(2,1)S(1)} %get-tuple-element.25), channel_id=1, source_target_pairs={{0,8},{8,0},{16,24},{24,16},{1,9},{9,1},{17,25},{25,17},{2,10},{10... | collective-permute-start | bytes 393224 | tf_op jit(solution)/shard_map/ppermute | solution.py:195
  68.5 12.6 %collective-permute-start.8 = (bf16[512,128]{1,0:T(8,128)(2,1)S(1)}, bf16[512,128]{1,0:T(8,128)(2,1)S(1)}, u32[]{:S(2)}, u32[]{:S(2)}) collective-permute-start(bf16[512,128]{1,0:T(8,128)(2,1)S(1)} %get-tuple-element.26), channel_id=1, source_target_pairs={{0,16},{8,24},{16,0},{24,8},{1,17},{9,25},{17,1},{25,9},{2,18},{10... | collective-permute-start | bytes 393224 | tf_op jit(solution)/shard_map/ppermute | solution.py:195
  68.6 12.5 %collective-permute-start.9 = (bf16[512,128]{1,0:T(8,128)(2,1)S(1)}, bf16[512,128]{1,0:T(8,128)(2,1)S(1)}, u32[]{:S(2)}, u32[]{:S(2)}) collective-permute-start(bf16[512,128]{1,0:T(8,128)(2,1)S(1)} %get-tuple-element.27), channel_id=1, source_target_pairs={{0,24},{8,16},{16,8},{24,0},{1,25},{9,17},{17,9},{25,1},{2,26},{10... | collective-permute-start | bytes 393224 | tf_op jit(solution)/shard_map/ppermute | solution.py:195

commit v4 on v3

--- a/solution.py
+++ b/solution.py
@@ -38,11 +38,11 @@
 
 
 def fwd_states_kernel(k_ref, v_ref, s_ref):
-    parts = DH // s_ref.shape[1]
+    width = s_ref.shape[1] // DH
     for h in range(HEADS):
         cols = pl.ds(h * DH, DH)
         fwd = dot(k_ref[:, cols], v_ref[:, cols], TN).astype(BF16)
-        s_ref[pl.ds(h * parts, parts)] = fwd.reshape(parts, DH // parts, DH)
+        s_ref[h // width, pl.ds(h % width * DH, DH), :] = fwd
 
 
 def back_states_kernel(q_hbm, g_hbm, c_hbm, *refs):
@@ -81,12 +81,24 @@
         copy.wait()
 
 
-def fwd_scan_kernel(in_ref, out_ref):
-    def step(i, total):
-        out_ref[i] = total.astype(BF16)
-        return total + in_ref[i].astype(F32)
-
-    lax.fori_loop(0, in_ref.shape[0], step, jnp.zeros(in_ref.shape[1:], F32), unroll=4)
+def fwd_total_kernel(in_ref, out_ref):
+    total = in_ref[0].astype(F32)
+    for z in range(1, in_ref.shape[0]):
+        total += in_ref[z].astype(F32)
+    out_ref[...] = total.astype(BF16)
+
+
+def fwd_combine_kernel(pair_ref, in_ref, *refs):
+    chip_refs, out_ref = refs[:-1], refs[-1]
+    span = lax.axis_index("span")
+    total = jnp.where(span % 2 == 1, pair_ref[...].astype(F32), 0.0)
+    chip = span // 2
+    for k in range(len(chip_refs)):
+        before = (chip ^ (k + 1)) < chip
+        total += jnp.where(before, chip_refs[k][...].astype(F32), 0.0)
+    for z in range(in_ref.shape[0]):
+        out_ref[z] = total.astype(BF16)
+        total += in_ref[z].astype(F32)
 
 
 def total_kernel(*refs):
@@ -143,7 +155,7 @@
 def fwd_final_kernel(q_ref, k_ref, v_ref, c_ref, f_ref, out_hbm, dq_hbm, held, sems):
     length = q_ref.shape[0]
     coef = coef_of(length)
-    parts = DH // f_ref.shape[1]
+    width_in = f_ref.shape[1] // DH
     slots = held.shape[1]
     row, col = square_of(length)
     copies = []
@@ -152,7 +164,7 @@
             h = slot * (HEADS // slots) + i
             cols, to = pl.ds(h * DH, DH), pl.ds(i * DH, DH)
             q, k, v, c = q_ref[:, cols], k_ref[:, cols], v_ref[:, cols], c_ref[:, cols]
-            fwd = f_ref[pl.ds(h * parts, parts)].reshape(DH, DH)
+            fwd = f_ref[h // width_in, pl.ds(h % width_in * DH, DH), :]
             own = dot(masked(q, k, col <= row), v) + dot(q, fwd)
             held[0, slot, :, to] = (own * coef).astype(BF16)
             dq = dot(masked(c, v, col <= row), k) + dot(c, fwd, NT)
@@ -187,16 +199,25 @@
         copy.wait()
 
 
-def exchange(x):
-    return lax.all_to_all(x, AXES, split_axis=0, concat_axis=0, tiled=True)
+def exchange(x, axes="head"):
+    return lax.all_to_all(x, axes, split_axis=0, concat_axis=0, tiled=True)
 
 
 def swap(x, axis, k):
     return lax.ppermute(x, axis, [(i, i ^ k) for i in range(lax.axis_size(axis))])
 
 
+def over_span(total):
+    other = swap(total, "span", 1)
+    both = call(pair_kernel, total, 0, total, other)
+    chips = range(1, lax.axis_size("span") // 2)
+    return other, [swap(both, "span", 2 * k) for k in chips]
+
+
 def call(kernel, out, flops, *args, scratch=(), ins=None, outs=None, limit=VMEM):
     moved = sum(a.size * a.dtype.itemsize for a in args)
+    if not isinstance(out, list):
+        out = jax.ShapeDtypeStruct(out.shape, out.dtype)
     vmem = pl.BlockSpec(memory_space=pltpu.VMEM)
     ins = [vmem] * len(args) if ins is None else ins
     if outs is None:
@@ -217,10 +238,9 @@
     length, feat = queries.shape
     share = feat // devices
     direct = direct_on(devices, planes, span)
-    block = share if direct else DH
     groups = planes if direct else 1
     rows_of = jax.ShapeDtypeStruct((length, feat), BF16)
-    state_of = jax.ShapeDtypeStruct((feat // block, block, DH), BF16)
+    state_of = jax.ShapeDtypeStruct((groups, feat // groups, DH), BF16)
     piece_of = jax.ShapeDtypeStruct((feat // groups, DH), BF16)
     matmul = 2 * HEADS * length * DH * DH
     hbm = pl.BlockSpec(memory_space=pltpu.HBM)
@@ -245,26 +265,24 @@
     states = call(fwd_states_kernel, state_of, matmul, keys, values)
     if direct:
         gathered = exchange(states)
-        fwd = exchange(
-            call(fwd_scan_kernel, jax.ShapeDtypeStruct(gathered.shape, BF16), 0, gathered),
-        )
         total = call(total_kernel, piece_of, 0, *own)
-        other = swap(total, "span", 1)
-        chip = call(pair_kernel, piece_of, 0, total, other)
-        chips = [swap(chip, "span", 2 * k) for k in range(1, span // 2)]
+        other, chips = over_span(total)
         carried = call(
             lambda *refs: back_combine_kernel(groups, *refs),
             [piece_of] * groups, 0, other, *own, *chips,
             scratch=[pltpu.VMEM((groups, feat // groups, DH), BF16)],
         )
         back = [carried[0]] + [swap(carried[k], "head", k) for k in range(1, groups)]
+        total = call(fwd_total_kernel, piece_of, 0, gathered)
+        other, chips = over_span(total)
+        fwd = exchange(call(fwd_combine_kernel, state_of, 0, other, gathered, *chips))
     else:
-        wide = exchange(states.reshape(devices, share, DH)).astype(F32)
+        wide = exchange(states.reshape(devices, share, DH), AXES).astype(F32)
         before = jnp.cumsum(wide, axis=0) - wide
-        fwd = exchange(before.astype(BF16)).reshape(states.shape)
-        wide = jnp.flip(exchange(back_states[0].reshape(devices, share, DH)), 0).astype(F32)
+        fwd = exchange(before.astype(BF16), AXES).reshape(states.shape)
+        wide = jnp.flip(exchange(back_states[0].reshape(devices, share, DH), AXES), 0).astype(F32)
         after = jnp.flip(jnp.cumsum(wide, axis=0) - wide, 0)
-        back = [exchange(after.astype(BF16)).reshape(feat, DH)]
+        back = [exchange(after.astype(BF16), AXES).reshape(feat, DH)]
 
     rows = (queries, keys, values, scaled)
     out, dq = call(

time: 88.4 us -> 97.9 us (1.11)
  waiting for transfers between devices: 34.1 us -> 41.5 us
  starting transfers between devices: 17.6 us -> 20.1 us
    ppermute x10 -> x14, waiting for transfers between devices: 34.1 us -> 41.5 us  [swap(): lax.ppermute(x, axis, [(i, i ^ k) for i in range(lax.axis_size(axis))])]
    ppermute x10 -> x14, starting transfers between devices: 13.4 us -> 16.7 us  [swap(): lax.ppermute(x, axis, [(i, i ^ k) for i in range(lax.axis_size(axis))])]
    pallas_call x8 -> x10, Pallas kernels: 11.3 us -> 11.5 us  [call(): pl.pallas_call(kernel, out_shape=out, in_specs=ins, out_specs=outs, scrat...]
  transfers between devices with their start and end apart: 11 -> 15, of which waited for: 7 -> 11; matrix products, arithmetic and copies ran while one was open for 0% -> 0% of each run, Pallas kernels for 8% -> 7%
where the time goes in v4:
time: 97.9 us; the launch traced here: 97.5 us
  waiting for transfers between devices  41.5 us (42%)
  blocking collectives  20.6 us (21%)
  starting transfers between devices  20.1 us (21%)
  Pallas kernels  11.5 us (12%)
  local copies, waits for them, and re-layouts  3 us (3%)
    ppermute x14, waiting for transfers between devices, swap(): lax.ppermute(x, axis, [(i, i ^ k) for i in range(lax.axis_size(axis))])  41.5 us
    all_to_all x1, blocking collectives, exchange(): return lax.all_to_all(x, axes, split_axis=0, concat_axis=0, tiled=True)  20.6 us
    ppermute x14, starting transfers between devices, swap(): lax.ppermute(x, axis, [(i, i ^ k) for i in range(lax.axis_size(axis))])  16.7 us
    pallas_call x10, Pallas kernels, call(): pl.pallas_call(kernel, out_shape=out, in_specs=ins, out_specs=outs, scrat...  11.5 us
    all_to_all x1, starting transfers between devices, exchange(): return lax.all_to_all(x, axes, split_axis=0, concat_axis=0, tiled=True)  3.47 us
    unnamed x14, local copies, waits for them, and re-layouts  3 us
  transfers between devices with their start and end apart: 15, of which 11 were waited for; matrix products, arithmetic and copies ran while one was open for 0% of the time, Pallas kernels for 7%

profile of v4, /device:TPU:0, one launch (start us, length us, event | category | flops | bytes accessed | tf_op | source)
XLA Modules:
  0.0 97.5 jit_solution(3099351750242444243)
XLA Ops:
  0.6 1.0 %copy-done = bf16[128,2048]{1,0:T(8,128)(2,1)S(1)} copy-done((bf16[128,2048]{1,0:T(8,128)(2,1)S(1)}, bf16[128,2048]{1,0:T(8,128)(2,1)}, u32[]{:S(2)}) %copy-start) | copy-done | bytes 524312
  1.7 1.0 %copy-done.2 = bf16[128,2048]{1,0:T(8,128)(2,1)S(1)} copy-done((bf16[128,2048]{1,0:T(8,128)(2,1)S(1)}, bf16[128,2048]{1,0:T(8,128)(2,1)}, u32[]{:S(2)}) %copy-start.2) | copy-done | bytes 524312
  2.7 0.3 shard_map.76
  3.1 20.6 %all_to_all.10.in_ref = bf16[4,512,128]{2,1,0:T(8,128)(2,1)S(1)} all-to-all(bf16[4,512,128]{2,1,0:T(8,128)(2,1)S(1)} %shard_map.76), channel_id=1, replica_groups=mesh['head'=4,'span'=8] {'head'}, dimensions={0} | all-to-all | bytes 1048576 | tf_op jit(solution)/shard_map/all_to_all | solution.py:203
  23.9 1.3 %collective-permute-done.b_ref.pair_ref = bf16[512,128]{1,0:T(8,128)(2,1)S(1)} collective-permute-done((bf16[512,128]{1,0:T(8,128)(2,1)S(1)}, bf16[512,128]{1,0:T(8,128)(2,1)S(1)}, u32[]{:S(2)}, u32[]{:S(2)}) %collective-permute-start) | collective-permute-done | bytes 131104 | tf_op jit(solution)/shard_map/ppermute | solution.py:207
  25.2 2.5 %collective-permute-start.3 = (bf16[512,128]{1,0:T(8,128)(2,1)S(1)}, bf16[512,128]{1,0:T(8,128)(2,1)S(1)}, u32[]{:S(2)}, u32[]{:S(2)}) collective-permute-start(bf16[512,128]{1,0:T(8,128)(2,1)S(1)} %shard_map.78), channel_id=1, source_target_pairs={{0,6},{1,7},{2,4},{3,5},{4,2},{5,3},{6,0},{7,1},{8,14},{9,15},{10,... | collective-permute-start | bytes 393224 | tf_op jit(solution)/shard_map/ppermute | solution.py:207
  27.7 0.5 collective-permute-start.2
  28.2 0.5 collective-permute-start.1
  28.8 3.3 %collective-permute-done.3.refs_2_ = bf16[512,128]{1,0:T(8,128)(2,1)S(1)} collective-permute-done((bf16[512,128]{1,0:T(8,128)(2,1)S(1)}, bf16[512,128]{1,0:T(8,128)(2,1)S(1)}, u32[]{:S(2)}, u32[]{:S(2)}) %collective-permute-start.3) | collective-permute-done | bytes 131104 | tf_op jit(solution)/shard_map/ppermute | solution.py:207
  32.1 2.5 %collective-permute-done.2.refs_1_ = bf16[512,128]{1,0:T(8,128)(2,1)S(1)} collective-permute-done((bf16[512,128]{1,0:T(8,128)(2,1)S(1)}, bf16[512,128]{1,0:T(8,128)(2,1)S(1)}, u32[]{:S(2)}, u32[]{:S(2)}) %collective-permute-start.2) | collective-permute-done | bytes 131104 | tf_op jit(solution)/shard_map/ppermute | solution.py:207
  34.5 0.1 collective-permute-done.1.refs_0_
  34.6 1.0 shard_map.79
  35.6 3.5 %all-to-all-start.1 = ((bf16[4,512,128]{2,1,0:T(8,128)(2,1)}), bf16[4,512,128]{2,1,0:T(8,128)(2,1)S(1)}, u32[]{:S(2)}, u32[]{:S(2)}) async-start(bf16[4,512,128]{2,1,0:T(8,128)(2,1)} %shard_map.79), calls=%async_computation.1 | async-start | bytes 1048576 | tf_op jit(solution)/shard_map/all_to_all | solution.py:203
  39.1 2.7 %shard_map.75 = (bf16[128,2048]{1,0:T(8,128)(2,1)}, bf16[512,128]{1,0:T(8,128)(2,1)}, bf16[512,128]{1,0:T(8,128)(2,1)}, bf16[512,128]{1,0:T(8,128)(2,1)}, bf16[512,128]{1,0:T(8,128)(2,1)}) custom-call(bf16[128,2048]{1,0:T(8,128)(2,1)} %q_ref.3, bf16[128,2048]{1,0:T(8,128)(2,1)} %g_hbm.1), custom_call_target="tpu_custom_call" | custom-call | flops 67108864 | bytes 2097152 | tf_op jit(solution)/shard_map/pallas_call | solution.py:225
  41.8 2.0 %collective-permute-start.4 = (bf16[512,128]{1,0:T(8,128)(2,1)}, bf16[512,128]{1,0:T(8,128)(2,1)S(1)}, u32[]{:S(2)}, u32[]{:S(2)}) collective-permute-start(bf16[512,128]{1,0:T(8,128)(2,1)} %get-tuple-element.21), channel_id=1, source_target_pairs={{0,8},{8,0},{16,24},{24,16},{1,9},{9,1},{17,25},{25,17},{2,10},{10... | collective-permute-start | bytes 393224 | tf_op jit(solution)/shard_map/ppermute | solution.py:207
  43.8 2.4 %collective-permute-start.5 = (bf16[512,128]{1,0:T(8,128)(2,1)}, bf16[512,128]{1,0:T(8,128)(2,1)S(1)}, u32[]{:S(2)}, u32[]{:S(2)}) collective-permute-start(bf16[512,128]{1,0:T(8,128)(2,1)} %get-tuple-element.22), channel_id=1, source_target_pairs={{0,16},{8,24},{16,0},{24,8},{1,17},{9,25},{17,1},{25,9},{2,18},{10... | collective-permute-start | bytes 393224 | tf_op jit(solution)/shard_map/ppermute | solution.py:207
  46.3 5.5 %collective-permute-done.4.refs_1_.refs_2_ = bf16[512,128]{1,0:T(8,128)(2,1)S(1)} collective-permute-done((bf16[512,128]{1,0:T(8,128)(2,1)}, bf16[512,128]{1,0:T(8,128)(2,1)S(1)}, u32[]{:S(2)}, u32[]{:S(2)}) %collective-permute-start.4) | collective-permute-done | bytes 131104 | tf_op jit(solution)/shard_map/ppermute | solution.py:207
  51.7 11.6 %collective-permute-done.5.refs_2_.refs_3_ = bf16[512,128]{1,0:T(8,128)(2,1)S(1)} collective-permute-done((bf16[512,128]{1,0:T(8,128)(2,1)}, bf16[512,128]{1,0:T(8,128)(2,1)S(1)}, u32[]{:S(2)}, u32[]{:S(2)}) %collective-permute-start.5) | collective-permute-done | bytes 131104 | tf_op jit(solution)/shard_map/ppermute | solution.py:207
  63.3 0.9 copy-done.6
  64.4 1.3 %collective-permute-done.7.b_ref.refs_0_ = bf16[512,128]{1,0:T(8,128)(2,1)S(1)} collective-permute-done((bf16[512,128]{1,0:T(8,128)(2,1)S(1)}, bf16[512,128]{1,0:T(8,128)(2,1)S(1)}, u32[]{:S(2)}, u32[]{:S(2)}) %collective-permute-start.7) | collective-permute-done | bytes 131104 | tf_op jit(solution)/shard_map/ppermute | solution.py:207
  65.8 1.1 %collective-permute-start.10 = (bf16[512,128]{1,0:T(8,128)(2,1)S(1)}, bf16[512,128]{1,0:T(8,128)(2,1)S(1)}, u32[]{:S(2)}, u32[]{:S(2)}) collective-permute-start(bf16[512,128]{1,0:T(8,128)(2,1)S(1)} %shard_map.82), channel_id=1, source_target_pairs={{0,6},{1,7},{2,4},{3,5},{4,2},{5,3},{6,0},{7,1},{8,14},{9,15},{10,... | collective-permute-start | bytes 393224 | tf_op jit(solution)/shard_map/ppermute | solution.py:207
  66.9 1.9 %collective-permute-start.9 = (bf16[512,128]{1,0:T(8,128)(2,1)S(1)}, bf16[512,128]{1,0:T(8,128)(2,1)S(1)}, u32[]{:S(2)}, u32[]{:S(2)}) collective-permute-start(bf16[512,128]{1,0:T(8,128)(2,1)S(1)} %shard_map.82), channel_id=1, source_target_pairs={{0,4},{1,5},{2,6},{3,7},{4,0},{5,1},{6,2},{7,3},{8,12},{9,13},{10,... | collective-permute-start | bytes 393224 | tf_op jit(solution)/shard_map/ppermute | solution.py:207
  68.8 0.5 collective-permute-start.8
  69.4 3.8 %collective-permute-done.10.refs_7_ = bf16[512,128]{1,0:T(8,128)(2,1)S(1)} collective-permute-done((bf16[512,128]{1,0:T(8,128)(2,1)S(1)}, bf16[512,128]{1,0:T(8,128)(2,1)S(1)}, u32[]{:S(2)}, u32[]{:S(2)}) %collective-permute-start.10) | collective-permute-done | bytes 131104 | tf_op jit(solution)/shard_map/ppermute | solution.py:207
  73.2 1.9 %collective-permute-done.9.refs_6_ = bf16[512,128]{1,0:T(8,128)(2,1)S(1)} collective-permute-done((bf16[512,128]{1,0:T(8,128)(2,1)S(1)}, bf16[512,128]{1,0:T(8,128)(2,1)S(1)}, u32[]{:S(2)}, u32[]{:S(2)}) %collective-permute-start.9) | collective-permute-done | bytes 131104 | tf_op jit(solution)/shard_map/ppermute | solution.py:207
  75.1 0.3 shard_map.83
  75.5 2.5 %collective-permute-start.11 = (bf16[512,128]{1,0:T(8,128)(2,1)S(1)}, bf16[512,128]{1,0:T(8,128)(2,1)S(1)}, u32[]{:S(2)}, u32[]{:S(2)}) collective-permute-start(bf16[512,128]{1,0:T(8,128)(2,1)S(1)} %get-tuple-element.25), channel_id=1, source_target_pairs={{0,8},{8,0},{16,24},{24,16},{1,9},{9,1},{17,25},{25,17},{2,10},{10... | collective-permute-start | bytes 393224 | tf_op jit(solution)/shard_map/ppermute | solution.py:207
  78.1 2.4 %collective-permute-start.13 = (bf16[512,128]{1,0:T(8,128)(2,1)S(1)}, bf16[512,128]{1,0:T(8,128)(2,1)S(1)}, u32[]{:S(2)}, u32[]{:S(2)}) collective-permute-start(bf16[512,128]{1,0:T(8,128)(2,1)S(1)} %get-tuple-element.27), channel_id=1, source_target_pairs={{0,24},{8,16},{16,8},{24,0},{1,25},{9,17},{17,9},{25,1},{2,26},{10... | collective-permute-start | bytes 393224 | tf_op jit(solution)/shard_map/ppermute | solution.py:207
  80.4 2.2 %collective-permute-done.11.refs_1_ = bf16[512,128]{1,0:T(8,128)(2,1)S(1)} collective-permute-done((bf16[512,128]{1,0:T(8,128)(2,1)S(1)}, bf16[512,128]{1,0:T(8,128)(2,1)S(1)}, u32[]{:S(2)}, u32[]{:S(2)}) %collective-permute-start.11) | collective-permute-done | bytes 131104 | tf_op jit(solution)/shard_map/ppermute | solution.py:207
  82.6 7.9 %collective-permute-done.12.refs_2_ = bf16[512,128]{1,0:T(8,128)(2,1)S(1)} collective-permute-done((bf16[512,128]{1,0:T(8,128)(2,1)S(1)}, bf16[512,128]{1,0:T(8,128)(2,1)S(1)}, u32[]{:S(2)}, u32[]{:S(2)}) %collective-permute-start.12) | collective-permute-done | bytes 131104 | tf_op jit(solution)/shard_map/ppermute | solution.py:207
  90.5 3.5 %shard_map.84 = (bf16[128,2048]{1,0:T(8,128)(2,1)}, bf16[128,2048]{1,0:T(8,128)(2,1)}) custom-call(bf16[128,2048]{1,0:T(8,128)(2,1)S(1)} %copy-done.4, bf16[128,2048]{1,0:T(8,128)(2,1)S(1)} %copy-done.1, bf16[128,2048]{1,0:T(8,128)(2,1)S(1)} %copy-done.3, bf16[128,2048]{1,0:T(8,128)(2,1)S(1)} %copy-done.5, bf16[512,128]{1,0:T(8,128)(2,1)S(1)} %get-tuple-element.24.refs_0_, ...), custom_call_target="tpu_custom_call" | custom-call | flops 402653184 | bytes 5242880 | tf_op jit(solution)/shard_map/pallas_call | solution.py:225
  94.0 3.5 %shard_map.80 = (bf16[128,2048]{1,0:T(8,128)(2,1)}, bf16[128,2048]{1,0:T(8,128)(2,1)}) custom-call(bf16[128,2048]{1,0:T(8,128)(2,1)S(1)} %copy-done.4, bf16[128,2048]{1,0:T(8,128)(2,1)S(1)} %copy-done.1, bf16[128,2048]{1,0:T(8,128)(2,1)S(1)} %copy-done.3, bf16[128,2048]{1,0:T(8,128)(2,1)S(1)} %copy-done.5, bf16[4,512,128]{2,1,0:T(8,128)(2,1)S(1)} %all-to-all-done.1.f_ref), custom_call_target="tpu_custom_call" | custom-call | flops 402653184 | bytes 5242880 | tf_op jit(solution)/shard_map/pallas_call | solution.py:225
  (23 shorter events, 0.5 us)
Async XLA Ops:
  0.6 1.0 %copy-start = (bf16[128,2048]{1,0:T(8,128)(2,1)S(1)}, bf16[128,2048]{1,0:T(8,128)(2,1)}, u32[]{:S(2)}) copy-start(bf16[128,2048]{1,0:T(8,128)(2,1)} %k_ref.5) | copy-start | bytes 1572868
  1.7 1.0 %copy-start.2 = (bf16[128,2048]{1,0:T(8,128)(2,1)S(1)}, bf16[128,2048]{1,0:T(8,128)(2,1)}, u32[]{:S(2)}) copy-start(bf16[128,2048]{1,0:T(8,128)(2,1)} %v_ref.5) | copy-start | bytes 1572868
  23.8 1.4 %collective-permute-start = (bf16[512,128]{1,0:T(8,128)(2,1)S(1)}, bf16[512,128]{1,0:T(8,128)(2,1)S(1)}, u32[]{:S(2)}, u32[]{:S(2)}) collective-permute-start(bf16[512,128]{1,0:T(8,128)(2,1)S(1)} %shard_map.77.a_ref), channel_id=1, source_target_pairs={{0,1},{1,0},{2,3},{3,2},{4,5},{5,4},{6,7},{7,6},{8,9},{9,8},{10,11... | collective-permute-start | bytes 393224 | tf_op jit(solution)/shard_map/ppermute | solution.py:207
  25.2 6.9 %collective-permute-start.3 = (bf16[512,128]{1,0:T(8,128)(2,1)S(1)}, bf16[512,128]{1,0:T(8,128)(2,1)S(1)}, u32[]{:S(2)}, u32[]{:S(2)}) collective-permute-start(bf16[512,128]{1,0:T(8,128)(2,1)S(1)} %shard_map.78), channel_id=1, source_target_pairs={{0,6},{1,7},{2,4},{3,5},{4,2},{5,3},{6,0},{7,1},{8,14},{9,15},{10,... | collective-permute-start | bytes 393224 | tf_op jit(solution)/shard_map/ppermute | solution.py:207
  27.7 6.8 %collective-permute-start.2 = (bf16[512,128]{1,0:T(8,128)(2,1)S(1)}, bf16[512,128]{1,0:T(8,128)(2,1)S(1)}, u32[]{:S(2)}, u32[]{:S(2)}) collective-permute-start(bf16[512,128]{1,0:T(8,128)(2,1)S(1)} %shard_map.78), channel_id=1, source_target_pairs={{0,4},{1,5},{2,6},{3,7},{4,0},{5,1},{6,2},{7,3},{8,12},{9,13},{10,... | collective-permute-start | bytes 393224 | tf_op jit(solution)/shard_map/ppermute | solution.py:207
  28.2 6.4 %collective-permute-start.1 = (bf16[512,128]{1,0:T(8,128)(2,1)S(1)}, bf16[512,128]{1,0:T(8,128)(2,1)S(1)}, u32[]{:S(2)}, u32[]{:S(2)}) collective-permute-start(bf16[512,128]{1,0:T(8,128)(2,1)S(1)} %shard_map.78), channel_id=1, source_target_pairs={{0,2},{1,3},{2,0},{3,1},{4,6},{5,7},{6,4},{7,5},{8,10},{9,11},{10,... | collective-permute-start | bytes 393224 | tf_op jit(solution)/shard_map/ppermute | solution.py:207
  35.6 58.4 %all-to-all-start.1 = ((bf16[4,512,128]{2,1,0:T(8,128)(2,1)}), bf16[4,512,128]{2,1,0:T(8,128)(2,1)S(1)}, u32[]{:S(2)}, u32[]{:S(2)}) async-start(bf16[4,512,128]{2,1,0:T(8,128)(2,1)} %shard_map.79), calls=%async_computation.1 | async-start | bytes 1048576 | tf_op jit(solution)/shard_map/all_to_all | solution.py:203
  41.8 9.9 %collective-permute-start.4 = (bf16[512,128]{1,0:T(8,128)(2,1)}, bf16[512,128]{1,0:T(8,128)(2,1)S(1)}, u32[]{:S(2)}, u32[]{:S(2)}) collective-permute-start(bf16[512,128]{1,0:T(8,128)(2,1)} %get-tuple-element.21), channel_id=1, source_target_pairs={{0,8},{8,0},{16,24},{24,16},{1,9},{9,1},{17,25},{25,17},{2,10},{10... | collective-permute-start | bytes 393224 | tf_op jit(solution)/shard_map/ppermute | solution.py:207
  43.8 19.5 %collective-permute-start.5 = (bf16[512,128]{1,0:T(8,128)(2,1)}, bf16[512,128]{1,0:T(8,128)(2,1)S(1)}, u32[]{:S(2)}, u32[]{:S(2)}) collective-permute-start(bf16[512,128]{1,0:T(8,128)(2,1)} %get-tuple-element.22), channel_id=1, source_target_pairs={{0,16},{8,24},{16,0},{24,8},{1,17},{9,25},{17,1},{25,9},{2,18},{10... | collective-permute-start | bytes 393224 | tf_op jit(solution)/shard_map/ppermute | solution.py:207
  46.2 17.1 %collective-permute-start.6 = (bf16[512,128]{1,0:T(8,128)(2,1)}, bf16[512,128]{1,0:T(8,128)(2,1)S(1)}, u32[]{:S(2)}, u32[]{:S(2)}) collective-permute-start(bf16[512,128]{1,0:T(8,128)(2,1)} %get-tuple-element.23), channel_id=1, source_target_pairs={{0,24},{8,16},{16,8},{24,0},{1,25},{9,17},{17,9},{25,1},{2,26},{10... | collective-permute-start | bytes 393224 | tf_op jit(solution)/shard_map/ppermute | solution.py:207
  63.3 0.9 copy-start.6
  64.3 26.3 %copy-start.4 = (bf16[128,2048]{1,0:T(8,128)(2,1)S(1)}, bf16[128,2048]{1,0:T(8,128)(2,1)}, u32[]{:S(2)}) copy-start(bf16[128,2048]{1,0:T(8,128)(2,1)} %q_ref.3) | copy-start | bytes 1572868
  64.3 26.3 %copy-start.5 = (bf16[128,2048]{1,0:T(8,128)(2,1)S(1)}, bf16[128,2048]{1,0:T(8,128)(2,1)}, u32[]{:S(2)}) copy-start(bf16[128,2048]{1,0:T(8,128)(2,1)} %get-tuple-element.17.c_ref) | copy-start | bytes 1572868
  64.3 1.4 %collective-permute-start.7 = (bf16[512,128]{1,0:T(8,128)(2,1)S(1)}, bf16[512,128]{1,0:T(8,128)(2,1)S(1)}, u32[]{:S(2)}, u32[]{:S(2)}) collective-permute-start(bf16[512,128]{1,0:T(8,128)(2,1)S(1)} %shard_map.81.a_ref), channel_id=1, source_target_pairs={{0,1},{1,0},{2,3},{3,2},{4,5},{5,4},{6,7},{7,6},{8,9},{9,8},{10,11... | collective-permute-start | bytes 393224 | tf_op jit(solution)/shard_map/ppermute | solution.py:207
  65.8 24.8 %copy-start.1 = (bf16[128,2048]{1,0:T(8,128)(2,1)S(1)}, bf16[128,2048]{1,0:T(8,128)(2,1)}, u32[]{:S(2)}) copy-start(bf16[128,2048]{1,0:T(8,128)(2,1)} %k_ref.5) | copy-start | bytes 1572868
  65.8 24.7 %copy-start.3 = (bf16[128,2048]{1,0:T(8,128)(2,1)S(1)}, bf16[128,2048]{1,0:T(8,128)(2,1)}, u32[]{:S(2)}) copy-start(bf16[128,2048]{1,0:T(8,128)(2,1)} %v_ref.5) | copy-start | bytes 1572868
  65.8 7.4 %collective-permute-start.10 = (bf16[512,128]{1,0:T(8,128)(2,1)S(1)}, bf16[512,128]{1,0:T(8,128)(2,1)S(1)}, u32[]{:S(2)}, u32[]{:S(2)}) collective-permute-start(bf16[512,128]{1,0:T(8,128)(2,1)S(1)} %shard_map.82), channel_id=1, source_target_pairs={{0,6},{1,7},{2,4},{3,5},{4,2},{5,3},{6,0},{7,1},{8,14},{9,15},{10,... | collective-permute-start | bytes 393224 | tf_op jit(solution)/shard_map/ppermute | solution.py:207
  66.9 8.2 %collective-permute-start.9 = (bf16[512,128]{1,0:T(8,128)(2,1)S(1)}, bf16[512,128]{1,0:T(8,128)(2,1)S(1)}, u32[]{:S(2)}, u32[]{:S(2)}) collective-permute-start(bf16[512,128]{1,0:T(8,128)(2,1)S(1)} %shard_map.82), channel_id=1, source_target_pairs={{0,4},{1,5},{2,6},{3,7},{4,0},{5,1},{6,2},{7,3},{8,12},{9,13},{10,... | collective-permute-start | bytes 393224 | tf_op jit(solution)/shard_map/ppermute | solution.py:207
  68.8 6.3 %collective-permute-start.8 = (bf16[512,128]{1,0:T(8,128)(2,1)S(1)}, bf16[512,128]{1,0:T(8,128)(2,1)S(1)}, u32[]{:S(2)}, u32[]{:S(2)}) collective-permute-start(bf16[512,128]{1,0:T(8,128)(2,1)S(1)} %shard_map.82), channel_id=1, source_target_pairs={{0,2},{1,3},{2,0},{3,1},{4,6},{5,7},{6,4},{7,5},{8,10},{9,11},{10,... | collective-permute-start | bytes 393224 | tf_op jit(solution)/shard_map/ppermute | solution.py:207
  75.5 7.2 %collective-permute-start.11 = (bf16[512,128]{1,0:T(8,128)(2,1)S(1)}, bf16[512,128]{1,0:T(8,128)(2,1)S(1)}, u32[]{:S(2)}, u32[]{:S(2)}) collective-permute-start(bf16[512,128]{1,0:T(8,128)(2,1)S(1)} %get-tuple-element.25), channel_id=1, source_target_pairs={{0,8},{8,0},{16,24},{24,16},{1,9},{9,1},{17,25},{25,17},{2,10},{10... | collective-permute-start | bytes 393224 | tf_op jit(solution)/shard_map/ppermute | solution.py:207
  78.0 12.5 %collective-permute-start.12 = (bf16[512,128]{1,0:T(8,128)(2,1)S(1)}, bf16[512,128]{1,0:T(8,128)(2,1)S(1)}, u32[]{:S(2)}, u32[]{:S(2)}) collective-permute-start(bf16[512,128]{1,0:T(8,128)(2,1)S(1)} %get-tuple-element.26), channel_id=1, source_target_pairs={{0,16},{8,24},{16,0},{24,8},{1,17},{9,25},{17,1},{25,9},{2,18},{10... | collective-permute-start | bytes 393224 | tf_op jit(solution)/shard_map/ppermute | solution.py:207
  78.1 12.5 %collective-permute-start.13 = (bf16[512,128]{1,0:T(8,128)(2,1)S(1)}, bf16[512,128]{1,0:T(8,128)(2,1)S(1)}, u32[]{:S(2)}, u32[]{:S(2)}) collective-permute-start(bf16[512,128]{1,0:T(8,128)(2,1)S(1)} %get-tuple-element.27), channel_id=1, source_target_pairs={{0,24},{8,16},{16,8},{24,0},{1,25},{9,17},{17,9},{25,1},{2,26},{10... | collective-permute-start | bytes 393224 | tf_op jit(solution)/shard_map/ppermute | solution.py:207

commit v5 on v3

--- a/solution.py
+++ b/solution.py
@@ -14,6 +14,8 @@
 TN = (((0,), (0,)), ((), ()))
 AXES = ("span", "head")
 VMEM = 20 * 2**20
+KEPT = 12
+FIRST = ((3,), (2, 1, 0))
 
 
 def dot(a, b, dims=None):
@@ -45,38 +47,33 @@
         s_ref[pl.ds(h * parts, parts)] = fwd.reshape(parts, DH // parts, DH)
 
 
-def back_states_kernel(q_hbm, g_hbm, c_hbm, *refs):
-    t_hbms, (q_ref, g_ref, c_ref, t_ref, in_sems, out_sems) = refs[:-6], refs[-6:]
-    groups = len(t_hbms)
+def scaled_of(g, coef):
+    return (g.astype(F32) * coef).astype(BF16)
+
+
+def back_states_kernel(groups, order, q_hbm, g_hbm, *refs):
+    t_hbms, (q_ref, g_ref, t_ref, in_sems, out_sems) = refs[:-5], refs[-5:]
     width = HEADS // groups * DH
-    order = list(range(1, groups)) + [0]
-    loads = {}
-    for k in order:
+    loads = []
+    for i, k in enumerate(order):
         cols = pl.ds(pl.multiple_of(group_of(k, groups) * width, DH), width)
-        loads[k] = [
-            pltpu.make_async_copy(g_hbm.at[:, cols], g_ref.at[k], in_sems.at[0, k]),
-            pltpu.make_async_copy(q_hbm.at[:, cols], q_ref.at[k], in_sems.at[1, k]),
-        ]
-        for copy in loads[k]:
+        loads.append((
+            pltpu.make_async_copy(g_hbm.at[:, cols], g_ref.at[i], in_sems.at[0, i]),
+            pltpu.make_async_copy(q_hbm.at[:, cols], q_ref.at[i], in_sems.at[1, i]),
+        ))
+        for copy in loads[-1]:
             copy.start()
     coef = coef_of(q_hbm.shape[0])
     stores = []
-    for k in order:
-        for copy in loads[k]:
+    for i in range(len(order)):
+        for copy in loads[i]:
             copy.wait()
         for h in range(HEADS // groups):
             cols = pl.ds(h * DH, DH)
-            scaled = (g_ref[k, :, cols].astype(F32) * coef).astype(BF16)
-            c_ref[k, :, cols] = scaled
-            t_ref[k, cols, :] = dot(scaled, q_ref[k, :, cols], TN).astype(BF16)
-        cols = pl.ds(pl.multiple_of(group_of(k, groups) * width, DH), width)
-        group = [
-            pltpu.make_async_copy(t_ref.at[k], t_hbms[k], out_sems.at[0, k]),
-            pltpu.make_async_copy(c_ref.at[k], c_hbm.at[:, cols], out_sems.at[1, k]),
-        ]
-        for copy in group:
-            copy.start()
-        stores += group
+            scaled = scaled_of(g_ref[i, :, cols], coef)
+            t_ref[i, cols, :] = dot(scaled, q_ref[i, :, cols], TN).astype(BF16)
+        stores.append(pltpu.make_async_copy(t_ref.at[i], t_hbms[i], out_sems.at[i]))
+        stores[-1].start()
     for copy in stores:
         copy.wait()
 
@@ -90,32 +87,45 @@
 
 
 def total_kernel(*refs):
-    total = refs[0][...].astype(F32)
-    for ref in refs[1:-1]:
-        total += ref[...].astype(F32)
-    refs[-1][...] = total.astype(BF16)
+    t_refs, keep_ref, send_ref = refs[:-2], refs[-2], refs[-1]
+    half = keep_ref.shape[0]
+    core = lax.axis_index("span") % 2
+    for out_ref, part in ((keep_ref, core), (send_ref, 1 - core)):
+        rows = pl.ds(pl.multiple_of(part * half, half), half)
+        total = t_refs[0][rows, :].astype(F32)
+        for ref in t_refs[1:]:
+            total += ref[rows, :].astype(F32)
+        out_ref[...] = total.astype(BF16)
 
 
 def pair_kernel(a_ref, b_ref, out_ref):
     out_ref[...] = (a_ref[...].astype(F32) + b_ref[...].astype(F32)).astype(BF16)
 
 
-def back_combine_kernel(groups, pair_ref, *refs):
-    chips = len(refs) - 2 * groups - 1
-    t_refs, chip_refs = refs[:groups], refs[groups : groups + chips]
-    b_refs, held = refs[groups + chips : -1], refs[-1]
-    span, plane = lax.axis_index("span"), lax.axis_index("head")
+def after_kernel(keep_ref, got_ref, *refs):
+    chip_refs, own_ref, send_ref = refs[:-2], refs[-2], refs[-1]
+    span = lax.axis_index("span")
+    chip, first = span // 2, span % 2 == 0
+    total = jnp.zeros(own_ref.shape, F32)
+    for k, ref in enumerate(chip_refs):
+        total += jnp.where((chip ^ (k + 1)) > chip, ref[...].astype(F32), 0.0)
+    own_ref[...] = total + jnp.where(first, got_ref[...].astype(F32), 0.0)
+    send_ref[...] = (total + jnp.where(first, 0.0, keep_ref[...].astype(F32))).astype(BF16)
+
+
+def back_combine_kernel(groups, own_ref, other_ref, *refs):
+    t_refs, b_refs, held = refs[:groups], refs[groups:-1], refs[-1]
+    plane, core = lax.axis_index("head"), lax.axis_index("span") % 2
+    half = own_ref.shape[0]
     for k in range(groups):
         held[plane ^ k] = t_refs[k][...]
-    total = jnp.where(span % 2 == 0, pair_ref[...].astype(F32), 0.0)
-    chip = span // 2
-    for k in range(chips):
-        after = (chip ^ (k + 1)) > chip
-        total += jnp.where(after, chip_refs[k][...].astype(F32), 0.0)
-    for z in reversed(range(groups)):
-        own = held[z].astype(F32)
-        held[z] = total.astype(BF16)
-        total += own
+    for part, ref in ((core, own_ref), (1 - core, other_ref)):
+        rows = pl.ds(pl.multiple_of(part * half, half), half)
+        total = ref[...].astype(F32)
+        for z in reversed(range(groups)):
+            own = held[z, rows, :].astype(F32)
+            held[z, rows, :] = total.astype(BF16)
+            total += own
     for k in range(groups):
         b_refs[k][...] = held[plane ^ k]
 
@@ -140,33 +150,45 @@
     return copies
 
 
-def fwd_final_kernel(q_ref, k_ref, v_ref, c_ref, f_ref, out_hbm, dq_hbm, held, sems):
-    length = q_ref.shape[0]
-    coef = coef_of(length)
+def fwd_scores_kernel(q_ref, k_ref, v_ref, g_ref, sc_ref, ds_ref):
+    coef = coef_of(q_ref.shape[0])
+    row, col = square_of(q_ref.shape[0])
+    for h in range(HEADS):
+        cols = pl.ds(h * DH, DH)
+        sc_ref[h] = masked(q_ref[:, cols], k_ref[:, cols], col <= row)
+        if h < ds_ref.shape[0]:
+            ds_ref[h] = masked(scaled_of(g_ref[:, cols], coef), v_ref[:, cols], col <= row)
+
+
+def fwd_final_kernel(
+    q_ref, k_ref, v_ref, g_ref, sc_ref, ds_ref, f_ref, out_hbm, dq_hbm, held, sems
+):
+    coef = coef_of(q_ref.shape[0])
+    row, col = square_of(q_ref.shape[0])
     parts = DH // f_ref.shape[1]
     slots = held.shape[1]
-    row, col = square_of(length)
     copies = []
     for slot in range(slots):
         for i in range(HEADS // slots):
             h = slot * (HEADS // slots) + i
             cols, to = pl.ds(h * DH, DH), pl.ds(i * DH, DH)
-            q, k, v, c = q_ref[:, cols], k_ref[:, cols], v_ref[:, cols], c_ref[:, cols]
+            q, k, v = q_ref[:, cols], k_ref[:, cols], v_ref[:, cols]
+            c = scaled_of(g_ref[:, cols], coef)
             fwd = f_ref[pl.ds(h * parts, parts)].reshape(DH, DH)
-            own = dot(masked(q, k, col <= row), v) + dot(q, fwd)
-            held[0, slot, :, to] = (own * coef).astype(BF16)
-            dq = dot(masked(c, v, col <= row), k) + dot(c, fwd, NT)
-            held[1, slot, :, to] = dq.astype(BF16)
+            held[0, slot, :, to] = ((dot(sc_ref[h], v) + dot(q, fwd)) * coef).astype(BF16)
+            ds = ds_ref[h] if h < ds_ref.shape[0] else masked(c, v, col <= row)
+            held[1, slot, :, to] = (dot(ds, k) + dot(c, fwd, NT)).astype(BF16)
         width = HEADS // slots * DH
         copies += write((out_hbm, dq_hbm), held, sems, slot, slot * width, width)
     for copy in copies:
         copy.wait()
 
 
-def back_final_kernel(q_ref, k_ref, v_ref, c_ref, *refs):
+def back_final_kernel(q_ref, k_ref, v_ref, g_ref, *refs):
     b_refs, (dk_hbm, dv_hbm, held, sems) = refs[:-4], refs[-4:]
     groups = len(b_refs)
     slots = held.shape[1]
+    coef = coef_of(q_ref.shape[0])
     row, col = square_of(q_ref.shape[0])
     copies = []
     for slot in range(slots):
@@ -174,7 +196,8 @@
             g = slot * groups // slots
             h = slot * (HEADS // slots) + i - g * (HEADS // groups)
             cols, to = columns(g, groups, h), pl.ds(i * DH, DH)
-            q, k, v, c = q_ref[:, cols], k_ref[:, cols], v_ref[:, cols], c_ref[:, cols]
+            q, k, v = q_ref[:, cols], k_ref[:, cols], v_ref[:, cols]
+            c = scaled_of(g_ref[:, cols], coef)
             back = b_refs[g][pl.ds(h * DH, DH), :]
             dk = dot(masked(v, c, col >= row), q) + dot(v, back)
             held[0, slot, :, to] = dk.astype(BF16)
@@ -225,21 +248,27 @@
     matmul = 2 * HEADS * length * DH * DH
     hbm = pl.BlockSpec(memory_space=pltpu.HBM)
     vmem = pl.BlockSpec(memory_space=pltpu.VMEM)
-    staged = [pltpu.VMEM((groups, length, feat // groups), BF16)] * 3
-    staged += [
-        pltpu.VMEM((groups, feat // groups, DH), BF16),
-        pltpu.SemaphoreType.DMA((2, groups)),
-        pltpu.SemaphoreType.DMA((2, groups)),
-    ]
     held = [
         pltpu.VMEM((2, 4, length, feat // 4), BF16),
         pltpu.SemaphoreType.DMA((2, 4)),
     ]
 
-    scaled, *back_states = call(
-        back_states_kernel, [rows_of] + [piece_of] * groups, matmul,
-        queries, out_grad, scratch=staged, ins=[hbm] * 2, outs=[hbm] * (groups + 1), limit=None,
-    )
+    back_states = [None] * groups
+    for order in FIRST if direct else ((0,),):
+        outs = call(
+            lambda *refs, order=order: back_states_kernel(groups, order, *refs),
+            [piece_of] * len(order), matmul * len(order) // groups,
+            queries, out_grad, ins=[hbm] * 2, outs=[hbm] * len(order), limit=None,
+            scratch=[
+                pltpu.VMEM((len(order), length, feat // groups), BF16),
+                pltpu.VMEM((len(order), length, feat // groups), BF16),
+                pltpu.VMEM((len(order), feat // groups, DH), BF16),
+                pltpu.SemaphoreType.DMA((2, len(order))),
+                pltpu.SemaphoreType.DMA((len(order),)),
+            ],
+        )
+        for k, piece in zip(order, outs):
+            back_states[k] = piece
     if direct:
         own = [back_states[0]] + [swap(back_states[k], "head", k) for k in range(1, groups)]
     states = call(fwd_states_kernel, state_of, matmul, keys, values)
@@ -248,13 +277,17 @@
         fwd = exchange(
             call(fwd_scan_kernel, jax.ShapeDtypeStruct(gathered.shape, BF16), 0, gathered),
         )
-        total = call(total_kernel, piece_of, 0, *own)
-        other = swap(total, "span", 1)
-        chip = call(pair_kernel, piece_of, 0, total, other)
-        chips = [swap(chip, "span", 2 * k) for k in range(1, span // 2)]
+        half_of = jax.ShapeDtypeStruct((feat // groups // 2, DH), BF16)
+        keep, send = call(total_kernel, [half_of] * 2, 0, *own)
+        got = swap(send, "span", 1)
+        both = call(pair_kernel, half_of, 0, keep, got)
+        chips = [swap(both, "span", 2 * k) for k in range(1, span // 2)]
+        wide_of = jax.ShapeDtypeStruct(half_of.shape, F32)
+        after, send = call(after_kernel, [wide_of, half_of], 0, keep, got, *chips)
+        other = swap(send, "span", 1)
         carried = call(
             lambda *refs: back_combine_kernel(groups, *refs),
-            [piece_of] * groups, 0, other, *own, *chips,
+            [piece_of] * groups, 0, after, other, *own,
             scratch=[pltpu.VMEM((groups, feat // groups, DH), BF16)],
         )
         back = [carried[0]] + [swap(carried[k], "head", k) for k in range(1, groups)]
@@ -266,9 +299,14 @@
         after = jnp.flip(jnp.cumsum(wide, axis=0) - wide, 0)
         back = [exchange(after.astype(BF16)).reshape(feat, DH)]
 
-    rows = (queries, keys, values, scaled)
+    rows = (queries, keys, values, out_grad)
+    scores = call(
+        fwd_scores_kernel,
+        [jax.ShapeDtypeStruct((heads, length, length), BF16) for heads in (HEADS, KEPT)],
+        2 * matmul, *rows,
+    )
     out, dq = call(
-        fwd_final_kernel, [rows_of] * 2, 6 * matmul, *rows, fwd,
+        fwd_final_kernel, [rows_of] * 2, 4 * matmul, *rows, *scores, fwd,
         scratch=held, outs=[hbm] * 2,
     )
     dk, dv = call(
@@ -279,7 +317,7 @@
 
 
 def direct_on(devices, planes, span):
-    return HEADS * DH // devices % 16 == 0 and planes in (2, 4) and span in (2, 4, 8)
+    return HEADS * DH // devices % 16 == 0 and planes == 4 and span in (4, 8)
 
 
 def solution(mesh):

time: 88.4 us -> 86.3 us (0.976)
  waiting for transfers between devices: 34.1 us -> 31.8 us
  Pallas kernels: 11.3 us -> 12.3 us
  local copies, waits for them, and re-layouts: 3 us -> 2.1 us
    ppermute x10 -> x11, waiting for transfers between devices: 34.1 us -> 31.8 us  [swap(): lax.ppermute(x, axis, [(i, i ^ k) for i in range(lax.axis_size(axis))])]
    pallas_call x8 -> x11, Pallas kernels: 11.3 us -> 12.3 us  [call(): pl.pallas_call(kernel, out_shape=out, in_specs=ins, out_specs=outs, scrat...]
    unnamed x14, local copies, waits for them, and re-layouts: 3 us -> 2.1 us
    ppermute x10 -> x11, starting transfers between devices: 13.4 us -> 13.5 us  [swap(): lax.ppermute(x, axis, [(i, i ^ k) for i in range(lax.axis_size(axis))])]
  transfers between devices with their start and end apart: 11 -> 12, of which waited for: 7 -> 9; matrix products, arithmetic and copies ran while one was open for 0% -> 0% of each run, Pallas kernels for 8% -> 10%
where the time goes in v5:
time: 86.3 us; the launch traced here: 86 us
  waiting for transfers between devices  31.8 us (37%)
  blocking collectives  21.4 us (25%)
  starting transfers between devices  17.7 us (21%)
  Pallas kernels  12.3 us (14%)
  local copies, waits for them, and re-layouts  2.1 us (2%)
    ppermute x11, waiting for transfers between devices, swap(): lax.ppermute(x, axis, [(i, i ^ k) for i in range(lax.axis_size(axis))])  31.8 us
    all_to_all x1, blocking collectives, exchange(): return lax.all_to_all(x, AXES, split_axis=0, concat_axis=0, tiled=True)  21.4 us
    ppermute x11, starting transfers between devices, swap(): lax.ppermute(x, axis, [(i, i ^ k) for i in range(lax.axis_size(axis))])  13.5 us
    pallas_call x11, Pallas kernels, call(): pl.pallas_call(kernel, out_shape=out, in_specs=ins, out_specs=outs, scrat...  12.3 us
    all_to_all x1, starting transfers between devices, exchange(): return lax.all_to_all(x, AXES, split_axis=0, concat_axis=0, tiled=True)  4.17 us
    unnamed x14, local copies, waits for them, and re-layouts  2.1 us
  transfers between devices with their start and end apart: 12, of which 9 were waited for; matrix products, arithmetic and copies ran while one was open for 0% of the time, Pallas kernels for 10%

profile of v5, /device:TPU:0, one launch (start us, length us, event | category | flops | bytes accessed | tf_op | source)
XLA Modules:
  0.0 86.0 jit_solution(5638620730860577256)
XLA Ops:
  0.6 1.0 %copy-done.2 = bf16[128,2048]{1,0:T(8,128)(2,1)S(1)} copy-done((bf16[128,2048]{1,0:T(8,128)(2,1)S(1)}, bf16[128,2048]{1,0:T(8,128)(2,1)}, u32[]{:S(2)}) %copy-start.2) | copy-done | bytes 524312
  1.7 1.0 %copy-done.4 = bf16[128,2048]{1,0:T(8,128)(2,1)S(1)} copy-done((bf16[128,2048]{1,0:T(8,128)(2,1)S(1)}, bf16[128,2048]{1,0:T(8,128)(2,1)}, u32[]{:S(2)}) %copy-start.4) | copy-done | bytes 524312
  2.7 0.3 shard_map.76
  3.1 21.4 %all_to_all.10.in_ref = bf16[32,64,128]{2,1,0:T(8,128)(2,1)S(1)} all-to-all(bf16[32,64,128]{2,1,0:T(8,128)(2,1)S(1)} %shard_map.76), channel_id=1, replica_groups=mesh['head'=4,'span'=8] {'span','head'}, dimensions={0} | all-to-all | bytes 1048576 | tf_op jit(solution)/shard_map/all_to_all | solution.py:214
  24.4 0.9 %shard_map.77 = bf16[32,64,128]{2,1,0:T(8,128)(2,1)} custom-call(bf16[32,64,128]{2,1,0:T(8,128)(2,1)S(1)} %all_to_all.10.in_ref), custom_call_target="tpu_custom_call" | custom-call | bytes 1048576 | tf_op jit(solution)/shard_map/pallas_call | solution.py:227
  25.3 4.2 %all-to-all-start.1 = ((bf16[32,64,128]{2,1,0:T(8,128)(2,1)}), bf16[32,64,128]{2,1,0:T(8,128)(2,1)S(1)}, u32[]{:S(2)}, u32[]{:S(2)}) async-start(bf16[32,64,128]{2,1,0:T(8,128)(2,1)} %shard_map.77), calls=%async_computation.1 | async-start | bytes 1048576 | tf_op jit(solution)/shard_map/all_to_all | solution.py:214
  29.5 2.4 %shard_map.79 = (bf16[512,128]{1,0:T(8,128)(2,1)}, bf16[512,128]{1,0:T(8,128)(2,1)}, bf16[512,128]{1,0:T(8,128)(2,1)}) custom-call(bf16[128,2048]{1,0:T(8,128)(2,1)} %q_ref.5, bf16[128,2048]{1,0:T(8,128)(2,1)} %g_ref.5), custom_call_target="tpu_custom_call" | custom-call | flops 50331648 | bytes 2097152 | tf_op jit(solution)/shard_map/pallas_call | solution.py:227
  31.9 1.8 %collective-permute-start = (bf16[512,128]{1,0:T(8,128)(2,1)}, bf16[512,128]{1,0:T(8,128)(2,1)S(1)}, u32[]{:S(2)}, u32[]{:S(2)}) collective-permute-start(bf16[512,128]{1,0:T(8,128)(2,1)} %get-tuple-element.26), channel_id=1, source_target_pairs={{0,8},{8,0},{16,24},{24,16},{1,9},{9,1},{17,25},{25,17},{2,10},{10... | collective-permute-start | bytes 393224 | tf_op jit(solution)/shard_map/ppermute | solution.py:218
  33.7 2.4 %collective-permute-start.1 = (bf16[512,128]{1,0:T(8,128)(2,1)}, bf16[512,128]{1,0:T(8,128)(2,1)S(1)}, u32[]{:S(2)}, u32[]{:S(2)}) collective-permute-start(bf16[512,128]{1,0:T(8,128)(2,1)} %get-tuple-element.27), channel_id=1, source_target_pairs={{0,16},{8,24},{16,0},{24,8},{1,17},{9,25},{17,1},{25,9},{2,18},{10... | collective-permute-start | bytes 393224 | tf_op jit(solution)/shard_map/ppermute | solution.py:218
  36.2 1.9 %shard_map.80 = bf16[512,128]{1,0:T(8,128)(2,1)} custom-call(bf16[128,2048]{1,0:T(8,128)(2,1)} %q_ref.5, bf16[128,2048]{1,0:T(8,128)(2,1)} %g_ref.5), custom_call_target="tpu_custom_call" | custom-call | flops 16777216 | bytes 2097152 | tf_op jit(solution)/shard_map/pallas_call | solution.py:227
  38.1 0.3 collective-permute-start.2
  38.4 4.5 %collective-permute-done.refs_1_.refs_3_ = bf16[512,128]{1,0:T(8,128)(2,1)S(1)} collective-permute-done((bf16[512,128]{1,0:T(8,128)(2,1)}, bf16[512,128]{1,0:T(8,128)(2,1)S(1)}, u32[]{:S(2)}, u32[]{:S(2)}) %collective-permute-start) | collective-permute-done | bytes 131104 | tf_op jit(solution)/shard_map/ppermute | solution.py:218
  42.9 10.6 %collective-permute-done.1.refs_2_.refs_4_ = bf16[512,128]{1,0:T(8,128)(2,1)S(1)} collective-permute-done((bf16[512,128]{1,0:T(8,128)(2,1)}, bf16[512,128]{1,0:T(8,128)(2,1)S(1)}, u32[]{:S(2)}, u32[]{:S(2)}) %collective-permute-start.1) | collective-permute-done | bytes 131104 | tf_op jit(solution)/shard_map/ppermute | solution.py:218
  53.5 0.1 shard_map.81
  53.6 0.1 collective-permute-start.3
  53.7 1.2 %collective-permute-done.3.b_ref.got_ref = bf16[256,128]{1,0:T(8,128)(2,1)S(1)} collective-permute-done((bf16[256,128]{1,0:T(8,128)(2,1)S(1)}, bf16[256,128]{1,0:T(8,128)(2,1)S(1)}, u32[]{:S(2)}, u32[]{:S(2)}) %collective-permute-start.3) | collective-permute-done | bytes 65568 | tf_op jit(solution)/shard_map/ppermute | solution.py:218
  55.0 1.5 %collective-permute-start.4 = (bf16[256,128]{1,0:T(8,128)(2,1)S(1)}, bf16[256,128]{1,0:T(8,128)(2,1)S(1)}, u32[]{:S(2)}, u32[]{:S(2)}) collective-permute-start(bf16[256,128]{1,0:T(8,128)(2,1)S(1)} %shard_map.82), channel_id=1, source_target_pairs={{0,2},{1,3},{2,0},{3,1},{4,6},{5,7},{6,4},{7,5},{8,10},{9,11},{10,... | collective-permute-start | bytes 196616 | tf_op jit(solution)/shard_map/ppermute | solution.py:218
  56.5 1.5 %collective-permute-start.5 = (bf16[256,128]{1,0:T(8,128)(2,1)S(1)}, bf16[256,128]{1,0:T(8,128)(2,1)S(1)}, u32[]{:S(2)}, u32[]{:S(2)}) collective-permute-start(bf16[256,128]{1,0:T(8,128)(2,1)S(1)} %shard_map.82), channel_id=1, source_target_pairs={{0,4},{1,5},{2,6},{3,7},{4,0},{5,1},{6,2},{7,3},{8,12},{9,13},{10,... | collective-permute-start | bytes 196616 | tf_op jit(solution)/shard_map/ppermute | solution.py:218
  58.0 0.5 collective-permute-start.6
  58.5 0.8 collective-permute-done.4.refs_0_
  59.3 1.5 %collective-permute-done.5.refs_1_ = bf16[256,128]{1,0:T(8,128)(2,1)S(1)} collective-permute-done((bf16[256,128]{1,0:T(8,128)(2,1)S(1)}, bf16[256,128]{1,0:T(8,128)(2,1)S(1)}, u32[]{:S(2)}, u32[]{:S(2)}) %collective-permute-start.5) | collective-permute-done | bytes 65568 | tf_op jit(solution)/shard_map/ppermute | solution.py:218
  60.8 2.4 %collective-permute-done.6.refs_2_ = bf16[256,128]{1,0:T(8,128)(2,1)S(1)} collective-permute-done((bf16[256,128]{1,0:T(8,128)(2,1)S(1)}, bf16[256,128]{1,0:T(8,128)(2,1)S(1)}, u32[]{:S(2)}, u32[]{:S(2)}) %collective-permute-start.6) | collective-permute-done | bytes 65568 | tf_op jit(solution)/shard_map/ppermute | solution.py:218
  63.1 0.1 shard_map.83
  63.3 1.2 %collective-permute-done.7.refs_1_ = bf16[256,128]{1,0:T(8,128)(2,1)S(1)} collective-permute-done((bf16[256,128]{1,0:T(8,128)(2,1)S(1)}, bf16[256,128]{1,0:T(8,128)(2,1)S(1)}, u32[]{:S(2)}, u32[]{:S(2)}) %collective-permute-start.7) | collective-permute-done | bytes 65568 | tf_op jit(solution)/shard_map/ppermute | solution.py:218
  64.6 0.2 shard_map.84
  64.7 2.8 %collective-permute-start.8 = (bf16[512,128]{1,0:T(8,128)(2,1)S(1)}, bf16[512,128]{1,0:T(8,128)(2,1)S(1)}, u32[]{:S(2)}, u32[]{:S(2)}) collective-permute-start(bf16[512,128]{1,0:T(8,128)(2,1)S(1)} %get-tuple-element.33), channel_id=1, source_target_pairs={{0,8},{8,0},{16,24},{24,16},{1,9},{9,1},{17,25},{25,17},{2,10},{10... | collective-permute-start | bytes 393224 | tf_op jit(solution)/shard_map/ppermute | solution.py:218
  67.6 2.4 %collective-permute-start.10 = (bf16[512,128]{1,0:T(8,128)(2,1)S(1)}, bf16[512,128]{1,0:T(8,128)(2,1)S(1)}, u32[]{:S(2)}, u32[]{:S(2)}) collective-permute-start(bf16[512,128]{1,0:T(8,128)(2,1)S(1)} %get-tuple-element.35), channel_id=1, source_target_pairs={{0,24},{8,16},{16,8},{24,0},{1,25},{9,17},{17,9},{25,1},{2,26},{10... | collective-permute-start | bytes 393224 | tf_op jit(solution)/shard_map/ppermute | solution.py:218
  70.0 0.8 shard_map.75
  70.8 1.8 %collective-permute-done.8.refs_1_ = bf16[512,128]{1,0:T(8,128)(2,1)S(1)} collective-permute-done((bf16[512,128]{1,0:T(8,128)(2,1)S(1)}, bf16[512,128]{1,0:T(8,128)(2,1)S(1)}, u32[]{:S(2)}, u32[]{:S(2)}) %collective-permute-start.8) | collective-permute-done | bytes 131104 | tf_op jit(solution)/shard_map/ppermute | solution.py:218
  72.6 7.7 %collective-permute-done.9.refs_2_ = bf16[512,128]{1,0:T(8,128)(2,1)S(1)} collective-permute-done((bf16[512,128]{1,0:T(8,128)(2,1)S(1)}, bf16[512,128]{1,0:T(8,128)(2,1)S(1)}, u32[]{:S(2)}, u32[]{:S(2)}) %collective-permute-start.9) | collective-permute-done | bytes 131104 | tf_op jit(solution)/shard_map/ppermute | solution.py:218
  80.3 3.5 %shard_map.85 = (bf16[128,2048]{1,0:T(8,128)(2,1)}, bf16[128,2048]{1,0:T(8,128)(2,1)}) custom-call(bf16[128,2048]{1,0:T(8,128)(2,1)S(1)} %copy-done, bf16[128,2048]{1,0:T(8,128)(2,1)S(1)} %copy-done.3, bf16[128,2048]{1,0:T(8,128)(2,1)S(1)} %copy-done.5, bf16[128,2048]{1,0:T(8,128)(2,1)S(1)} %copy-done.1, bf16[512,128]{1,0:T(8,128)(2,1)S(1)} %get-tuple-element.32.refs_0_, ...), custom_call_target="tpu_custom_call" | custom-call | flops 402653184 | bytes 5242880 | tf_op jit(solution)/shard_map/pallas_call | solution.py:227
  83.8 2.2 %shard_map.78 = (bf16[128,2048]{1,0:T(8,128)(2,1)}, bf16[128,2048]{1,0:T(8,128)(2,1)}) custom-call(bf16[128,2048]{1,0:T(8,128)(2,1)S(1)} %copy-done, bf16[128,2048]{1,0:T(8,128)(2,1)S(1)} %copy-done.3, bf16[128,2048]{1,0:T(8,128)(2,1)S(1)} %copy-done.5, bf16[128,2048]{1,0:T(8,128)(2,1)S(1)} %copy-done.1, bf16[16,128,128]{2,1,0:T(8,128)(2,1)S(1)} %get-tuple-element.21.sc_ref, ...), custom_call_target="tpu_custom_call" | custom-call | flops 268435456 | bytes 7077888 | tf_op jit(solution)/shard_map/pallas_call | solution.py:227
  (18 shorter events, 0.2 us)
Async XLA Ops:
  0.6 1.0 %copy-start.2 = (bf16[128,2048]{1,0:T(8,128)(2,1)S(1)}, bf16[128,2048]{1,0:T(8,128)(2,1)}, u32[]{:S(2)}) copy-start(bf16[128,2048]{1,0:T(8,128)(2,1)} %k_ref.7) | copy-start | bytes 1572868
  1.7 1.0 %copy-start.4 = (bf16[128,2048]{1,0:T(8,128)(2,1)S(1)}, bf16[128,2048]{1,0:T(8,128)(2,1)}, u32[]{:S(2)}) copy-start(bf16[128,2048]{1,0:T(8,128)(2,1)} %v_ref.7) | copy-start | bytes 1572868
  25.3 58.5 %all-to-all-start.1 = ((bf16[32,64,128]{2,1,0:T(8,128)(2,1)}), bf16[32,64,128]{2,1,0:T(8,128)(2,1)S(1)}, u32[]{:S(2)}, u32[]{:S(2)}) async-start(bf16[32,64,128]{2,1,0:T(8,128)(2,1)} %shard_map.77), calls=%async_computation.1 | async-start | bytes 1048576 | tf_op jit(solution)/shard_map/all_to_all | solution.py:214
  31.9 11.0 %collective-permute-start = (bf16[512,128]{1,0:T(8,128)(2,1)}, bf16[512,128]{1,0:T(8,128)(2,1)S(1)}, u32[]{:S(2)}, u32[]{:S(2)}) collective-permute-start(bf16[512,128]{1,0:T(8,128)(2,1)} %get-tuple-element.26), channel_id=1, source_target_pairs={{0,8},{8,0},{16,24},{24,16},{1,9},{9,1},{17,25},{25,17},{2,10},{10... | collective-permute-start | bytes 393224 | tf_op jit(solution)/shard_map/ppermute | solution.py:218
  33.7 19.8 %copy-start.6 = (bf16[512,128]{1,0:T(8,128)(2,1)S(1)}, bf16[512,128]{1,0:T(8,128)(2,1)}, u32[]{:S(2)}) copy-start(bf16[512,128]{1,0:T(8,128)(2,1)} %get-tuple-element.25.refs_0_.refs_2_) | copy-start | bytes 393220
  33.7 19.7 %collective-permute-start.1 = (bf16[512,128]{1,0:T(8,128)(2,1)}, bf16[512,128]{1,0:T(8,128)(2,1)S(1)}, u32[]{:S(2)}, u32[]{:S(2)}) collective-permute-start(bf16[512,128]{1,0:T(8,128)(2,1)} %get-tuple-element.27), channel_id=1, source_target_pairs={{0,16},{8,24},{16,0},{24,8},{1,17},{9,25},{17,1},{25,9},{2,18},{10... | collective-permute-start | bytes 393224 | tf_op jit(solution)/shard_map/ppermute | solution.py:218
  36.2 33.9 %copy-start.5 = (bf16[128,2048]{1,0:T(8,128)(2,1)S(1)}, bf16[128,2048]{1,0:T(8,128)(2,1)}, u32[]{:S(2)}) copy-start(bf16[128,2048]{1,0:T(8,128)(2,1)} %v_ref.7) | copy-start | bytes 1572868
  38.1 15.4 %collective-permute-start.2 = (bf16[512,128]{1,0:T(8,128)(2,1)}, bf16[512,128]{1,0:T(8,128)(2,1)S(1)}, u32[]{:S(2)}, u32[]{:S(2)}) collective-permute-start(bf16[512,128]{1,0:T(8,128)(2,1)} %shard_map.80), channel_id=1, source_target_pairs={{0,24},{8,16},{16,8},{24,0},{1,25},{9,17},{17,9},{25,1},{2,26},{10... | collective-permute-start | bytes 393224 | tf_op jit(solution)/shard_map/ppermute | solution.py:218
  53.5 16.5 %copy-start.3 = (bf16[128,2048]{1,0:T(8,128)(2,1)S(1)}, bf16[128,2048]{1,0:T(8,128)(2,1)}, u32[]{:S(2)}) copy-start(bf16[128,2048]{1,0:T(8,128)(2,1)} %k_ref.7) | copy-start | bytes 1572868
  53.6 1.3 %collective-permute-start.3 = (bf16[256,128]{1,0:T(8,128)(2,1)S(1)}, bf16[256,128]{1,0:T(8,128)(2,1)S(1)}, u32[]{:S(2)}, u32[]{:S(2)}) collective-permute-start(bf16[256,128]{1,0:T(8,128)(2,1)S(1)} %get-tuple-element.29), channel_id=1, source_target_pairs={{0,1},{1,0},{2,3},{3,2},{4,5},{5,4},{6,7},{7,6},{8,9},{9,8},{10,11... | collective-permute-start | bytes 196616 | tf_op jit(solution)/shard_map/ppermute | solution.py:218
  54.9 15.1 %copy-start = (bf16[128,2048]{1,0:T(8,128)(2,1)S(1)}, bf16[128,2048]{1,0:T(8,128)(2,1)}, u32[]{:S(2)}) copy-start(bf16[128,2048]{1,0:T(8,128)(2,1)} %q_ref.5) | copy-start | bytes 1572868
  54.9 15.1 %copy-start.1 = (bf16[128,2048]{1,0:T(8,128)(2,1)S(1)}, bf16[128,2048]{1,0:T(8,128)(2,1)}, u32[]{:S(2)}) copy-start(bf16[128,2048]{1,0:T(8,128)(2,1)} %g_ref.5) | copy-start | bytes 1572868
  55.0 4.3 %collective-permute-start.4 = (bf16[256,128]{1,0:T(8,128)(2,1)S(1)}, bf16[256,128]{1,0:T(8,128)(2,1)S(1)}, u32[]{:S(2)}, u32[]{:S(2)}) collective-permute-start(bf16[256,128]{1,0:T(8,128)(2,1)S(1)} %shard_map.82), channel_id=1, source_target_pairs={{0,2},{1,3},{2,0},{3,1},{4,6},{5,7},{6,4},{7,5},{8,10},{9,11},{10,... | collective-permute-start | bytes 196616 | tf_op jit(solution)/shard_map/ppermute | solution.py:218
  56.5 4.3 %collective-permute-start.5 = (bf16[256,128]{1,0:T(8,128)(2,1)S(1)}, bf16[256,128]{1,0:T(8,128)(2,1)S(1)}, u32[]{:S(2)}, u32[]{:S(2)}) collective-permute-start(bf16[256,128]{1,0:T(8,128)(2,1)S(1)} %shard_map.82), channel_id=1, source_target_pairs={{0,4},{1,5},{2,6},{3,7},{4,0},{5,1},{6,2},{7,3},{8,12},{9,13},{10,... | collective-permute-start | bytes 196616 | tf_op jit(solution)/shard_map/ppermute | solution.py:218
  58.0 5.2 %collective-permute-start.6 = (bf16[256,128]{1,0:T(8,128)(2,1)S(1)}, bf16[256,128]{1,0:T(8,128)(2,1)S(1)}, u32[]{:S(2)}, u32[]{:S(2)}) collective-permute-start(bf16[256,128]{1,0:T(8,128)(2,1)S(1)} %shard_map.82), channel_id=1, source_target_pairs={{0,6},{1,7},{2,4},{3,5},{4,2},{5,3},{6,0},{7,1},{8,14},{9,15},{10,... | collective-permute-start | bytes 196616 | tf_op jit(solution)/shard_map/ppermute | solution.py:218
  63.2 1.3 %collective-permute-start.7 = (bf16[256,128]{1,0:T(8,128)(2,1)S(1)}, bf16[256,128]{1,0:T(8,128)(2,1)S(1)}, u32[]{:S(2)}, u32[]{:S(2)}) collective-permute-start(bf16[256,128]{1,0:T(8,128)(2,1)S(1)} %get-tuple-element.31), channel_id=1, source_target_pairs={{0,1},{1,0},{2,3},{3,2},{4,5},{5,4},{6,7},{7,6},{8,9},{9,8},{10,11... | collective-permute-start | bytes 196616 | tf_op jit(solution)/shard_map/ppermute | solution.py:218
  64.7 7.9 %collective-permute-start.8 = (bf16[512,128]{1,0:T(8,128)(2,1)S(1)}, bf16[512,128]{1,0:T(8,128)(2,1)S(1)}, u32[]{:S(2)}, u32[]{:S(2)}) collective-permute-start(bf16[512,128]{1,0:T(8,128)(2,1)S(1)} %get-tuple-element.33), channel_id=1, source_target_pairs={{0,8},{8,0},{16,24},{24,16},{1,9},{9,1},{17,25},{25,17},{2,10},{10... | collective-permute-start | bytes 393224 | tf_op jit(solution)/shard_map/ppermute | solution.py:218
  67.6 12.7 %collective-permute-start.9 = (bf16[512,128]{1,0:T(8,128)(2,1)S(1)}, bf16[512,128]{1,0:T(8,128)(2,1)S(1)}, u32[]{:S(2)}, u32[]{:S(2)}) collective-permute-start(bf16[512,128]{1,0:T(8,128)(2,1)S(1)} %get-tuple-element.34), channel_id=1, source_target_pairs={{0,16},{8,24},{16,0},{24,8},{1,17},{9,25},{17,1},{25,9},{2,18},{10... | collective-permute-start | bytes 393224 | tf_op jit(solution)/shard_map/ppermute | solution.py:218
  67.6 12.7 %collective-permute-start.10 = (bf16[512,128]{1,0:T(8,128)(2,1)S(1)}, bf16[512,128]{1,0:T(8,128)(2,1)S(1)}, u32[]{:S(2)}, u32[]{:S(2)}) collective-permute-start(bf16[512,128]{1,0:T(8,128)(2,1)S(1)} %get-tuple-element.35), channel_id=1, source_target_pairs={{0,24},{8,16},{16,8},{24,0},{1,25},{9,17},{17,9},{25,1},{2,26},{10... | collective-permute-start | bytes 393224 | tf_op jit(solution)/shard_map/ppermute | solution.py:218

commit v6 on v5

--- a/solution.py
+++ b/solution.py
@@ -22,6 +22,10 @@
     if dims is None:
         return jnp.dot(a, b, preferred_element_type=F32)
     return lax.dot_general(a, b, dims, preferred_element_type=F32)
+
+
+def joint(a, b, c, d):
+    return dot(jnp.concatenate((a, b), 1), jnp.concatenate((c, d), 0))
 
 
 def coef_of(length):
@@ -175,7 +179,8 @@
             q, k, v = q_ref[:, cols], k_ref[:, cols], v_ref[:, cols]
             c = scaled_of(g_ref[:, cols], coef)
             fwd = f_ref[pl.ds(h * parts, parts)].reshape(DH, DH)
-            held[0, slot, :, to] = ((dot(sc_ref[h], v) + dot(q, fwd)) * coef).astype(BF16)
+            out = joint(sc_ref[h], q, v, fwd)
+            held[0, slot, :, to] = (out * coef).astype(BF16)
             ds = ds_ref[h] if h < ds_ref.shape[0] else masked(c, v, col <= row)
             held[1, slot, :, to] = (dot(ds, k) + dot(c, fwd, NT)).astype(BF16)
         width = HEADS // slots * DH
@@ -199,7 +204,7 @@
             q, k, v = q_ref[:, cols], k_ref[:, cols], v_ref[:, cols]
             c = scaled_of(g_ref[:, cols], coef)
             back = b_refs[g][pl.ds(h * DH, DH), :]
-            dk = dot(masked(v, c, col >= row), q) + dot(v, back)
+            dk = joint(masked(v, c, col >= row), v, q, back)
             held[0, slot, :, to] = dk.astype(BF16)
             dv = dot(masked(k, q, col >= row), c) + dot(k, back, NT)
             held[1, slot, :, to] = dv.astype(BF16)

time: 86.3 us -> 85 us (0.985)
  Pallas kernels: 12.3 us -> 11 us
    pallas_call x11, Pallas kernels: 12.3 us -> 11 us  [call(): pl.pallas_call(kernel, out_shape=out, in_specs=ins, out_specs=outs, scrat...]
  transfers between devices with their start and end apart: 12 -> 12, of which waited for: 9 -> 9; matrix products, arithmetic and copies ran while one was open for 0% -> 0% of each run, Pallas kernels for 10% -> 9%
where the time goes in v6:
time: 85 us; the launch traced here: 84.6 us
  waiting for transfers between devices  31.8 us (37%)
  blocking collectives  21.4 us (25%)
  starting transfers between devices  17.7 us (21%)
  Pallas kernels  11 us (13%)
  local copies, waits for them, and re-layouts  2.1 us (2%)
    ppermute x11, waiting for transfers between devices, swap(): lax.ppermute(x, axis, [(i, i ^ k) for i in range(lax.axis_size(axis))])  31.8 us
    all_to_all x1, blocking collectives, exchange(): return lax.all_to_all(x, AXES, split_axis=0, concat_axis=0, tiled=True)  21.4 us
    ppermute x11, starting transfers between devices, swap(): lax.ppermute(x, axis, [(i, i ^ k) for i in range(lax.axis_size(axis))])  13.5 us
    pallas_call x11, Pallas kernels, call(): pl.pallas_call(kernel, out_shape=out, in_specs=ins, out_specs=outs, scrat...  11 us
    all_to_all x1, starting transfers between devices, exchange(): return lax.all_to_all(x, AXES, split_axis=0, concat_axis=0, tiled=True)  4.17 us
    unnamed x14, local copies, waits for them, and re-layouts  2.1 us
  transfers between devices with their start and end apart: 12, of which 9 were waited for; matrix products, arithmetic and copies ran while one was open for 0% of the time, Pallas kernels for 9%

profile of v6, /device:TPU:0, one launch (start us, length us, event | category | flops | bytes accessed | tf_op | source)
XLA Modules:
  0.0 84.6 jit_solution(12901667201526692640)
XLA Ops:
  0.6 1.0 %copy-done.2 = bf16[128,2048]{1,0:T(8,128)(2,1)S(1)} copy-done((bf16[128,2048]{1,0:T(8,128)(2,1)S(1)}, bf16[128,2048]{1,0:T(8,128)(2,1)}, u32[]{:S(2)}) %copy-start.2) | copy-done | bytes 524312
  1.7 1.0 %copy-done.4 = bf16[128,2048]{1,0:T(8,128)(2,1)S(1)} copy-done((bf16[128,2048]{1,0:T(8,128)(2,1)S(1)}, bf16[128,2048]{1,0:T(8,128)(2,1)}, u32[]{:S(2)}) %copy-start.4) | copy-done | bytes 524312
  2.7 0.3 shard_map.76
  3.1 21.4 %all_to_all.10.in_ref = bf16[32,64,128]{2,1,0:T(8,128)(2,1)S(1)} all-to-all(bf16[32,64,128]{2,1,0:T(8,128)(2,1)S(1)} %shard_map.76), channel_id=1, replica_groups=mesh['head'=4,'span'=8] {'span','head'}, dimensions={0} | all-to-all | bytes 1048576 | tf_op jit(solution)/shard_map/all_to_all | solution.py:219
  24.4 0.9 %shard_map.77 = bf16[32,64,128]{2,1,0:T(8,128)(2,1)} custom-call(bf16[32,64,128]{2,1,0:T(8,128)(2,1)S(1)} %all_to_all.10.in_ref), custom_call_target="tpu_custom_call" | custom-call | bytes 1048576 | tf_op jit(solution)/shard_map/pallas_call | solution.py:232
  25.3 4.2 %all-to-all-start.1 = ((bf16[32,64,128]{2,1,0:T(8,128)(2,1)}), bf16[32,64,128]{2,1,0:T(8,128)(2,1)S(1)}, u32[]{:S(2)}, u32[]{:S(2)}) async-start(bf16[32,64,128]{2,1,0:T(8,128)(2,1)} %shard_map.77), calls=%async_computation.1 | async-start | bytes 1048576 | tf_op jit(solution)/shard_map/all_to_all | solution.py:219
  29.5 2.4 %shard_map.79 = (bf16[512,128]{1,0:T(8,128)(2,1)}, bf16[512,128]{1,0:T(8,128)(2,1)}, bf16[512,128]{1,0:T(8,128)(2,1)}) custom-call(bf16[128,2048]{1,0:T(8,128)(2,1)} %q_ref.5, bf16[128,2048]{1,0:T(8,128)(2,1)} %g_ref.5), custom_call_target="tpu_custom_call" | custom-call | flops 50331648 | bytes 2097152 | tf_op jit(solution)/shard_map/pallas_call | solution.py:232
  31.9 1.8 %collective-permute-start = (bf16[512,128]{1,0:T(8,128)(2,1)}, bf16[512,128]{1,0:T(8,128)(2,1)S(1)}, u32[]{:S(2)}, u32[]{:S(2)}) collective-permute-start(bf16[512,128]{1,0:T(8,128)(2,1)} %get-tuple-element.26), channel_id=1, source_target_pairs={{0,8},{8,0},{16,24},{24,16},{1,9},{9,1},{17,25},{25,17},{2,10},{10... | collective-permute-start | bytes 393224 | tf_op jit(solution)/shard_map/ppermute | solution.py:223
  33.7 2.4 %collective-permute-start.1 = (bf16[512,128]{1,0:T(8,128)(2,1)}, bf16[512,128]{1,0:T(8,128)(2,1)S(1)}, u32[]{:S(2)}, u32[]{:S(2)}) collective-permute-start(bf16[512,128]{1,0:T(8,128)(2,1)} %get-tuple-element.27), channel_id=1, source_target_pairs={{0,16},{8,24},{16,0},{24,8},{1,17},{9,25},{17,1},{25,9},{2,18},{10... | collective-permute-start | bytes 393224 | tf_op jit(solution)/shard_map/ppermute | solution.py:223
  36.2 1.9 %shard_map.80 = bf16[512,128]{1,0:T(8,128)(2,1)} custom-call(bf16[128,2048]{1,0:T(8,128)(2,1)} %q_ref.5, bf16[128,2048]{1,0:T(8,128)(2,1)} %g_ref.5), custom_call_target="tpu_custom_call" | custom-call | flops 16777216 | bytes 2097152 | tf_op jit(solution)/shard_map/pallas_call | solution.py:232
  38.1 0.3 collective-permute-start.2
  38.4 4.5 %collective-permute-done.refs_1_.refs_3_ = bf16[512,128]{1,0:T(8,128)(2,1)S(1)} collective-permute-done((bf16[512,128]{1,0:T(8,128)(2,1)}, bf16[512,128]{1,0:T(8,128)(2,1)S(1)}, u32[]{:S(2)}, u32[]{:S(2)}) %collective-permute-start) | collective-permute-done | bytes 131104 | tf_op jit(solution)/shard_map/ppermute | solution.py:223
  42.9 10.6 %collective-permute-done.1.refs_2_.refs_4_ = bf16[512,128]{1,0:T(8,128)(2,1)S(1)} collective-permute-done((bf16[512,128]{1,0:T(8,128)(2,1)}, bf16[512,128]{1,0:T(8,128)(2,1)S(1)}, u32[]{:S(2)}, u32[]{:S(2)}) %collective-permute-start.1) | collective-permute-done | bytes 131104 | tf_op jit(solution)/shard_map/ppermute | solution.py:223
  53.5 0.1 shard_map.81
  53.6 0.1 collective-permute-start.3
  53.7 1.2 %collective-permute-done.3.b_ref.got_ref = bf16[256,128]{1,0:T(8,128)(2,1)S(1)} collective-permute-done((bf16[256,128]{1,0:T(8,128)(2,1)S(1)}, bf16[256,128]{1,0:T(8,128)(2,1)S(1)}, u32[]{:S(2)}, u32[]{:S(2)}) %collective-permute-start.3) | collective-permute-done | bytes 65568 | tf_op jit(solution)/shard_map/ppermute | solution.py:223
  55.0 1.5 %collective-permute-start.4 = (bf16[256,128]{1,0:T(8,128)(2,1)S(1)}, bf16[256,128]{1,0:T(8,128)(2,1)S(1)}, u32[]{:S(2)}, u32[]{:S(2)}) collective-permute-start(bf16[256,128]{1,0:T(8,128)(2,1)S(1)} %shard_map.82), channel_id=1, source_target_pairs={{0,2},{1,3},{2,0},{3,1},{4,6},{5,7},{6,4},{7,5},{8,10},{9,11},{10,... | collective-permute-start | bytes 196616 | tf_op jit(solution)/shard_map/ppermute | solution.py:223
  56.5 1.5 %collective-permute-start.5 = (bf16[256,128]{1,0:T(8,128)(2,1)S(1)}, bf16[256,128]{1,0:T(8,128)(2,1)S(1)}, u32[]{:S(2)}, u32[]{:S(2)}) collective-permute-start(bf16[256,128]{1,0:T(8,128)(2,1)S(1)} %shard_map.82), channel_id=1, source_target_pairs={{0,4},{1,5},{2,6},{3,7},{4,0},{5,1},{6,2},{7,3},{8,12},{9,13},{10,... | collective-permute-start | bytes 196616 | tf_op jit(solution)/shard_map/ppermute | solution.py:223
  58.0 0.5 collective-permute-start.6
  58.5 0.8 collective-permute-done.4.refs_0_
  59.3 1.5 %collective-permute-done.5.refs_1_ = bf16[256,128]{1,0:T(8,128)(2,1)S(1)} collective-permute-done((bf16[256,128]{1,0:T(8,128)(2,1)S(1)}, bf16[256,128]{1,0:T(8,128)(2,1)S(1)}, u32[]{:S(2)}, u32[]{:S(2)}) %collective-permute-start.5) | collective-permute-done | bytes 65568 | tf_op jit(solution)/shard_map/ppermute | solution.py:223
  60.8 2.4 %collective-permute-done.6.refs_2_ = bf16[256,128]{1,0:T(8,128)(2,1)S(1)} collective-permute-done((bf16[256,128]{1,0:T(8,128)(2,1)S(1)}, bf16[256,128]{1,0:T(8,128)(2,1)S(1)}, u32[]{:S(2)}, u32[]{:S(2)}) %collective-permute-start.6) | collective-permute-done | bytes 65568 | tf_op jit(solution)/shard_map/ppermute | solution.py:223
  63.1 0.1 shard_map.83
  63.3 1.2 %collective-permute-done.7.refs_1_ = bf16[256,128]{1,0:T(8,128)(2,1)S(1)} collective-permute-done((bf16[256,128]{1,0:T(8,128)(2,1)S(1)}, bf16[256,128]{1,0:T(8,128)(2,1)S(1)}, u32[]{:S(2)}, u32[]{:S(2)}) %collective-permute-start.7) | collective-permute-done | bytes 65568 | tf_op jit(solution)/shard_map/ppermute | solution.py:223
  64.6 0.2 shard_map.84
  64.7 2.8 %collective-permute-start.8 = (bf16[512,128]{1,0:T(8,128)(2,1)S(1)}, bf16[512,128]{1,0:T(8,128)(2,1)S(1)}, u32[]{:S(2)}, u32[]{:S(2)}) collective-permute-start(bf16[512,128]{1,0:T(8,128)(2,1)S(1)} %get-tuple-element.33), channel_id=1, source_target_pairs={{0,8},{8,0},{16,24},{24,16},{1,9},{9,1},{17,25},{25,17},{2,10},{10... | collective-permute-start | bytes 393224 | tf_op jit(solution)/shard_map/ppermute | solution.py:223
  67.6 2.4 %collective-permute-start.10 = (bf16[512,128]{1,0:T(8,128)(2,1)S(1)}, bf16[512,128]{1,0:T(8,128)(2,1)S(1)}, u32[]{:S(2)}, u32[]{:S(2)}) collective-permute-start(bf16[512,128]{1,0:T(8,128)(2,1)S(1)} %get-tuple-element.35), channel_id=1, source_target_pairs={{0,24},{8,16},{16,8},{24,0},{1,25},{9,17},{17,9},{25,1},{2,26},{10... | collective-permute-start | bytes 393224 | tf_op jit(solution)/shard_map/ppermute | solution.py:223
  70.0 0.8 shard_map.75
  70.8 1.8 %collective-permute-done.8.refs_1_ = bf16[512,128]{1,0:T(8,128)(2,1)S(1)} collective-permute-done((bf16[512,128]{1,0:T(8,128)(2,1)S(1)}, bf16[512,128]{1,0:T(8,128)(2,1)S(1)}, u32[]{:S(2)}, u32[]{:S(2)}) %collective-permute-start.8) | collective-permute-done | bytes 131104 | tf_op jit(solution)/shard_map/ppermute | solution.py:223
  72.6 7.7 %collective-permute-done.9.refs_2_ = bf16[512,128]{1,0:T(8,128)(2,1)S(1)} collective-permute-done((bf16[512,128]{1,0:T(8,128)(2,1)S(1)}, bf16[512,128]{1,0:T(8,128)(2,1)S(1)}, u32[]{:S(2)}, u32[]{:S(2)}) %collective-permute-start.9) | collective-permute-done | bytes 131104 | tf_op jit(solution)/shard_map/ppermute | solution.py:223
  80.3 2.6 %shard_map.85 = (bf16[128,2048]{1,0:T(8,128)(2,1)}, bf16[128,2048]{1,0:T(8,128)(2,1)}) custom-call(bf16[128,2048]{1,0:T(8,128)(2,1)S(1)} %copy-done, bf16[128,2048]{1,0:T(8,128)(2,1)S(1)} %copy-done.3, bf16[128,2048]{1,0:T(8,128)(2,1)S(1)} %copy-done.5, bf16[128,2048]{1,0:T(8,128)(2,1)S(1)} %copy-done.1, bf16[512,128]{1,0:T(8,128)(2,1)S(1)} %get-tuple-element.32.refs_0_, ...), custom_call_target="tpu_custom_call" | custom-call | flops 402653184 | bytes 5242880 | tf_op jit(solution)/shard_map/pallas_call | solution.py:232
  82.9 1.7 %shard_map.78 = (bf16[128,2048]{1,0:T(8,128)(2,1)}, bf16[128,2048]{1,0:T(8,128)(2,1)}) custom-call(bf16[128,2048]{1,0:T(8,128)(2,1)S(1)} %copy-done, bf16[128,2048]{1,0:T(8,128)(2,1)S(1)} %copy-done.3, bf16[128,2048]{1,0:T(8,128)(2,1)S(1)} %copy-done.5, bf16[128,2048]{1,0:T(8,128)(2,1)S(1)} %copy-done.1, bf16[16,128,128]{2,1,0:T(8,128)(2,1)S(1)} %get-tuple-element.21.sc_ref, ...), custom_call_target="tpu_custom_call" | custom-call | flops 268435456 | bytes 7077888 | tf_op jit(solution)/shard_map/pallas_call | solution.py:232
  (18 shorter events, 0.2 us)
Async XLA Ops:
  0.6 1.0 %copy-start.2 = (bf16[128,2048]{1,0:T(8,128)(2,1)S(1)}, bf16[128,2048]{1,0:T(8,128)(2,1)}, u32[]{:S(2)}) copy-start(bf16[128,2048]{1,0:T(8,128)(2,1)} %k_ref.7) | copy-start | bytes 1572868
  1.7 1.0 %copy-start.4 = (bf16[128,2048]{1,0:T(8,128)(2,1)S(1)}, bf16[128,2048]{1,0:T(8,128)(2,1)}, u32[]{:S(2)}) copy-start(bf16[128,2048]{1,0:T(8,128)(2,1)} %v_ref.7) | copy-start | bytes 1572868
  25.3 57.6 %all-to-all-start.1 = ((bf16[32,64,128]{2,1,0:T(8,128)(2,1)}), bf16[32,64,128]{2,1,0:T(8,128)(2,1)S(1)}, u32[]{:S(2)}, u32[]{:S(2)}) async-start(bf16[32,64,128]{2,1,0:T(8,128)(2,1)} %shard_map.77), calls=%async_computation.1 | async-start | bytes 1048576 | tf_op jit(solution)/shard_map/all_to_all | solution.py:219
  31.9 11.0 %collective-permute-start = (bf16[512,128]{1,0:T(8,128)(2,1)}, bf16[512,128]{1,0:T(8,128)(2,1)S(1)}, u32[]{:S(2)}, u32[]{:S(2)}) collective-permute-start(bf16[512,128]{1,0:T(8,128)(2,1)} %get-tuple-element.26), channel_id=1, source_target_pairs={{0,8},{8,0},{16,24},{24,16},{1,9},{9,1},{17,25},{25,17},{2,10},{10... | collective-permute-start | bytes 393224 | tf_op jit(solution)/shard_map/ppermute | solution.py:223
  33.7 19.8 %copy-start.6 = (bf16[512,128]{1,0:T(8,128)(2,1)S(1)}, bf16[512,128]{1,0:T(8,128)(2,1)}, u32[]{:S(2)}) copy-start(bf16[512,128]{1,0:T(8,128)(2,1)} %get-tuple-element.25.refs_0_.refs_2_) | copy-start | bytes 393220
  33.7 19.7 %collective-permute-start.1 = (bf16[512,128]{1,0:T(8,128)(2,1)}, bf16[512,128]{1,0:T(8,128)(2,1)S(1)}, u32[]{:S(2)}, u32[]{:S(2)}) collective-permute-start(bf16[512,128]{1,0:T(8,128)(2,1)} %get-tuple-element.27), channel_id=1, source_target_pairs={{0,16},{8,24},{16,0},{24,8},{1,17},{9,25},{17,1},{25,9},{2,18},{10... | collective-permute-start | bytes 393224 | tf_op jit(solution)/shard_map/ppermute | solution.py:223
  36.2 33.9 %copy-start.5 = (bf16[128,2048]{1,0:T(8,128)(2,1)S(1)}, bf16[128,2048]{1,0:T(8,128)(2,1)}, u32[]{:S(2)}) copy-start(bf16[128,2048]{1,0:T(8,128)(2,1)} %v_ref.7) | copy-start | bytes 1572868
  38.1 15.4 %collective-permute-start.2 = (bf16[512,128]{1,0:T(8,128)(2,1)}, bf16[512,128]{1,0:T(8,128)(2,1)S(1)}, u32[]{:S(2)}, u32[]{:S(2)}) collective-permute-start(bf16[512,128]{1,0:T(8,128)(2,1)} %shard_map.80), channel_id=1, source_target_pairs={{0,24},{8,16},{16,8},{24,0},{1,25},{9,17},{17,9},{25,1},{2,26},{10... | collective-permute-start | bytes 393224 | tf_op jit(solution)/shard_map/ppermute | solution.py:223
  53.5 16.5 %copy-start.3 = (bf16[128,2048]{1,0:T(8,128)(2,1)S(1)}, bf16[128,2048]{1,0:T(8,128)(2,1)}, u32[]{:S(2)}) copy-start(bf16[128,2048]{1,0:T(8,128)(2,1)} %k_ref.7) | copy-start | bytes 1572868
  53.6 1.3 %collective-permute-start.3 = (bf16[256,128]{1,0:T(8,128)(2,1)S(1)}, bf16[256,128]{1,0:T(8,128)(2,1)S(1)}, u32[]{:S(2)}, u32[]{:S(2)}) collective-permute-start(bf16[256,128]{1,0:T(8,128)(2,1)S(1)} %get-tuple-element.29), channel_id=1, source_target_pairs={{0,1},{1,0},{2,3},{3,2},{4,5},{5,4},{6,7},{7,6},{8,9},{9,8},{10,11... | collective-permute-start | bytes 196616 | tf_op jit(solution)/shard_map/ppermute | solution.py:223
  54.9 15.1 %copy-start = (bf16[128,2048]{1,0:T(8,128)(2,1)S(1)}, bf16[128,2048]{1,0:T(8,128)(2,1)}, u32[]{:S(2)}) copy-start(bf16[128,2048]{1,0:T(8,128)(2,1)} %q_ref.5) | copy-start | bytes 1572868
  54.9 15.1 %copy-start.1 = (bf16[128,2048]{1,0:T(8,128)(2,1)S(1)}, bf16[128,2048]{1,0:T(8,128)(2,1)}, u32[]{:S(2)}) copy-start(bf16[128,2048]{1,0:T(8,128)(2,1)} %g_ref.5) | copy-start | bytes 1572868
  55.0 4.3 %collective-permute-start.4 = (bf16[256,128]{1,0:T(8,128)(2,1)S(1)}, bf16[256,128]{1,0:T(8,128)(2,1)S(1)}, u32[]{:S(2)}, u32[]{:S(2)}) collective-permute-start(bf16[256,128]{1,0:T(8,128)(2,1)S(1)} %shard_map.82), channel_id=1, source_target_pairs={{0,2},{1,3},{2,0},{3,1},{4,6},{5,7},{6,4},{7,5},{8,10},{9,11},{10,... | collective-permute-start | bytes 196616 | tf_op jit(solution)/shard_map/ppermute | solution.py:223
  56.5 4.3 %collective-permute-start.5 = (bf16[256,128]{1,0:T(8,128)(2,1)S(1)}, bf16[256,128]{1,0:T(8,128)(2,1)S(1)}, u32[]{:S(2)}, u32[]{:S(2)}) collective-permute-start(bf16[256,128]{1,0:T(8,128)(2,1)S(1)} %shard_map.82), channel_id=1, source_target_pairs={{0,4},{1,5},{2,6},{3,7},{4,0},{5,1},{6,2},{7,3},{8,12},{9,13},{10,... | collective-permute-start | bytes 196616 | tf_op jit(solution)/shard_map/ppermute | solution.py:223
  58.0 5.2 %collective-permute-start.6 = (bf16[256,128]{1,0:T(8,128)(2,1)S(1)}, bf16[256,128]{1,0:T(8,128)(2,1)S(1)}, u32[]{:S(2)}, u32[]{:S(2)}) collective-permute-start(bf16[256,128]{1,0:T(8,128)(2,1)S(1)} %shard_map.82), channel_id=1, source_target_pairs={{0,6},{1,7},{2,4},{3,5},{4,2},{5,3},{6,0},{7,1},{8,14},{9,15},{10,... | collective-permute-start | bytes 196616 | tf_op jit(solution)/shard_map/ppermute | solution.py:223
  63.2 1.3 %collective-permute-start.7 = (bf16[256,128]{1,0:T(8,128)(2,1)S(1)}, bf16[256,128]{1,0:T(8,128)(2,1)S(1)}, u32[]{:S(2)}, u32[]{:S(2)}) collective-permute-start(bf16[256,128]{1,0:T(8,128)(2,1)S(1)} %get-tuple-element.31), channel_id=1, source_target_pairs={{0,1},{1,0},{2,3},{3,2},{4,5},{5,4},{6,7},{7,6},{8,9},{9,8},{10,11... | collective-permute-start | bytes 196616 | tf_op jit(solution)/shard_map/ppermute | solution.py:223
  64.7 7.9 %collective-permute-start.8 = (bf16[512,128]{1,0:T(8,128)(2,1)S(1)}, bf16[512,128]{1,0:T(8,128)(2,1)S(1)}, u32[]{:S(2)}, u32[]{:S(2)}) collective-permute-start(bf16[512,128]{1,0:T(8,128)(2,1)S(1)} %get-tuple-element.33), channel_id=1, source_target_pairs={{0,8},{8,0},{16,24},{24,16},{1,9},{9,1},{17,25},{25,17},{2,10},{10... | collective-permute-start | bytes 393224 | tf_op jit(solution)/shard_map/ppermute | solution.py:223
  67.6 12.7 %collective-permute-start.9 = (bf16[512,128]{1,0:T(8,128)(2,1)S(1)}, bf16[512,128]{1,0:T(8,128)(2,1)S(1)}, u32[]{:S(2)}, u32[]{:S(2)}) collective-permute-start(bf16[512,128]{1,0:T(8,128)(2,1)S(1)} %get-tuple-element.34), channel_id=1, source_target_pairs={{0,16},{8,24},{16,0},{24,8},{1,17},{9,25},{17,1},{25,9},{2,18},{10... | collective-permute-start | bytes 393224 | tf_op jit(solution)/shard_map/ppermute | solution.py:223
  67.6 12.7 %collective-permute-start.10 = (bf16[512,128]{1,0:T(8,128)(2,1)S(1)}, bf16[512,128]{1,0:T(8,128)(2,1)S(1)}, u32[]{:S(2)}, u32[]{:S(2)}) collective-permute-start(bf16[512,128]{1,0:T(8,128)(2,1)S(1)} %get-tuple-element.35), channel_id=1, source_target_pairs={{0,24},{8,16},{16,8},{24,0},{1,25},{9,17},{17,9},{25,1},{2,26},{10... | collective-permute-start | bytes 393224 | tf_op jit(solution)/shard_map/ppermute | solution.py:223

commit v7 on v6

--- a/solution.py
+++ b/solution.py
@@ -15,7 +15,7 @@
 AXES = ("span", "head")
 VMEM = 20 * 2**20
 KEPT = 12
-FIRST = ((3,), (2, 1, 0))
+FIRST = ((3, 2), (1, 0))
 
 
 def dot(a, b, dims=None):
@@ -76,8 +76,14 @@
             cols = pl.ds(h * DH, DH)
             scaled = scaled_of(g_ref[i, :, cols], coef)
             t_ref[i, cols, :] = dot(scaled, q_ref[i, :, cols], TN).astype(BF16)
-        stores.append(pltpu.make_async_copy(t_ref.at[i], t_hbms[i], out_sems.at[i]))
-        stores[-1].start()
+            if h % 2 == 1:
+                done = pl.ds((h - 1) * DH, 2 * DH)
+                stores.append(
+                    pltpu.make_async_copy(
+                        t_ref.at[i, done], t_hbms[i].at[done], out_sems.at[i, h // 2]
+                    )
+                )
+                stores[-1].start()
     for copy in stores:
         copy.wait()
 
@@ -269,7 +275,7 @@
                 pltpu.VMEM((len(order), length, feat // groups), BF16),
                 pltpu.VMEM((len(order), feat // groups, DH), BF16),
                 pltpu.SemaphoreType.DMA((2, len(order))),
-                pltpu.SemaphoreType.DMA((len(order),)),
+                pltpu.SemaphoreType.DMA((len(order), HEADS // groups // 2)),
             ],
         )
         for k, piece in zip(order, outs):

time: 85 us -> 85 us (level)
  no operation moved by 1% of the time
where the time goes in v7:
time: 85 us; the launch traced here: 84.6 us
  waiting for transfers between devices  31.8 us (37%)
  blocking collectives  21.4 us (25%)
  starting transfers between devices  17.7 us (21%)
  Pallas kernels  10.9 us (13%)
  local copies, waits for them, and re-layouts  2.1 us (2%)
    ppermute x11, waiting for transfers between devices, swap(): lax.ppermute(x, axis, [(i, i ^ k) for i in range(lax.axis_size(axis))])  31.8 us
    all_to_all x1, blocking collectives, exchange(): return lax.all_to_all(x, AXES, split_axis=0, concat_axis=0, tiled=True)  21.4 us
    ppermute x11, starting transfers between devices, swap(): lax.ppermute(x, axis, [(i, i ^ k) for i in range(lax.axis_size(axis))])  13.5 us
    pallas_call x11, Pallas kernels, call(): pl.pallas_call(kernel, out_shape=out, in_specs=ins, out_specs=outs, scrat...  10.9 us
    all_to_all x1, starting transfers between devices, exchange(): return lax.all_to_all(x, AXES, split_axis=0, concat_axis=0, tiled=True)  4.17 us
    unnamed x14, local copies, waits for them, and re-layouts  2.1 us
  transfers between devices with their start and end apart: 12, of which 9 were waited for; matrix products, arithmetic and copies ran while one was open for 0% of the time, Pallas kernels for 9%

profile of v7, /device:TPU:0, one launch (start us, length us, event | category | flops | bytes accessed | tf_op | source)
XLA Modules:
  0.0 84.6 jit_solution(11592302921001489506)
XLA Ops:
  0.6 1.0 %copy-done.2 = bf16[128,2048]{1,0:T(8,128)(2,1)S(1)} copy-done((bf16[128,2048]{1,0:T(8,128)(2,1)S(1)}, bf16[128,2048]{1,0:T(8,128)(2,1)}, u32[]{:S(2)}) %copy-start.2) | copy-done | bytes 524312
  1.7 1.0 %copy-done.4 = bf16[128,2048]{1,0:T(8,128)(2,1)S(1)} copy-done((bf16[128,2048]{1,0:T(8,128)(2,1)S(1)}, bf16[128,2048]{1,0:T(8,128)(2,1)}, u32[]{:S(2)}) %copy-start.4) | copy-done | bytes 524312
  2.7 0.3 shard_map.76
  3.1 21.4 %all_to_all.10.in_ref = bf16[32,64,128]{2,1,0:T(8,128)(2,1)S(1)} all-to-all(bf16[32,64,128]{2,1,0:T(8,128)(2,1)S(1)} %shard_map.76), channel_id=1, replica_groups=mesh['head'=4,'span'=8] {'span','head'}, dimensions={0} | all-to-all | bytes 1048576 | tf_op jit(solution)/shard_map/all_to_all | solution.py:225
  24.4 0.9 %shard_map.77 = bf16[32,64,128]{2,1,0:T(8,128)(2,1)} custom-call(bf16[32,64,128]{2,1,0:T(8,128)(2,1)S(1)} %all_to_all.10.in_ref), custom_call_target="tpu_custom_call" | custom-call | bytes 1048576 | tf_op jit(solution)/shard_map/pallas_call | solution.py:238
  25.3 4.2 %all-to-all-start.1 = ((bf16[32,64,128]{2,1,0:T(8,128)(2,1)}), bf16[32,64,128]{2,1,0:T(8,128)(2,1)S(1)}, u32[]{:S(2)}, u32[]{:S(2)}) async-start(bf16[32,64,128]{2,1,0:T(8,128)(2,1)} %shard_map.77), calls=%async_computation.1 | async-start | bytes 1048576 | tf_op jit(solution)/shard_map/all_to_all | solution.py:225
  29.5 2.1 %shard_map.79 = (bf16[512,128]{1,0:T(8,128)(2,1)}, bf16[512,128]{1,0:T(8,128)(2,1)}) custom-call(bf16[128,2048]{1,0:T(8,128)(2,1)} %q_ref.5, bf16[128,2048]{1,0:T(8,128)(2,1)} %g_ref.5), custom_call_target="tpu_custom_call" | custom-call | flops 33554432 | bytes 2097152 | tf_op jit(solution)/shard_map/pallas_call | solution.py:238
  31.7 1.8 %collective-permute-start = (bf16[512,128]{1,0:T(8,128)(2,1)}, bf16[512,128]{1,0:T(8,128)(2,1)S(1)}, u32[]{:S(2)}, u32[]{:S(2)}) collective-permute-start(bf16[512,128]{1,0:T(8,128)(2,1)} %get-tuple-element.27), channel_id=1, source_target_pairs={{0,8},{8,0},{16,24},{24,16},{1,9},{9,1},{17,25},{25,17},{2,10},{10... | collective-permute-start | bytes 393224 | tf_op jit(solution)/shard_map/ppermute | solution.py:229
  33.5 2.2 %shard_map.80 = (bf16[512,128]{1,0:T(8,128)(2,1)}, bf16[512,128]{1,0:T(8,128)(2,1)}) custom-call(bf16[128,2048]{1,0:T(8,128)(2,1)} %q_ref.5, bf16[128,2048]{1,0:T(8,128)(2,1)} %g_ref.5), custom_call_target="tpu_custom_call" | custom-call | flops 33554432 | bytes 2097152 | tf_op jit(solution)/shard_map/pallas_call | solution.py:238
  35.7 2.5 %collective-permute-start.1 = (bf16[512,128]{1,0:T(8,128)(2,1)}, bf16[512,128]{1,0:T(8,128)(2,1)S(1)}, u32[]{:S(2)}, u32[]{:S(2)}) collective-permute-start(bf16[512,128]{1,0:T(8,128)(2,1)} %get-tuple-element.28), channel_id=1, source_target_pairs={{0,16},{8,24},{16,0},{24,8},{1,17},{9,25},{17,1},{25,9},{2,18},{10... | collective-permute-start | bytes 393224 | tf_op jit(solution)/shard_map/ppermute | solution.py:229
  38.2 0.2 collective-permute-start.2
  38.4 4.5 %collective-permute-done.refs_1_.refs_3_ = bf16[512,128]{1,0:T(8,128)(2,1)S(1)} collective-permute-done((bf16[512,128]{1,0:T(8,128)(2,1)}, bf16[512,128]{1,0:T(8,128)(2,1)S(1)}, u32[]{:S(2)}, u32[]{:S(2)}) %collective-permute-start) | collective-permute-done | bytes 131104 | tf_op jit(solution)/shard_map/ppermute | solution.py:229
  42.9 10.6 %collective-permute-done.1.refs_2_.refs_4_ = bf16[512,128]{1,0:T(8,128)(2,1)S(1)} collective-permute-done((bf16[512,128]{1,0:T(8,128)(2,1)}, bf16[512,128]{1,0:T(8,128)(2,1)S(1)}, u32[]{:S(2)}, u32[]{:S(2)}) %collective-permute-start.1) | collective-permute-done | bytes 131104 | tf_op jit(solution)/shard_map/ppermute | solution.py:229
  53.5 0.1 shard_map.81
  53.6 0.1 collective-permute-start.3
  53.7 1.2 %collective-permute-done.3.b_ref.got_ref = bf16[256,128]{1,0:T(8,128)(2,1)S(1)} collective-permute-done((bf16[256,128]{1,0:T(8,128)(2,1)S(1)}, bf16[256,128]{1,0:T(8,128)(2,1)S(1)}, u32[]{:S(2)}, u32[]{:S(2)}) %collective-permute-start.3) | collective-permute-done | bytes 65568 | tf_op jit(solution)/shard_map/ppermute | solution.py:229
  55.0 1.5 %collective-permute-start.4 = (bf16[256,128]{1,0:T(8,128)(2,1)S(1)}, bf16[256,128]{1,0:T(8,128)(2,1)S(1)}, u32[]{:S(2)}, u32[]{:S(2)}) collective-permute-start(bf16[256,128]{1,0:T(8,128)(2,1)S(1)} %shard_map.82), channel_id=1, source_target_pairs={{0,2},{1,3},{2,0},{3,1},{4,6},{5,7},{6,4},{7,5},{8,10},{9,11},{10,... | collective-permute-start | bytes 196616 | tf_op jit(solution)/shard_map/ppermute | solution.py:229
  56.5 1.5 %collective-permute-start.5 = (bf16[256,128]{1,0:T(8,128)(2,1)S(1)}, bf16[256,128]{1,0:T(8,128)(2,1)S(1)}, u32[]{:S(2)}, u32[]{:S(2)}) collective-permute-start(bf16[256,128]{1,0:T(8,128)(2,1)S(1)} %shard_map.82), channel_id=1, source_target_pairs={{0,4},{1,5},{2,6},{3,7},{4,0},{5,1},{6,2},{7,3},{8,12},{9,13},{10,... | collective-permute-start | bytes 196616 | tf_op jit(solution)/shard_map/ppermute | solution.py:229
  58.0 0.5 collective-permute-start.6
  58.5 0.8 collective-permute-done.4.refs_0_
  59.3 1.5 %collective-permute-done.5.refs_1_ = bf16[256,128]{1,0:T(8,128)(2,1)S(1)} collective-permute-done((bf16[256,128]{1,0:T(8,128)(2,1)S(1)}, bf16[256,128]{1,0:T(8,128)(2,1)S(1)}, u32[]{:S(2)}, u32[]{:S(2)}) %collective-permute-start.5) | collective-permute-done | bytes 65568 | tf_op jit(solution)/shard_map/ppermute | solution.py:229
  60.8 2.4 %collective-permute-done.6.refs_2_ = bf16[256,128]{1,0:T(8,128)(2,1)S(1)} collective-permute-done((bf16[256,128]{1,0:T(8,128)(2,1)S(1)}, bf16[256,128]{1,0:T(8,128)(2,1)S(1)}, u32[]{:S(2)}, u32[]{:S(2)}) %collective-permute-start.6) | collective-permute-done | bytes 65568 | tf_op jit(solution)/shard_map/ppermute | solution.py:229
  63.1 0.1 shard_map.83
  63.3 1.2 %collective-permute-done.7.refs_1_ = bf16[256,128]{1,0:T(8,128)(2,1)S(1)} collective-permute-done((bf16[256,128]{1,0:T(8,128)(2,1)S(1)}, bf16[256,128]{1,0:T(8,128)(2,1)S(1)}, u32[]{:S(2)}, u32[]{:S(2)}) %collective-permute-start.7) | collective-permute-done | bytes 65568 | tf_op jit(solution)/shard_map/ppermute | solution.py:229
  64.6 0.2 shard_map.84
  64.7 2.8 %collective-permute-start.8 = (bf16[512,128]{1,0:T(8,128)(2,1)S(1)}, bf16[512,128]{1,0:T(8,128)(2,1)S(1)}, u32[]{:S(2)}, u32[]{:S(2)}) collective-permute-start(bf16[512,128]{1,0:T(8,128)(2,1)S(1)} %get-tuple-element.35), channel_id=1, source_target_pairs={{0,8},{8,0},{16,24},{24,16},{1,9},{9,1},{17,25},{25,17},{2,10},{10... | collective-permute-start | bytes 393224 | tf_op jit(solution)/shard_map/ppermute | solution.py:229
  67.6 2.4 %collective-permute-start.10 = (bf16[512,128]{1,0:T(8,128)(2,1)S(1)}, bf16[512,128]{1,0:T(8,128)(2,1)S(1)}, u32[]{:S(2)}, u32[]{:S(2)}) collective-permute-start(bf16[512,128]{1,0:T(8,128)(2,1)S(1)} %get-tuple-element.37), channel_id=1, source_target_pairs={{0,24},{8,16},{16,8},{24,0},{1,25},{9,17},{17,9},{25,1},{2,26},{10... | collective-permute-start | bytes 393224 | tf_op jit(solution)/shard_map/ppermute | solution.py:229
  70.0 0.8 shard_map.75
  70.8 1.8 %collective-permute-done.8.refs_1_ = bf16[512,128]{1,0:T(8,128)(2,1)S(1)} collective-permute-done((bf16[512,128]{1,0:T(8,128)(2,1)S(1)}, bf16[512,128]{1,0:T(8,128)(2,1)S(1)}, u32[]{:S(2)}, u32[]{:S(2)}) %collective-permute-start.8) | collective-permute-done | bytes 131104 | tf_op jit(solution)/shard_map/ppermute | solution.py:229
  72.6 7.7 %collective-permute-done.9.refs_2_ = bf16[512,128]{1,0:T(8,128)(2,1)S(1)} collective-permute-done((bf16[512,128]{1,0:T(8,128)(2,1)S(1)}, bf16[512,128]{1,0:T(8,128)(2,1)S(1)}, u32[]{:S(2)}, u32[]{:S(2)}) %collective-permute-start.9) | collective-permute-done | bytes 131104 | tf_op jit(solution)/shard_map/ppermute | solution.py:229
  80.3 2.6 %shard_map.85 = (bf16[128,2048]{1,0:T(8,128)(2,1)}, bf16[128,2048]{1,0:T(8,128)(2,1)}) custom-call(bf16[128,2048]{1,0:T(8,128)(2,1)S(1)} %copy-done, bf16[128,2048]{1,0:T(8,128)(2,1)S(1)} %copy-done.3, bf16[128,2048]{1,0:T(8,128)(2,1)S(1)} %copy-done.5, bf16[128,2048]{1,0:T(8,128)(2,1)S(1)} %copy-done.1, bf16[512,128]{1,0:T(8,128)(2,1)S(1)} %get-tuple-element.34.refs_0_, ...), custom_call_target="tpu_custom_call" | custom-call | flops 402653184 | bytes 5242880 | tf_op jit(solution)/shard_map/pallas_call | solution.py:238
  82.9 1.7 %shard_map.78 = (bf16[128,2048]{1,0:T(8,128)(2,1)}, bf16[128,2048]{1,0:T(8,128)(2,1)}) custom-call(bf16[128,2048]{1,0:T(8,128)(2,1)S(1)} %copy-done, bf16[128,2048]{1,0:T(8,128)(2,1)S(1)} %copy-done.3, bf16[128,2048]{1,0:T(8,128)(2,1)S(1)} %copy-done.5, bf16[128,2048]{1,0:T(8,128)(2,1)S(1)} %copy-done.1, bf16[16,128,128]{2,1,0:T(8,128)(2,1)S(1)} %get-tuple-element.22.sc_ref, ...), custom_call_target="tpu_custom_call" | custom-call | flops 268435456 | bytes 7077888 | tf_op jit(solution)/shard_map/pallas_call | solution.py:238
  (18 shorter events, 0.2 us)
Async XLA Ops:
  0.6 1.0 %copy-start.2 = (bf16[128,2048]{1,0:T(8,128)(2,1)S(1)}, bf16[128,2048]{1,0:T(8,128)(2,1)}, u32[]{:S(2)}) copy-start(bf16[128,2048]{1,0:T(8,128)(2,1)} %k_ref.7) | copy-start | bytes 1572868
  1.7 1.0 %copy-start.4 = (bf16[128,2048]{1,0:T(8,128)(2,1)S(1)}, bf16[128,2048]{1,0:T(8,128)(2,1)}, u32[]{:S(2)}) copy-start(bf16[128,2048]{1,0:T(8,128)(2,1)} %v_ref.7) | copy-start | bytes 1572868
  25.3 57.6 %all-to-all-start.1 = ((bf16[32,64,128]{2,1,0:T(8,128)(2,1)}), bf16[32,64,128]{2,1,0:T(8,128)(2,1)S(1)}, u32[]{:S(2)}, u32[]{:S(2)}) async-start(bf16[32,64,128]{2,1,0:T(8,128)(2,1)} %shard_map.77), calls=%async_computation.1 | async-start | bytes 1048576 | tf_op jit(solution)/shard_map/all_to_all | solution.py:225
  31.7 21.8 %copy-start.6 = (bf16[512,128]{1,0:T(8,128)(2,1)S(1)}, bf16[512,128]{1,0:T(8,128)(2,1)}, u32[]{:S(2)}) copy-start(bf16[512,128]{1,0:T(8,128)(2,1)} %get-tuple-element.26.refs_0_.refs_2_) | copy-start | bytes 393220
  31.7 11.2 %collective-permute-start = (bf16[512,128]{1,0:T(8,128)(2,1)}, bf16[512,128]{1,0:T(8,128)(2,1)S(1)}, u32[]{:S(2)}, u32[]{:S(2)}) collective-permute-start(bf16[512,128]{1,0:T(8,128)(2,1)} %get-tuple-element.27), channel_id=1, source_target_pairs={{0,8},{8,0},{16,24},{24,16},{1,9},{9,1},{17,25},{25,17},{2,10},{10... | collective-permute-start | bytes 393224 | tf_op jit(solution)/shard_map/ppermute | solution.py:229
  33.5 36.5 %copy-start.5 = (bf16[128,2048]{1,0:T(8,128)(2,1)S(1)}, bf16[128,2048]{1,0:T(8,128)(2,1)}, u32[]{:S(2)}) copy-start(bf16[128,2048]{1,0:T(8,128)(2,1)} %v_ref.7) | copy-start | bytes 1572868
  35.7 17.8 %collective-permute-start.1 = (bf16[512,128]{1,0:T(8,128)(2,1)}, bf16[512,128]{1,0:T(8,128)(2,1)S(1)}, u32[]{:S(2)}, u32[]{:S(2)}) collective-permute-start(bf16[512,128]{1,0:T(8,128)(2,1)} %get-tuple-element.28), channel_id=1, source_target_pairs={{0,16},{8,24},{16,0},{24,8},{1,17},{9,25},{17,1},{25,9},{2,18},{10... | collective-permute-start | bytes 393224 | tf_op jit(solution)/shard_map/ppermute | solution.py:229
  38.2 15.3 %collective-permute-start.2 = (bf16[512,128]{1,0:T(8,128)(2,1)}, bf16[512,128]{1,0:T(8,128)(2,1)S(1)}, u32[]{:S(2)}, u32[]{:S(2)}) collective-permute-start(bf16[512,128]{1,0:T(8,128)(2,1)} %get-tuple-element.29), channel_id=1, source_target_pairs={{0,24},{8,16},{16,8},{24,0},{1,25},{9,17},{17,9},{25,1},{2,26},{10... | collective-permute-start | bytes 393224 | tf_op jit(solution)/shard_map/ppermute | solution.py:229
  53.5 16.5 %copy-start.3 = (bf16[128,2048]{1,0:T(8,128)(2,1)S(1)}, bf16[128,2048]{1,0:T(8,128)(2,1)}, u32[]{:S(2)}) copy-start(bf16[128,2048]{1,0:T(8,128)(2,1)} %k_ref.7) | copy-start | bytes 1572868
  53.6 1.3 %collective-permute-start.3 = (bf16[256,128]{1,0:T(8,128)(2,1)S(1)}, bf16[256,128]{1,0:T(8,128)(2,1)S(1)}, u32[]{:S(2)}, u32[]{:S(2)}) collective-permute-start(bf16[256,128]{1,0:T(8,128)(2,1)S(1)} %get-tuple-element.31), channel_id=1, source_target_pairs={{0,1},{1,0},{2,3},{3,2},{4,5},{5,4},{6,7},{7,6},{8,9},{9,8},{10,11... | collective-permute-start | bytes 196616 | tf_op jit(solution)/shard_map/ppermute | solution.py:229
  54.9 15.1 %copy-start = (bf16[128,2048]{1,0:T(8,128)(2,1)S(1)}, bf16[128,2048]{1,0:T(8,128)(2,1)}, u32[]{:S(2)}) copy-start(bf16[128,2048]{1,0:T(8,128)(2,1)} %q_ref.5) | copy-start | bytes 1572868
  54.9 15.1 %copy-start.1 = (bf16[128,2048]{1,0:T(8,128)(2,1)S(1)}, bf16[128,2048]{1,0:T(8,128)(2,1)}, u32[]{:S(2)}) copy-start(bf16[128,2048]{1,0:T(8,128)(2,1)} %g_ref.5) | copy-start | bytes 1572868
  55.0 4.3 %collective-permute-start.4 = (bf16[256,128]{1,0:T(8,128)(2,1)S(1)}, bf16[256,128]{1,0:T(8,128)(2,1)S(1)}, u32[]{:S(2)}, u32[]{:S(2)}) collective-permute-start(bf16[256,128]{1,0:T(8,128)(2,1)S(1)} %shard_map.82), channel_id=1, source_target_pairs={{0,2},{1,3},{2,0},{3,1},{4,6},{5,7},{6,4},{7,5},{8,10},{9,11},{10,... | collective-permute-start | bytes 196616 | tf_op jit(solution)/shard_map/ppermute | solution.py:229
  56.5 4.3 %collective-permute-start.5 = (bf16[256,128]{1,0:T(8,128)(2,1)S(1)}, bf16[256,128]{1,0:T(8,128)(2,1)S(1)}, u32[]{:S(2)}, u32[]{:S(2)}) collective-permute-start(bf16[256,128]{1,0:T(8,128)(2,1)S(1)} %shard_map.82), channel_id=1, source_target_pairs={{0,4},{1,5},{2,6},{3,7},{4,0},{5,1},{6,2},{7,3},{8,12},{9,13},{10,... | collective-permute-start | bytes 196616 | tf_op jit(solution)/shard_map/ppermute | solution.py:229
  58.0 5.2 %collective-permute-start.6 = (bf16[256,128]{1,0:T(8,128)(2,1)S(1)}, bf16[256,128]{1,0:T(8,128)(2,1)S(1)}, u32[]{:S(2)}, u32[]{:S(2)}) collective-permute-start(bf16[256,128]{1,0:T(8,128)(2,1)S(1)} %shard_map.82), channel_id=1, source_target_pairs={{0,6},{1,7},{2,4},{3,5},{4,2},{5,3},{6,0},{7,1},{8,14},{9,15},{10,... | collective-permute-start | bytes 196616 | tf_op jit(solution)/shard_map/ppermute | solution.py:229
  63.2 1.3 %collective-permute-start.7 = (bf16[256,128]{1,0:T(8,128)(2,1)S(1)}, bf16[256,128]{1,0:T(8,128)(2,1)S(1)}, u32[]{:S(2)}, u32[]{:S(2)}) collective-permute-start(bf16[256,128]{1,0:T(8,128)(2,1)S(1)} %get-tuple-element.33), channel_id=1, source_target_pairs={{0,1},{1,0},{2,3},{3,2},{4,5},{5,4},{6,7},{7,6},{8,9},{9,8},{10,11... | collective-permute-start | bytes 196616 | tf_op jit(solution)/shard_map/ppermute | solution.py:229
  64.7 7.9 %collective-permute-start.8 = (bf16[512,128]{1,0:T(8,128)(2,1)S(1)}, bf16[512,128]{1,0:T(8,128)(2,1)S(1)}, u32[]{:S(2)}, u32[]{:S(2)}) collective-permute-start(bf16[512,128]{1,0:T(8,128)(2,1)S(1)} %get-tuple-element.35), channel_id=1, source_target_pairs={{0,8},{8,0},{16,24},{24,16},{1,9},{9,1},{17,25},{25,17},{2,10},{10... | collective-permute-start | bytes 393224 | tf_op jit(solution)/shard_map/ppermute | solution.py:229
  67.6 12.7 %collective-permute-start.9 = (bf16[512,128]{1,0:T(8,128)(2,1)S(1)}, bf16[512,128]{1,0:T(8,128)(2,1)S(1)}, u32[]{:S(2)}, u32[]{:S(2)}) collective-permute-start(bf16[512,128]{1,0:T(8,128)(2,1)S(1)} %get-tuple-element.36), channel_id=1, source_target_pairs={{0,16},{8,24},{16,0},{24,8},{1,17},{9,25},{17,1},{25,9},{2,18},{10... | collective-permute-start | bytes 393224 | tf_op jit(solution)/shard_map/ppermute | solution.py:229
  67.6 12.7 %collective-permute-start.10 = (bf16[512,128]{1,0:T(8,128)(2,1)S(1)}, bf16[512,128]{1,0:T(8,128)(2,1)S(1)}, u32[]{:S(2)}, u32[]{:S(2)}) collective-permute-start(bf16[512,128]{1,0:T(8,128)(2,1)S(1)} %get-tuple-element.37), channel_id=1, source_target_pairs={{0,24},{8,16},{16,8},{24,0},{1,25},{9,17},{17,9},{25,1},{2,26},{10... | collective-permute-start | bytes 393224 | tf_op jit(solution)/shard_map/ppermute | solution.py:229
